TPU v7x, 256 devices: a whole 4x4x8 slice. The times are simulated.
256 devices in a mesh: blk: 128 (over z, x, y_hi, core), rep: 2 (over y_lo).
Axes of the slice: x: 4, y: 4 (y_hi: 2, y_lo: 2; y = y_hi * 2 + y_lo), z: 8, core: 2. Of those that a mesh axis runs over, the one named last changes fastest.
Arguments:
- block_inputs: bfloat16 [40960, 4096], P(('blk', 'rep')), may hold values from -120 to 120
- out_cotangent: bfloat16 [40960, 4096], P(('blk', 'rep')), may hold values from -6 to 6
- dnormed_in: float32 [40960, 4096], P(('blk', 'rep')), may hold values from -6 to 6
- carried_sums: float32 [3, 14336, 4096], P(None, ('blk', 'rep')), may hold values from -384 to 384
- norm_gain: float32 [4096], replicated, may hold values from 0.1 to 1.9
- w_gate: bfloat16 [7168, 4096], P('blk'), may hold values from -0.09375 to 0.09375
- w_up: bfloat16 [7168, 4096], P('blk'), may hold values from -0.09375 to 0.09375
- w_down: bfloat16 [7168, 4096], P('blk'), may hold values from -0.0625 to 0.0625
Outputs:
- input_grad: bfloat16 [40960, 4096], P(('blk', 'rep'))
- grad_gate: bfloat16 [7168, 4096], P('blk')
- grad_up: bfloat16 [7168, 4096], P('blk')
- grad_down: bfloat16 [7168, 4096], P('blk')
All inputs are finite; a program needn't handle non-finite values.
Results may differ from a plain program's by a relative error of at most 0.0038.
Values may be sent and summed in bfloat16 or wider, within the bound.
No kernel may reach another device: no remote copies, remote signals or barrier semaphores. Data moves between devices by JAX's collectives and lax.ppermute only.
A program may use at most 64 MiB of HBM per device.

v0:
```python
import math

import jax
import jax.numpy as jnp
from jax import lax
from jax.sharding import PartitionSpec as P

CYCLE_STEPS = 6


epsilon = 1e-05


def passed_along(value, axis, steps):
    count = lax.axis_size(axis)
    pairs = [(source, (source + steps) % count) for source in range(count)]
    return lax.ppermute(value, axis, pairs)


def local_terms(normed, grad_in, gate_rows, up_rows, down_rows):
    gate = jnp.einsum("td,fd->tf", normed, gate_rows, preferred_element_type=jnp.float32)
    upper = jnp.einsum("td,fd->tf", normed, up_rows, preferred_element_type=jnp.float32)
    sigma = jax.nn.sigmoid(gate)
    act = gate * sigma
    hidden = (act * upper).astype(jnp.bfloat16)
    dhidden = jnp.einsum("td,fd->tf", grad_in, down_rows, preferred_element_type=jnp.float32)
    dgate = (dhidden * upper * sigma * (1.0 + gate * (1.0 - sigma))).astype(jnp.bfloat16)
    dup = (dhidden * act).astype(jnp.bfloat16)
    dnormed = jnp.einsum("tf,fd->td", dgate, gate_rows, preferred_element_type=jnp.float32)
    dnormed = dnormed + jnp.einsum("tf,fd->td", dup, up_rows, preferred_element_type=jnp.float32)
    terms = (
        jnp.einsum("tf,td->fd", dgate, normed, preferred_element_type=jnp.float32),
        jnp.einsum("tf,td->fd", dup, normed, preferred_element_type=jnp.float32),
        jnp.einsum("tf,td->fd", hidden, grad_in, preferred_element_type=jnp.float32),
    )
    return (terms, dnormed)


def shards(block_inputs, out_cotangent, dnormed_in, carried_sums, norm_gain, w_gate, w_up, w_down):
    steps = CYCLE_STEPS
    scale = 1.0 / math.sqrt(lax.axis_size("blk") * block_inputs.shape[0] * lax.axis_size("rep"))
    values = block_inputs.astype(jnp.float32)
    rstd = lax.rsqrt(jnp.mean(values * values, axis=-1, keepdims=True) + epsilon)
    normed = (values * rstd * norm_gain).astype(jnp.bfloat16)
    weights = passed_along((w_gate, w_up, w_down), "blk", -steps)
    terms, part = local_terms(normed, out_cotangent, weights[0], weights[1], weights[2])
    dnormed = dnormed_in + part
    fresh = (carried_sums[0] + terms[0], carried_sums[1] + terms[1], carried_sums[2] + terms[2])
    sums = fresh

    def advance(index, state):
        weights_now, sums_now, dnormed_now = state
        weights_now = passed_along((weights_now[0], weights_now[1], weights_now[2]), "blk", 1)
        step_terms, step_part = local_terms(
            normed, out_cotangent, weights_now[0], weights_now[1], weights_now[2]
        )
        dnormed_now = dnormed_now + step_part
        moved = passed_along((sums_now[0], sums_now[1], sums_now[2]), "blk", 1)
        sums_now = (moved[0] + step_terms[0], moved[1] + step_terms[1], moved[2] + step_terms[2])
        return (weights_now, sums_now, dnormed_now)

    weights, sums, dnormed = lax.fori_loop(1, steps, advance, (weights, sums, dnormed))
    home = passed_along((sums[0], sums[1], sums[2]), "blk", 1)
    summed = lax.psum((home[0], home[1], home[2]), "rep")
    finals = tuple(((piece * scale).astype(jnp.bfloat16) for piece in summed))
    scaled = norm_gain * dnormed
    dx = rstd * scaled - values * rstd**3 * jnp.mean(values * scaled, axis=-1, keepdims=True)
    input_grad = (out_cotangent.astype(jnp.float32) + dx).astype(jnp.bfloat16)
    return (input_grad, finals[0], finals[1], finals[2])


def solution(mesh):
    placed = (
        P(("blk", "rep"), None),
        P(("blk", "rep"), None),
        P(("blk", "rep"), None),
        P(None, ("blk", "rep"), None),
        P(),
        P("blk", None),
        P("blk", None),
        P("blk", None),
    )
    return jax.shard_map(
        shards,
        mesh=mesh,
        in_specs=placed,
        out_specs=(P(("blk", "rep"), None), P("blk", None), P("blk", None), P("blk", None)),
        check_vma=False,
    )
```

profile of v0, /device:TPU:1, one launch (start us, length us, event | category | flops | bytes accessed | tf_op | source)
XLA Modules:
  0.0 463.3 jit_solution(1371777728415848374)
XLA Ops:
  7.2 11.6 %collective-permute-start.6 = (bf16[56,4096]{1,0:T(8,128)(2,1)}, bf16[56,4096]{1,0:T(8,128)(2,1)S(1)}, u32[]{:S(2)}, u32[]{:S(2)}) collective-permute-start(bf16[56,4096]{1,0:T(8,128)(2,1)} %param.15), channel_id=1, source_target_pairs={{0,244},{2,246},{4,248},{6,250},{8,252},{10,254},{12,0},{14,2},{16... | collective-permute-start | bytes 1376264 | tf_op jit(solution)/shard_map/ppermute | solution.py:17
  18.9 4.9 %collective-permute-start.8 = (bf16[56,4096]{1,0:T(8,128)(2,1)}, bf16[56,4096]{1,0:T(8,128)(2,1)S(1)}, u32[]{:S(2)}, u32[]{:S(2)}) collective-permute-start(bf16[56,4096]{1,0:T(8,128)(2,1)} %param.17), channel_id=1, source_target_pairs={{0,244},{2,246},{4,248},{6,250},{8,252},{10,254},{12,0},{14,2},{16... | collective-permute-start | bytes 1376264 | tf_op jit(solution)/shard_map/ppermute | solution.py:17
  25.4 1.8 fusion.7
  28.9 9.3 %collective-permute-done.7 = bf16[56,4096]{1,0:T(8,128)(2,1)} collective-permute-done((bf16[56,4096]{1,0:T(8,128)(2,1)}, bf16[56,4096]{1,0:T(8,128)(2,1)}, u32[]{:S(2)}, u32[]{:S(2)}) %collective-permute-start.7) | collective-permute-done | bytes 458784 | tf_op jit(solution)/shard_map/ppermute | solution.py:17
  41.0 7.0 %collective-permute-done.8 = bf16[56,4096]{1,0:T(8,128)(2,1)S(1)} collective-permute-done((bf16[56,4096]{1,0:T(8,128)(2,1)}, bf16[56,4096]{1,0:T(8,128)(2,1)S(1)}, u32[]{:S(2)}, u32[]{:S(2)}) %collective-permute-start.8) | collective-permute-done | bytes 458784 | tf_op jit(solution)/shard_map/ppermute | solution.py:17
  52.6 2.0 fusion.4
  54.7 252.2 %while.22 = (s32[]{:T(128)}, bf16[56,4096]{1,0:T(8,128)(2,1)S(1)}, bf16[56,4096]{1,0:T(8,128)(2,1)}, bf16[56,4096]{1,0:T(8,128)(2,1)S(1)}, f32[56,4096]{1,0:T(8,...) while((s32[]{:T(128)}, bf16[56,4096]{1,0:T(8,128)(2,1)S(1)}, ...), condition=%wide.region_2.0_spmd, body=%wide.region_1.0_spmd.sunk | while | flops 589371648 | bytes 74051080 | solution.py:62
  57.4 2.8 collective-permute-start.2
  62.4 3.9 collective-permute-start.3
  69.2 3.0 collective-permute-done.2
  72.2 1.8 copy.31
  77.2 14.6 %collective-permute-done.4 = f32[56,4096]{1,0:T(8,128)} collective-permute-done((f32[56,4096]{1,0:T(8,128)}, f32[56,4096]{1,0:T(8,128)}, u32[]{:S(2)}, u32[]{:S(2)}) %collective-permute-start.4) | collective-permute-done | bytes 917536 | tf_op jit(solution)/shard_map/while/body/eval_jaxpr/ppermute | solution.py:17
  91.9 2.4 convolution_add_fusion.12
  94.3 2.5 convolution_add_fusion.13
  96.9 4.8 %collective-permute-done.3 = f32[56,4096]{1,0:T(8,128)S(1)} collective-permute-done((f32[56,4096]{1,0:T(8,128)}, f32[56,4096]{1,0:T(8,128)S(1)}, u32[]{:S(2)}, u32[]{:S(2)}) %collective-permute-start.3) | collective-permute-done | bytes 917536 | tf_op jit(solution)/shard_map/while/body/eval_jaxpr/ppermute | solution.py:17
  103.7 3.9 collective-permute-start.1
  108.4 3.7 collective-permute-start.2
  113.7 3.6 collective-permute-start.3
  120.2 3.0 collective-permute-done.2
  123.2 1.8 copy.31
  125.0 1.7 multiply_convert_fusion.14
  128.2 14.6 %collective-permute-done.4 = f32[56,4096]{1,0:T(8,128)} collective-permute-done((f32[56,4096]{1,0:T(8,128)}, f32[56,4096]{1,0:T(8,128)}, u32[]{:S(2)}, u32[]{:S(2)}) %collective-permute-start.4) | collective-permute-done | bytes 917536 | tf_op jit(solution)/shard_map/while/body/eval_jaxpr/ppermute | solution.py:17
  142.8 2.5 convolution_add_fusion.12
  145.3 2.5 convolution_add_fusion.13
  147.8 4.8 %collective-permute-done.3 = f32[56,4096]{1,0:T(8,128)S(1)} collective-permute-done((f32[56,4096]{1,0:T(8,128)}, f32[56,4096]{1,0:T(8,128)S(1)}, u32[]{:S(2)}, u32[]{:S(2)}) %collective-permute-start.3) | collective-permute-done | bytes 917536 | tf_op jit(solution)/shard_map/while/body/eval_jaxpr/ppermute | solution.py:17
  154.7 3.9 collective-permute-start.1
  159.4 4.6 collective-permute-start.2
  164.8 4.1 collective-permute-done.1
  171.6 2.6 collective-permute-done.2
  174.2 1.8 copy.31
  176.0 1.7 multiply_convert_fusion.14
  179.2 14.6 %collective-permute-done.4 = f32[56,4096]{1,0:T(8,128)} collective-permute-done((f32[56,4096]{1,0:T(8,128)}, f32[56,4096]{1,0:T(8,128)}, u32[]{:S(2)}, u32[]{:S(2)}) %collective-permute-start.4) | collective-permute-done | bytes 917536 | tf_op jit(solution)/shard_map/while/body/eval_jaxpr/ppermute | solution.py:17
  193.8 2.4 convolution_add_fusion.12
  196.3 2.5 convolution_add_fusion.13
  198.8 4.8 %collective-permute-done.3 = f32[56,4096]{1,0:T(8,128)S(1)} collective-permute-done((f32[56,4096]{1,0:T(8,128)}, f32[56,4096]{1,0:T(8,128)S(1)}, u32[]{:S(2)}, u32[]{:S(2)}) %collective-permute-start.3) | collective-permute-done | bytes 917536 | tf_op jit(solution)/shard_map/while/body/eval_jaxpr/ppermute | solution.py:17
  205.7 3.9 collective-permute-start.1
  211.1 4.8 %collective-permute-start.2 = (bf16[56,4096]{1,0:T(8,128)(2,1)}, bf16[56,4096]{1,0:T(8,128)(2,1)}, u32[]{:S(2)}, u32[]{:S(2)}) collective-permute-start(bf16[56,4096]{1,0:T(8,128)(2,1)} %copy-done.9), channel_id=1, source_target_pairs={{0,2},{2,4},{4,6},{6,8},{8,10},{10,12},{12,14},{14,16},{16,18},{18... | collective-permute-start | bytes 1376264 | tf_op jit(solution)/shard_map/while/body/eval_jaxpr/ppermute | solution.py:17
  216.7 7.4 %collective-permute-done.1 = bf16[56,4096]{1,0:T(8,128)(2,1)S(1)} collective-permute-done((bf16[56,4096]{1,0:T(8,128)(2,1)}, bf16[56,4096]{1,0:T(8,128)(2,1)S(1)}, u32[]{:S(2)}, u32[]{:S(2)}) %collective-permute-start.1) | collective-permute-done | bytes 458784 | tf_op jit(solution)/shard_map/while/body/eval_jaxpr/ppermute | solution.py:17
  226.8 1.8 copy.31
  228.6 1.7 multiply_convert_fusion.14
  231.8 13.0 %collective-permute-done.4 = f32[56,4096]{1,0:T(8,128)} collective-permute-done((f32[56,4096]{1,0:T(8,128)}, f32[56,4096]{1,0:T(8,128)}, u32[]{:S(2)}, u32[]{:S(2)}) %collective-permute-start.4) | collective-permute-done | bytes 917536 | tf_op jit(solution)/shard_map/while/body/eval_jaxpr/ppermute | solution.py:17
  244.8 2.4 convolution_add_fusion.12
  247.3 2.5 convolution_add_fusion.13
  249.8 4.8 %collective-permute-done.3 = f32[56,4096]{1,0:T(8,128)S(1)} collective-permute-done((f32[56,4096]{1,0:T(8,128)}, f32[56,4096]{1,0:T(8,128)S(1)}, u32[]{:S(2)}, u32[]{:S(2)}) %collective-permute-start.3) | collective-permute-done | bytes 917536 | tf_op jit(solution)/shard_map/while/body/eval_jaxpr/ppermute | solution.py:17
  256.7 3.9 collective-permute-start.1
  260.6 2.4 collective-permute-start
  263.0 4.8 %collective-permute-start.2 = (bf16[56,4096]{1,0:T(8,128)(2,1)}, bf16[56,4096]{1,0:T(8,128)(2,1)}, u32[]{:S(2)}, u32[]{:S(2)}) collective-permute-start(bf16[56,4096]{1,0:T(8,128)(2,1)} %copy-done.9), channel_id=1, source_target_pairs={{0,2},{2,4},{4,6},{6,8},{8,10},{10,12},{12,14},{14,16},{16,18},{18... | collective-permute-start | bytes 1376264 | tf_op jit(solution)/shard_map/while/body/eval_jaxpr/ppermute | solution.py:17
  268.5 10.7 %collective-permute-done.1 = bf16[56,4096]{1,0:T(8,128)(2,1)S(1)} collective-permute-done((bf16[56,4096]{1,0:T(8,128)(2,1)}, bf16[56,4096]{1,0:T(8,128)(2,1)S(1)}, u32[]{:S(2)}, u32[]{:S(2)}) %collective-permute-start.1) | collective-permute-done | bytes 458784 | tf_op jit(solution)/shard_map/while/body/eval_jaxpr/ppermute | solution.py:17
  282.0 1.8 copy.31
  283.8 1.7 multiply_convert_fusion.14
  287.0 8.8 %collective-permute-done.4 = f32[56,4096]{1,0:T(8,128)} collective-permute-done((f32[56,4096]{1,0:T(8,128)}, f32[56,4096]{1,0:T(8,128)}, u32[]{:S(2)}, u32[]{:S(2)}) %collective-permute-start.4) | collective-permute-done | bytes 917536 | tf_op jit(solution)/shard_map/while/body/eval_jaxpr/ppermute | solution.py:17
  295.8 2.5 convolution_add_fusion.12
  298.3 2.5 convolution_add_fusion.13
  300.8 4.8 %collective-permute-done.3 = f32[56,4096]{1,0:T(8,128)S(1)} collective-permute-done((f32[56,4096]{1,0:T(8,128)}, f32[56,4096]{1,0:T(8,128)S(1)}, u32[]{:S(2)}, u32[]{:S(2)}) %collective-permute-start.3) | collective-permute-done | bytes 917536 | tf_op jit(solution)/shard_map/while/body/eval_jaxpr/ppermute | solution.py:17
  306.9 4.0 collective-permute-start.9
  310.9 3.3 collective-permute-start.10
  314.2 4.8 %collective-permute-start.11 = (f32[56,4096]{1,0:T(8,128)}, f32[56,4096]{1,0:T(8,128)}, u32[]{:S(2)}, u32[]{:S(2)}) collective-permute-start(f32[56,4096]{1,0:T(8,128)} %get-tuple-element.62), channel_id=1, source_target_pairs={{0,2},{2,4},{4,6},{6,8},{8,10},{10,12},{12,14},{14,16},{16,18},{18... | collective-permute-start | bytes 2752520 | tf_op jit(solution)/shard_map/ppermute | solution.py:17
  319.0 15.6 %collective-permute-done.9 = f32[56,4096]{1,0:T(8,128)} collective-permute-done((f32[56,4096]{1,0:T(8,128)}, f32[56,4096]{1,0:T(8,128)}, u32[]{:S(2)}, u32[]{:S(2)}) %collective-permute-start.9) | collective-permute-done | bytes 917536 | tf_op jit(solution)/shard_map/ppermute | solution.py:17
  335.9 5.3 %collective-permute-done.11 = f32[56,4096]{1,0:T(8,128)} collective-permute-done((f32[56,4096]{1,0:T(8,128)}, f32[56,4096]{1,0:T(8,128)}, u32[]{:S(2)}, u32[]{:S(2)}) %collective-permute-start.11) | collective-permute-done | bytes 917536 | tf_op jit(solution)/shard_map/ppermute | solution.py:17
  341.2 2.3 fusion.12
  343.7 2.0 fusion.11
  345.7 106.2 %all-reduce.3.cloned.1.call-done = (f32[56,4096]{1,0:T(8,128)}, f32[56,4096]{1,0:T(8,128)}, f32[56,4096]{1,0:T(8,128)}) async-done(((f32[56,4096]{1,0:T(8,128)}, f32[56,4096]{1,0:T(8,128)}, f32[56,4096]{1,0:T(8,128)}), (f32[56,4096]{1,0:T(8,128)}, f32[56,4096]{1,0:T(8,128)}, f32[56,4096]{1,0:T(8,128)})) %all-reduce.3.cloned.1.call-update) | async-done | bytes 2752528 | tf_op jit(solution)/shard_map/psum | solution.py:64
  451.9 2.0 multiply_convert_fusion.6
  453.9 2.5 multiply_convert_fusion.4
  (155 shorter events, 56.6 us)
Async XLA Ops:
  7.2 444.8 %all-reduce.3.cloned.1.call-start = ((), (), s32[]{:S(2)}) async-start(), calls=%async_computation | async-start | bytes 5505024 | tf_op jit(solution)/shard_map/psum | solution.py:64
  7.2 21.1 %collective-permute-start.6 = (bf16[56,4096]{1,0:T(8,128)(2,1)}, bf16[56,4096]{1,0:T(8,128)(2,1)S(1)}, u32[]{:S(2)}, u32[]{:S(2)}) collective-permute-start(bf16[56,4096]{1,0:T(8,128)(2,1)} %param.15), channel_id=1, source_target_pairs={{0,244},{2,246},{4,248},{6,250},{8,252},{10,254},{12,0},{14,2},{16... | collective-permute-start | bytes 1376264 | tf_op jit(solution)/shard_map/ppermute | solution.py:17
  18.8 19.4 %collective-permute-start.7 = (bf16[56,4096]{1,0:T(8,128)(2,1)}, bf16[56,4096]{1,0:T(8,128)(2,1)}, u32[]{:S(2)}, u32[]{:S(2)}) collective-permute-start(bf16[56,4096]{1,0:T(8,128)(2,1)} %param.16), channel_id=1, source_target_pairs={{0,244},{2,246},{4,248},{6,250},{8,252},{10,254},{12,0},{14,2},{16... | collective-permute-start | bytes 1376264 | tf_op jit(solution)/shard_map/ppermute | solution.py:17
  18.9 29.1 %collective-permute-start.8 = (bf16[56,4096]{1,0:T(8,128)(2,1)}, bf16[56,4096]{1,0:T(8,128)(2,1)S(1)}, u32[]{:S(2)}, u32[]{:S(2)}) collective-permute-start(bf16[56,4096]{1,0:T(8,128)(2,1)} %param.17), channel_id=1, source_target_pairs={{0,244},{2,246},{4,248},{6,250},{8,252},{10,254},{12,0},{14,2},{16... | collective-permute-start | bytes 1376264 | tf_op jit(solution)/shard_map/ppermute | solution.py:17
  25.4 14.3 %copy-start = (bf16[160,4096]{1,0:T(8,128)(2,1)S(1)}, bf16[160,4096]{1,0:T(8,128)(2,1)}, u32[]{:S(2)}) copy-start(bf16[160,4096]{1,0:T(8,128)(2,1)} %param.11) | copy-start | bytes 3932164
  27.2 12.5 %copy-start.5 = (f32[3,56,4096]{2,1,0:T(8,128)S(1)}, f32[3,56,4096]{2,1,0:T(8,128)}, u32[]{:S(2)}) copy-start(f32[3,56,4096]{2,1,0:T(8,128)} %param.13) | copy-start | bytes 8257540
  49.8 2.8 copy-start.6
  55.4 6.9 %collective-permute-start.1 = (bf16[56,4096]{1,0:T(8,128)(2,1)}, bf16[56,4096]{1,0:T(8,128)(2,1)S(1)}, u32[]{:S(2)}, u32[]{:S(2)}) collective-permute-start(bf16[56,4096]{1,0:T(8,128)(2,1)} %get-tuple-element.172), channel_id=1, source_target_pairs={{0,2},{2,4},{4,6},{6,8},{8,10},{10,12},{12,14},{14,16},{16,18},{18... | collective-permute-start | bytes 1376264 | tf_op jit(solution)/shard_map/while/body/eval_jaxpr/ppermute | solution.py:17
  56.6 10.7 %collective-permute-start = (bf16[56,4096]{1,0:T(8,128)(2,1)}, bf16[56,4096]{1,0:T(8,128)(2,1)S(1)}, u32[]{:S(2)}, u32[]{:S(2)}) collective-permute-start(bf16[56,4096]{1,0:T(8,128)(2,1)} %copy-done.7), channel_id=1, source_target_pairs={{0,2},{2,4},{4,6},{6,8},{8,10},{10,12},{12,14},{14,16},{16,18},{18... | collective-permute-start | bytes 1376264 | tf_op jit(solution)/shard_map/while/body/eval_jaxpr/ppermute | solution.py:17
  57.4 14.8 %collective-permute-start.2 = (bf16[56,4096]{1,0:T(8,128)(2,1)}, bf16[56,4096]{1,0:T(8,128)(2,1)}, u32[]{:S(2)}, u32[]{:S(2)}) collective-permute-start(bf16[56,4096]{1,0:T(8,128)(2,1)} %copy-done.9), channel_id=1, source_target_pairs={{0,2},{2,4},{4,6},{6,8},{8,10},{10,12},{12,14},{14,16},{16,18},{18... | collective-permute-start | bytes 1376264 | tf_op jit(solution)/shard_map/while/body/eval_jaxpr/ppermute | solution.py:17
  60.2 34.1 %collective-permute-start.5 = (f32[56,4096]{1,0:T(8,128)}, f32[56,4096]{1,0:T(8,128)}, u32[]{:S(2)}, u32[]{:S(2)}) collective-permute-start(f32[56,4096]{1,0:T(8,128)} %get-tuple-element.176), channel_id=1, source_target_pairs={{0,2},{2,4},{4,6},{6,8},{8,10},{10,12},{12,14},{14,16},{16,18},{18... | collective-permute-start | bytes 2752520 | tf_op jit(solution)/shard_map/while/body/eval_jaxpr/ppermute | solution.py:17
  61.0 30.9 %collective-permute-start.4 = (f32[56,4096]{1,0:T(8,128)}, f32[56,4096]{1,0:T(8,128)}, u32[]{:S(2)}, u32[]{:S(2)}) collective-permute-start(f32[56,4096]{1,0:T(8,128)} %get-tuple-element.175), channel_id=1, source_target_pairs={{0,2},{2,4},{4,6},{6,8},{8,10},{10,12},{12,14},{14,16},{16,18},{18... | collective-permute-start | bytes 2752520 | tf_op jit(solution)/shard_map/while/body/eval_jaxpr/ppermute | solution.py:17
  62.4 39.3 %collective-permute-start.3 = (f32[56,4096]{1,0:T(8,128)}, f32[56,4096]{1,0:T(8,128)S(1)}, u32[]{:S(2)}, u32[]{:S(2)}) collective-permute-start(f32[56,4096]{1,0:T(8,128)} %get-tuple-element.174), channel_id=1, source_target_pairs={{0,2},{2,4},{4,6},{6,8},{8,10},{10,12},{12,14},{14,16},{16,18},{18... | collective-permute-start | bytes 2752520 | tf_op jit(solution)/shard_map/while/body/eval_jaxpr/ppermute | solution.py:17
  77.2 19.7 %copy-start.2 = (f32[160,4096]{1,0:T(8,128)}, f32[160,4096]{1,0:T(8,128)S(1)}, u32[]{:S(2)}) copy-start(f32[160,4096]{1,0:T(8,128)S(1)} %fusion.89) | copy-start | bytes 7864324 | tf_op jit(solution)/shard_map/while
  94.3 8.7 %copy-start.8 = (bf16[56,4096]{1,0:T(8,128)(2,1)S(1)}, bf16[56,4096]{1,0:T(8,128)(2,1)}, u32[]{:S(2)}) copy-start(bf16[56,4096]{1,0:T(8,128)(2,1)} %copy.29) | copy-start | bytes 1376260 | tf_op jit(solution)/shard_map/while
  94.3 8.7 %copy-start.10 = (bf16[56,4096]{1,0:T(8,128)(2,1)S(1)}, bf16[56,4096]{1,0:T(8,128)(2,1)}, u32[]{:S(2)}) copy-start(bf16[56,4096]{1,0:T(8,128)(2,1)} %copy.31) | copy-start | bytes 1376260 | tf_op jit(solution)/shard_map/while
  103.7 3.9 copy-start.7
  103.7 9.9 %collective-permute-start.1 = (bf16[56,4096]{1,0:T(8,128)(2,1)}, bf16[56,4096]{1,0:T(8,128)(2,1)S(1)}, u32[]{:S(2)}, u32[]{:S(2)}) collective-permute-start(bf16[56,4096]{1,0:T(8,128)(2,1)} %get-tuple-element.172), channel_id=1, source_target_pairs={{0,2},{2,4},{4,6},{6,8},{8,10},{10,12},{12,14},{14,16},{16,18},{18... | collective-permute-start | bytes 1376264 | tf_op jit(solution)/shard_map/while/body/eval_jaxpr/ppermute | solution.py:17
  107.6 10.7 %collective-permute-start = (bf16[56,4096]{1,0:T(8,128)(2,1)}, bf16[56,4096]{1,0:T(8,128)(2,1)S(1)}, u32[]{:S(2)}, u32[]{:S(2)}) collective-permute-start(bf16[56,4096]{1,0:T(8,128)(2,1)} %copy-done.7), channel_id=1, source_target_pairs={{0,2},{2,4},{4,6},{6,8},{8,10},{10,12},{12,14},{14,16},{16,18},{18... | collective-permute-start | bytes 1376264 | tf_op jit(solution)/shard_map/while/body/eval_jaxpr/ppermute | solution.py:17
  108.4 14.8 %collective-permute-start.2 = (bf16[56,4096]{1,0:T(8,128)(2,1)}, bf16[56,4096]{1,0:T(8,128)(2,1)}, u32[]{:S(2)}, u32[]{:S(2)}) collective-permute-start(bf16[56,4096]{1,0:T(8,128)(2,1)} %copy-done.9), channel_id=1, source_target_pairs={{0,2},{2,4},{4,6},{6,8},{8,10},{10,12},{12,14},{14,16},{16,18},{18... | collective-permute-start | bytes 1376264 | tf_op jit(solution)/shard_map/while/body/eval_jaxpr/ppermute | solution.py:17
  112.1 33.2 %collective-permute-start.5 = (f32[56,4096]{1,0:T(8,128)}, f32[56,4096]{1,0:T(8,128)}, u32[]{:S(2)}, u32[]{:S(2)}) collective-permute-start(f32[56,4096]{1,0:T(8,128)} %get-tuple-element.176), channel_id=1, source_target_pairs={{0,2},{2,4},{4,6},{6,8},{8,10},{10,12},{12,14},{14,16},{16,18},{18... | collective-permute-start | bytes 2752520 | tf_op jit(solution)/shard_map/while/body/eval_jaxpr/ppermute | solution.py:17
  112.9 30.0 %collective-permute-start.4 = (f32[56,4096]{1,0:T(8,128)}, f32[56,4096]{1,0:T(8,128)}, u32[]{:S(2)}, u32[]{:S(2)}) collective-permute-start(f32[56,4096]{1,0:T(8,128)} %get-tuple-element.175), channel_id=1, source_target_pairs={{0,2},{2,4},{4,6},{6,8},{8,10},{10,12},{12,14},{14,16},{16,18},{18... | collective-permute-start | bytes 2752520 | tf_op jit(solution)/shard_map/while/body/eval_jaxpr/ppermute | solution.py:17
  113.7 39.0 %collective-permute-start.3 = (f32[56,4096]{1,0:T(8,128)}, f32[56,4096]{1,0:T(8,128)S(1)}, u32[]{:S(2)}, u32[]{:S(2)}) collective-permute-start(f32[56,4096]{1,0:T(8,128)} %get-tuple-element.174), channel_id=1, source_target_pairs={{0,2},{2,4},{4,6},{6,8},{8,10},{10,12},{12,14},{14,16},{16,18},{18... | collective-permute-start | bytes 2752520 | tf_op jit(solution)/shard_map/while/body/eval_jaxpr/ppermute | solution.py:17
  125.0 2.3 copy-start.1
  128.2 19.6 %copy-start.2 = (f32[160,4096]{1,0:T(8,128)}, f32[160,4096]{1,0:T(8,128)S(1)}, u32[]{:S(2)}) copy-start(f32[160,4096]{1,0:T(8,128)S(1)} %fusion.89) | copy-start | bytes 7864324 | tf_op jit(solution)/shard_map/while
  145.3 8.6 %copy-start.8 = (bf16[56,4096]{1,0:T(8,128)(2,1)S(1)}, bf16[56,4096]{1,0:T(8,128)(2,1)}, u32[]{:S(2)}) copy-start(bf16[56,4096]{1,0:T(8,128)(2,1)} %copy.29) | copy-start | bytes 1376260 | tf_op jit(solution)/shard_map/while
  145.3 8.7 %copy-start.10 = (bf16[56,4096]{1,0:T(8,128)(2,1)S(1)}, bf16[56,4096]{1,0:T(8,128)(2,1)}, u32[]{:S(2)}) copy-start(bf16[56,4096]{1,0:T(8,128)(2,1)} %copy.31) | copy-start | bytes 1376260 | tf_op jit(solution)/shard_map/while
  154.7 3.9 copy-start.7
  154.7 14.2 %collective-permute-start.1 = (bf16[56,4096]{1,0:T(8,128)(2,1)}, bf16[56,4096]{1,0:T(8,128)(2,1)S(1)}, u32[]{:S(2)}, u32[]{:S(2)}) collective-permute-start(bf16[56,4096]{1,0:T(8,128)(2,1)} %get-tuple-element.172), channel_id=1, source_target_pairs={{0,2},{2,4},{4,6},{6,8},{8,10},{10,12},{12,14},{14,16},{16,18},{18... | collective-permute-start | bytes 1376264 | tf_op jit(solution)/shard_map/while/body/eval_jaxpr/ppermute | solution.py:17
  158.6 11.1 %collective-permute-start = (bf16[56,4096]{1,0:T(8,128)(2,1)}, bf16[56,4096]{1,0:T(8,128)(2,1)S(1)}, u32[]{:S(2)}, u32[]{:S(2)}) collective-permute-start(bf16[56,4096]{1,0:T(8,128)(2,1)} %copy-done.7), channel_id=1, source_target_pairs={{0,2},{2,4},{4,6},{6,8},{8,10},{10,12},{12,14},{14,16},{16,18},{18... | collective-permute-start | bytes 1376264 | tf_op jit(solution)/shard_map/while/body/eval_jaxpr/ppermute | solution.py:17
  159.4 14.8 %collective-permute-start.2 = (bf16[56,4096]{1,0:T(8,128)(2,1)}, bf16[56,4096]{1,0:T(8,128)(2,1)}, u32[]{:S(2)}, u32[]{:S(2)}) collective-permute-start(bf16[56,4096]{1,0:T(8,128)(2,1)} %copy-done.9), channel_id=1, source_target_pairs={{0,2},{2,4},{4,6},{6,8},{8,10},{10,12},{12,14},{14,16},{16,18},{18... | collective-permute-start | bytes 1376264 | tf_op jit(solution)/shard_map/while/body/eval_jaxpr/ppermute | solution.py:17
  164.0 32.3 %collective-permute-start.5 = (f32[56,4096]{1,0:T(8,128)}, f32[56,4096]{1,0:T(8,128)}, u32[]{:S(2)}, u32[]{:S(2)}) collective-permute-start(f32[56,4096]{1,0:T(8,128)} %get-tuple-element.176), channel_id=1, source_target_pairs={{0,2},{2,4},{4,6},{6,8},{8,10},{10,12},{12,14},{14,16},{16,18},{18... | collective-permute-start | bytes 2752520 | tf_op jit(solution)/shard_map/while/body/eval_jaxpr/ppermute | solution.py:17
  164.8 29.1 %collective-permute-start.4 = (f32[56,4096]{1,0:T(8,128)}, f32[56,4096]{1,0:T(8,128)}, u32[]{:S(2)}, u32[]{:S(2)}) collective-permute-start(f32[56,4096]{1,0:T(8,128)} %get-tuple-element.175), channel_id=1, source_target_pairs={{0,2},{2,4},{4,6},{6,8},{8,10},{10,12},{12,14},{14,16},{16,18},{18... | collective-permute-start | bytes 2752520 | tf_op jit(solution)/shard_map/while/body/eval_jaxpr/ppermute | solution.py:17
  168.9 34.8 %collective-permute-start.3 = (f32[56,4096]{1,0:T(8,128)}, f32[56,4096]{1,0:T(8,128)S(1)}, u32[]{:S(2)}, u32[]{:S(2)}) collective-permute-start(f32[56,4096]{1,0:T(8,128)} %get-tuple-element.174), channel_id=1, source_target_pairs={{0,2},{2,4},{4,6},{6,8},{8,10},{10,12},{12,14},{14,16},{16,18},{18... | collective-permute-start | bytes 2752520 | tf_op jit(solution)/shard_map/while/body/eval_jaxpr/ppermute | solution.py:17
  176.0 2.3 copy-start.1
  179.2 19.6 %copy-start.2 = (f32[160,4096]{1,0:T(8,128)}, f32[160,4096]{1,0:T(8,128)S(1)}, u32[]{:S(2)}) copy-start(f32[160,4096]{1,0:T(8,128)S(1)} %fusion.89) | copy-start | bytes 7864324 | tf_op jit(solution)/shard_map/while
  196.3 8.6 %copy-start.8 = (bf16[56,4096]{1,0:T(8,128)(2,1)S(1)}, bf16[56,4096]{1,0:T(8,128)(2,1)}, u32[]{:S(2)}) copy-start(bf16[56,4096]{1,0:T(8,128)(2,1)} %copy.29) | copy-start | bytes 1376260 | tf_op jit(solution)/shard_map/while
  196.3 8.6 %copy-start.10 = (bf16[56,4096]{1,0:T(8,128)(2,1)S(1)}, bf16[56,4096]{1,0:T(8,128)(2,1)}, u32[]{:S(2)}) copy-start(bf16[56,4096]{1,0:T(8,128)(2,1)} %copy.31) | copy-start | bytes 1376260 | tf_op jit(solution)/shard_map/while
  205.7 3.9 copy-start.7
  205.7 18.4 %collective-permute-start.1 = (bf16[56,4096]{1,0:T(8,128)(2,1)}, bf16[56,4096]{1,0:T(8,128)(2,1)S(1)}, u32[]{:S(2)}, u32[]{:S(2)}) collective-permute-start(bf16[56,4096]{1,0:T(8,128)(2,1)} %get-tuple-element.172), channel_id=1, source_target_pairs={{0,2},{2,4},{4,6},{6,8},{8,10},{10,12},{12,14},{14,16},{16,18},{18... | collective-permute-start | bytes 1376264 | tf_op jit(solution)/shard_map/while/body/eval_jaxpr/ppermute | solution.py:17
  209.6 15.3 %collective-permute-start = (bf16[56,4096]{1,0:T(8,128)(2,1)}, bf16[56,4096]{1,0:T(8,128)(2,1)S(1)}, u32[]{:S(2)}, u32[]{:S(2)}) collective-permute-start(bf16[56,4096]{1,0:T(8,128)(2,1)} %copy-done.7), channel_id=1, source_target_pairs={{0,2},{2,4},{4,6},{6,8},{8,10},{10,12},{12,14},{14,16},{16,18},{18... | collective-permute-start | bytes 1376264 | tf_op jit(solution)/shard_map/while/body/eval_jaxpr/ppermute | solution.py:17
  211.1 15.7 %collective-permute-start.2 = (bf16[56,4096]{1,0:T(8,128)(2,1)}, bf16[56,4096]{1,0:T(8,128)(2,1)}, u32[]{:S(2)}, u32[]{:S(2)}) collective-permute-start(bf16[56,4096]{1,0:T(8,128)(2,1)} %copy-done.9), channel_id=1, source_target_pairs={{0,2},{2,4},{4,6},{6,8},{8,10},{10,12},{12,14},{14,16},{16,18},{18... | collective-permute-start | bytes 1376264 | tf_op jit(solution)/shard_map/while/body/eval_jaxpr/ppermute | solution.py:17
  215.9 31.4 %collective-permute-start.5 = (f32[56,4096]{1,0:T(8,128)}, f32[56,4096]{1,0:T(8,128)}, u32[]{:S(2)}, u32[]{:S(2)}) collective-permute-start(f32[56,4096]{1,0:T(8,128)} %get-tuple-element.176), channel_id=1, source_target_pairs={{0,2},{2,4},{4,6},{6,8},{8,10},{10,12},{12,14},{14,16},{16,18},{18... | collective-permute-start | bytes 2752520 | tf_op jit(solution)/shard_map/while/body/eval_jaxpr/ppermute | solution.py:17
  216.6 28.2 %collective-permute-start.4 = (f32[56,4096]{1,0:T(8,128)}, f32[56,4096]{1,0:T(8,128)}, u32[]{:S(2)}, u32[]{:S(2)}) collective-permute-start(f32[56,4096]{1,0:T(8,128)} %get-tuple-element.175), channel_id=1, source_target_pairs={{0,2},{2,4},{4,6},{6,8},{8,10},{10,12},{12,14},{14,16},{16,18},{18... | collective-permute-start | bytes 2752520 | tf_op jit(solution)/shard_map/while/body/eval_jaxpr/ppermute | solution.py:17
  224.1 30.6 %collective-permute-start.3 = (f32[56,4096]{1,0:T(8,128)}, f32[56,4096]{1,0:T(8,128)S(1)}, u32[]{:S(2)}, u32[]{:S(2)}) collective-permute-start(f32[56,4096]{1,0:T(8,128)} %get-tuple-element.174), channel_id=1, source_target_pairs={{0,2},{2,4},{4,6},{6,8},{8,10},{10,12},{12,14},{14,16},{16,18},{18... | collective-permute-start | bytes 2752520 | tf_op jit(solution)/shard_map/while/body/eval_jaxpr/ppermute | solution.py:17
  231.8 18.0 %copy-start.2 = (f32[160,4096]{1,0:T(8,128)}, f32[160,4096]{1,0:T(8,128)S(1)}, u32[]{:S(2)}) copy-start(f32[160,4096]{1,0:T(8,128)S(1)} %fusion.89) | copy-start | bytes 7864324 | tf_op jit(solution)/shard_map/while
  247.3 8.6 %copy-start.8 = (bf16[56,4096]{1,0:T(8,128)(2,1)S(1)}, bf16[56,4096]{1,0:T(8,128)(2,1)}, u32[]{:S(2)}) copy-start(bf16[56,4096]{1,0:T(8,128)(2,1)} %copy.29) | copy-start | bytes 1376260 | tf_op jit(solution)/shard_map/while
  247.3 8.6 %copy-start.10 = (bf16[56,4096]{1,0:T(8,128)(2,1)S(1)}, bf16[56,4096]{1,0:T(8,128)(2,1)}, u32[]{:S(2)}) copy-start(bf16[56,4096]{1,0:T(8,128)(2,1)} %copy.31) | copy-start | bytes 1376260 | tf_op jit(solution)/shard_map/while
  256.7 3.9 copy-start.7
  256.7 22.6 %collective-permute-start.1 = (bf16[56,4096]{1,0:T(8,128)(2,1)}, bf16[56,4096]{1,0:T(8,128)(2,1)S(1)}, u32[]{:S(2)}, u32[]{:S(2)}) collective-permute-start(bf16[56,4096]{1,0:T(8,128)(2,1)} %get-tuple-element.172), channel_id=1, source_target_pairs={{0,2},{2,4},{4,6},{6,8},{8,10},{10,12},{12,14},{14,16},{16,18},{18... | collective-permute-start | bytes 1376264 | tf_op jit(solution)/shard_map/while/body/eval_jaxpr/ppermute | solution.py:17
  260.6 19.5 %collective-permute-start = (bf16[56,4096]{1,0:T(8,128)(2,1)}, bf16[56,4096]{1,0:T(8,128)(2,1)S(1)}, u32[]{:S(2)}, u32[]{:S(2)}) collective-permute-start(bf16[56,4096]{1,0:T(8,128)(2,1)} %copy-done.7), channel_id=1, source_target_pairs={{0,2},{2,4},{4,6},{6,8},{8,10},{10,12},{12,14},{14,16},{16,18},{18... | collective-permute-start | bytes 1376264 | tf_op jit(solution)/shard_map/while/body/eval_jaxpr/ppermute | solution.py:17
  263.0 19.0 %collective-permute-start.2 = (bf16[56,4096]{1,0:T(8,128)(2,1)}, bf16[56,4096]{1,0:T(8,128)(2,1)}, u32[]{:S(2)}, u32[]{:S(2)}) collective-permute-start(bf16[56,4096]{1,0:T(8,128)(2,1)} %copy-done.9), channel_id=1, source_target_pairs={{0,2},{2,4},{4,6},{6,8},{8,10},{10,12},{12,14},{14,16},{16,18},{18... | collective-permute-start | bytes 1376264 | tf_op jit(solution)/shard_map/while/body/eval_jaxpr/ppermute | solution.py:17
  267.8 30.5 %collective-permute-start.5 = (f32[56,4096]{1,0:T(8,128)}, f32[56,4096]{1,0:T(8,128)}, u32[]{:S(2)}, u32[]{:S(2)}) collective-permute-start(f32[56,4096]{1,0:T(8,128)} %get-tuple-element.176), channel_id=1, source_target_pairs={{0,2},{2,4},{4,6},{6,8},{8,10},{10,12},{12,14},{14,16},{16,18},{18... | collective-permute-start | bytes 2752520 | tf_op jit(solution)/shard_map/while/body/eval_jaxpr/ppermute | solution.py:17
  268.5 27.3 %collective-permute-start.4 = (f32[56,4096]{1,0:T(8,128)}, f32[56,4096]{1,0:T(8,128)}, u32[]{:S(2)}, u32[]{:S(2)}) collective-permute-start(f32[56,4096]{1,0:T(8,128)} %get-tuple-element.175), channel_id=1, source_target_pairs={{0,2},{2,4},{4,6},{6,8},{8,10},{10,12},{12,14},{14,16},{16,18},{18... | collective-permute-start | bytes 2752520 | tf_op jit(solution)/shard_map/while/body/eval_jaxpr/ppermute | solution.py:17
  279.3 26.3 %collective-permute-start.3 = (f32[56,4096]{1,0:T(8,128)}, f32[56,4096]{1,0:T(8,128)S(1)}, u32[]{:S(2)}, u32[]{:S(2)}) collective-permute-start(f32[56,4096]{1,0:T(8,128)} %get-tuple-element.174), channel_id=1, source_target_pairs={{0,2},{2,4},{4,6},{6,8},{8,10},{10,12},{12,14},{14,16},{16,18},{18... | collective-permute-start | bytes 2752520 | tf_op jit(solution)/shard_map/while/body/eval_jaxpr/ppermute | solution.py:17
  287.0 13.8 %copy-start.2 = (f32[160,4096]{1,0:T(8,128)}, f32[160,4096]{1,0:T(8,128)S(1)}, u32[]{:S(2)}) copy-start(f32[160,4096]{1,0:T(8,128)S(1)} %fusion.89) | copy-start | bytes 7864324 | tf_op jit(solution)/shard_map/while
  298.3 8.6 %copy-start.8 = (bf16[56,4096]{1,0:T(8,128)(2,1)S(1)}, bf16[56,4096]{1,0:T(8,128)(2,1)}, u32[]{:S(2)}) copy-start(bf16[56,4096]{1,0:T(8,128)(2,1)} %copy.29) | copy-start | bytes 1376260 | tf_op jit(solution)/shard_map/while
  298.3 8.6 %copy-start.10 = (bf16[56,4096]{1,0:T(8,128)(2,1)S(1)}, bf16[56,4096]{1,0:T(8,128)(2,1)}, u32[]{:S(2)}) copy-start(bf16[56,4096]{1,0:T(8,128)(2,1)} %copy.31) | copy-start | bytes 1376260 | tf_op jit(solution)/shard_map/while
  306.9 34.3 %copy-start.4 = (bf16[160,4096]{1,0:T(8,128)(2,1)S(1)}, bf16[160,4096]{1,0:T(8,128)(2,1)}, u32[]{:S(2)}) copy-start(bf16[160,4096]{1,0:T(8,128)(2,1)} %param.10) | copy-start | bytes 3932164
  306.9 34.3 %copy-start.11 = (f32[4096]{0:T(1024)S(1)}, f32[4096]{0:T(1024)}, u32[]{:S(2)}) copy-start(f32[4096]{0:T(1024)} %param.14) | copy-start | bytes 49156
  306.9 27.7 %collective-permute-start.9 = (f32[56,4096]{1,0:T(8,128)}, f32[56,4096]{1,0:T(8,128)}, u32[]{:S(2)}, u32[]{:S(2)}) collective-permute-start(f32[56,4096]{1,0:T(8,128)} %get-tuple-element.60), channel_id=1, source_target_pairs={{0,2},{2,4},{4,6},{6,8},{8,10},{10,12},{12,14},{14,16},{16,18},{18... | collective-permute-start | bytes 2752520 | tf_op jit(solution)/shard_map/ppermute | solution.py:17
  310.9 25.0 %collective-permute-start.10 = (f32[56,4096]{1,0:T(8,128)}, f32[56,4096]{1,0:T(8,128)}, u32[]{:S(2)}, u32[]{:S(2)}) collective-permute-start(f32[56,4096]{1,0:T(8,128)} %get-tuple-element.61), channel_id=1, source_target_pairs={{0,2},{2,4},{4,6},{6,8},{8,10},{10,12},{12,14},{14,16},{16,18},{18... | collective-permute-start | bytes 2752520 | tf_op jit(solution)/shard_map/ppermute | solution.py:17
  314.2 27.0 %collective-permute-start.11 = (f32[56,4096]{1,0:T(8,128)}, f32[56,4096]{1,0:T(8,128)}, u32[]{:S(2)}, u32[]{:S(2)}) collective-permute-start(f32[56,4096]{1,0:T(8,128)} %get-tuple-element.62), channel_id=1, source_target_pairs={{0,2},{2,4},{4,6},{6,8},{8,10},{10,12},{12,14},{14,16},{16,18},{18... | collective-permute-start | bytes 2752520 | tf_op jit(solution)/shard_map/ppermute | solution.py:17
  341.2 2.5 copy-start.3
  (9 other events, 11.8 us)
Sparse Core Ops, SparseCore 0:
  341.3 110.5 all-reduce.2
where the time goes:
time: 464 us; the launch traced here: 463 us
  waiting for transfers between devices  269 us (58%)
  starting transfers between devices  83.6 us (18%)
  matrix products  62.8 us (14%)
  local copies, waits for them, and re-layouts  20.9 us (5%)
  between operations  14.1 us (3%)
  other arithmetic  12.4 us (3%)
    ppermute x36, waiting for transfers between devices, passed_along(): return lax.ppermute(value, axis, pairs)  163 us
    psum x1, waiting for transfers between devices, shards(): summed = lax.psum((home[0], home[1], home[2]), 'rep')  106 us
    ppermute x36, starting transfers between devices, passed_along(): return lax.ppermute(value, axis, pairs)  83.6 us
    while x75, local copies, waits for them, and re-layouts  20.7 us
    dot_general x6, matrix products, local_terms(): jnp.einsum('tf,td->fd', hidden, grad_in, preferred_element_type=jnp.float32)  14 us
    dot_general x6, matrix products, local_terms(): jnp.einsum('tf,td->fd', dup, normed, preferred_element_type=jnp.float32)  13.5 us
  transfers between devices with their start and end apart: 37, of which 27 were waited for; matrix products, arithmetic and copies ran while one was open for 16% of the time, Pallas kernels for 0%

commit v1 on v0

v1 whole, which is shorter than its diff:
```python
import math

import jax
import jax.numpy as jnp
from jax import lax
from jax.sharding import PartitionSpec as P


AXES = ("blk", "rep")
BF, F32 = jnp.bfloat16, jnp.float32
epsilon = 1e-05


def hop(value, source_of):
    columns = lax.axis_size("blk") // 4
    pairs = []
    for c in range(columns):
        for q in range(2):
            for k in range(2):
                for r in range(2):
                    found = source_of(c, q, k, r)
                    if found is not None:
                        sc, sq, sk, sr = found
                        pairs.append(
                            (((sc % columns) * 4 + sq * 2 + sk) * 2 + sr, (c * 4 + q * 2 + k) * 2 + r)
                        )
    return lax.ppermute(value, AXES, pairs)


def core_swap(c, q, k, r):
    return c, q, 1 - k, r


def rep_swap(c, q, k, r):
    return c, q, k, 1 - r


def cross_swap(c, q, k, r):
    return c, 1 - q, k, 1 - r


def dot(a, b, contract):
    return lax.dot_general(a, b, (contract, ((), ())), preferred_element_type=F32)


def shards(block_inputs, out_cotangent, dnormed_in, carried_sums, norm_gain, w_gate, w_up, w_down):
    rows, width = block_inputs.shape
    units = w_gate.shape[0]
    half = width // 2
    blk, rep = lax.axis_index("blk"), lax.axis_index("rep")
    k, q = blk % 2, (blk // 2) % 2
    h = jnp.bitwise_xor(q, rep)
    scale = 1.0 / math.sqrt(lax.axis_size("blk") * rows * lax.axis_size("rep"))

    def mine(value):
        return lax.dynamic_slice_in_dim(value, h * half, half, value.ndim - 1)

    def other(value):
        return lax.dynamic_slice_in_dim(value, (1 - h) * half, half, value.ndim - 1)

    def joined(own, got):
        return jnp.concatenate([jnp.where(h == 0, own, got), jnp.where(h == 0, got, own)], axis=-1)

    cot_other = hop(other(out_cotangent), rep_swap)
    weights = [mine(w) for w in (w_gate, w_up, w_down)]
    second = [hop(w, lambda c, q, k, r: (c + 1, q, k, r)) for w in weights]
    near = hop(jnp.stack(weights), lambda c, q, k, r: (c, 1, k, 1 - r) if q == 0 else None)
    held = hop(carried_sums.astype(BF), lambda c, q, k, r: (c - 1, q, k, r))
    values = block_inputs.astype(F32)
    rstd = lax.rsqrt(jnp.mean(values * values, axis=-1, keepdims=True) + epsilon)
    normed = (values * rstd * norm_gain).astype(BF)
    norm_other = hop(other(normed), rep_swap)
    cot_mine, norm_mine = mine(out_cotangent), mine(normed)
    cot_mine_p = hop(cot_mine, core_swap)
    norm_mine_p = hop(norm_mine, core_swap)
    crossed = [hop(w, cross_swap) for w in second]
    far = [hop(w, lambda c, q, k, r: (c + 1, 1, k, r) if q == 1 else None) for w in crossed]
    cot_other_p = hop(cot_other, core_swap)
    norm_other_p = hop(norm_other, core_swap)
    held = hop(held, lambda c, q, k, r: (c, 0, k, 1 - r) if q == 1 else (c - 1, 1, k, 1 - r))
    held = mine(held).astype(F32) + hop(other(held), rep_swap).astype(F32)

    norms = (jnp.concatenate([norm_mine, norm_other]), jnp.concatenate([norm_mine_p, norm_other_p]))
    cots = (jnp.concatenate([cot_mine, cot_other]), jnp.concatenate([cot_mine_p, cot_other_p]))
    nt, tn, nn = ((1,), (1,)), ((0,), (0,)), ((1,), (0,))
    sums, met = [], []
    for i, w in enumerate(weights):
        first = jnp.where(q == 0, near[i], crossed[i])
        third = jnp.where(q == 0, crossed[i], far[i])
        both = (
            jnp.concatenate([first, second[i], third]),
            jnp.concatenate([first, second[i], jnp.where(k == 0, third, w)]),
        )
        met.append(both)
        left = norms if i < 2 else cots
        sums.append([dot(left[s], both[s], nt) for s in range(2)])
    held_units = 3 * units
    here = jnp.concatenate([jnp.concatenate([sums[i][s][:rows] for i in range(3)], axis=1) for s in range(2)])
    there = jnp.concatenate([jnp.concatenate([sums[i][s][rows:] for i in range(3)], axis=1) for s in range(2)])
    here = here + hop(there, rep_swap)
    gate = here[:, :held_units]
    upper = here[:, held_units : 2 * held_units]
    dhidden = here[:, 2 * held_units :]
    sigma = jax.nn.sigmoid(gate)
    act = gate * sigma
    hidden = (act * upper).astype(BF)
    dgate = (dhidden * upper * sigma * (1.0 + gate * (1.0 - sigma))).astype(BF)
    dup = (dhidden * act).astype(BF)
    acts = jnp.concatenate([dgate, dup, hidden], axis=1)
    acts_other = hop(acts, rep_swap)
    acts = [jnp.concatenate([acts[s * rows : (s + 1) * rows], acts_other[s * rows : (s + 1) * rows]]) for s in range(2)]

    finals = []
    for i in (2, 0, 1):
        right = norms if i < 2 else cots
        parts = [dot(acts[s][:, i * held_units : (i + 1) * held_units], right[s], tn) for s in range(2)]
        near_sums = parts[0][: 2 * units] + parts[1][: 2 * units]
        own, partner = parts[0][2 * units :], parts[1][2 * units :]
        third_sum = (own + jnp.where(k == 0, partner, 0.0)).astype(BF)
        along = hop(third_sum, lambda c, q, k, r: (c - 1, 1, k, r) if q == 1 else None)
        over = hop(third_sum, lambda c, q, k, r: (c, 0, k, 1 - r) if q == 1 else None)
        first_sum = near_sums[:units] + along.astype(F32)
        swapped = hop(first_sum.astype(BF), cross_swap)
        second_sum = near_sums[units:] + jnp.where(q == 0, swapped, over).astype(F32)
        home = hop(second_sum.astype(BF), lambda c, q, k, r: (c - 1, q, k, r)).astype(F32)
        total = held[i] + home + jnp.where(k == 1, partner, 0.0) + jnp.where(q == 1, swapped.astype(F32), 0.0)
        final = (total * scale).astype(BF)
        finals.append(joined(final, hop(final, rep_swap)))

    back = [
        dot(acts[s][:, :held_units], met[0][s], nn) + dot(acts[s][:, held_units : 2 * held_units], met[1][s], nn)
        for s in range(2)
    ]
    back = back[0] + hop(back[1], core_swap)
    back_got = hop(back[rows:].astype(BF), rep_swap).astype(F32)
    dnormed = dnormed_in + joined(back[:rows], back_got)
    scaled = norm_gain * dnormed
    dx = rstd * scaled - values * rstd**3 * jnp.mean(values * scaled, axis=-1, keepdims=True)
    input_grad = (out_cotangent.astype(F32) + dx).astype(BF)
    return (input_grad, finals[1], finals[2], finals[0])


def solution(mesh):
    placed = (
        P(("blk", "rep"), None),
        P(("blk", "rep"), None),
        P(("blk", "rep"), None),
        P(None, ("blk", "rep"), None),
        P(),
        P("blk", None),
        P("blk", None),
        P("blk", None),
    )

    def step(*args):
        return shards(*args)

    step = jax.shard_map(
        step,
        mesh=mesh,
        in_specs=placed,
        out_specs=(P(("blk", "rep"), None), P("blk", None), P("blk", None), P("blk", None)),
        check_vma=False,
    )
    return step
```

time: 464 us -> 222 us (0.48)
  the two profiles are of different devices: /device:TPU:1 before, /device:TPU:24 now
where the time goes in v1:
time: 222 us; the launch traced here: 221 us
  waiting for transfers between devices  110 us (50%)
  starting transfers between devices  52.2 us (24%)
  matrix products  21 us (9%)
  other arithmetic  18.4 us (8%)
  local copies, waits for them, and re-layouts  18.2 us (8%)
    ppermute x38, waiting for transfers between devices, hop(): return lax.ppermute(value, AXES, pairs)  110 us
    ppermute x38, starting transfers between devices, hop(): return lax.ppermute(value, AXES, pairs)  52.2 us
    dot_general x16, matrix products, dot(): lax.dot_general(a, b, (contract, ((), ())), preferred_element_type=F32)  21 us
    dynamic_slice x3, local copies, waits for them, and re-layouts, mine(): return lax.dynamic_slice_in_dim(value, h * half, half, value.ndim - 1)  5.02 us
  transfers between devices with their start and end apart: 38, of which 20 were waited for; matrix products, arithmetic and copies ran while one was open for 22% of the time, Pallas kernels for 0%

profile of v1, /device:TPU:24, one launch (start us, length us, event | category | flops | bytes accessed | tf_op | source)
XLA Modules:
  0.0 221.1 jit_solution(15155024470831157933)
XLA Ops:
  0.7 1.7 constant_dynamic-slice_fusion.3
  2.4 8.1 %collective-permute-start.9 = (bf16[56,2048]{1,0:T(8,128)(2,1)}, bf16[56,2048]{1,0:T(8,128)(2,1)}, u32[]{:S(2)}, u32[]{:S(2)}) collective-permute-start(bf16[56,2048]{1,0:T(8,128)(2,1)} %constant_dynamic-slice_fusion.3), channel_id=1, source_target_pairs={{8,0},{9,1},{10,2},{11,3},{12,4},{13,5},{14,6},{15,7},{16,8},{17,9... | collective-permute-start | bytes 688136 | tf_op jit(solution)/shard_map/ppermute | solution.py:27
  10.5 1.6 constant_dynamic-slice_fusion.4
  12.9 1.6 constant_dynamic-slice_fusion.5
  15.9 1.0 constant_dynamic-slice_fusion.6
  17.8 1.2 constant_dynamic-slice_fusion.1
  19.6 2.1 collective-permute-done.5
  21.9 3.6 %collective-permute-done.2 = bf16[56,2048]{1,0:T(8,128)(2,1)S(1)} collective-permute-done((bf16[56,2048]{1,0:T(8,128)(2,1)}, bf16[56,2048]{1,0:T(8,128)(2,1)S(1)}, u32[]{:S(2)}, u32[]{:S(2)}) %collective-permute-start.2) | collective-permute-done | bytes 229408 | tf_op jit(solution)/shard_map/ppermute | solution.py:27
  25.7 0.9 pad_maximum_fusion.4
  26.6 3.3 %collective-permute-done.10 = bf16[56,2048]{1,0:T(8,128)(2,1)} collective-permute-done((bf16[56,2048]{1,0:T(8,128)(2,1)}, bf16[56,2048]{1,0:T(8,128)(2,1)}, u32[]{:S(2)}, u32[]{:S(2)}) %collective-permute-start.10) | collective-permute-done | bytes 229408 | tf_op jit(solution)/shard_map/ppermute | solution.py:27
  29.9 3.6 %collective-permute-start.1 = (bf16[3,56,2048]{2,1,0:T(8,128)(2,1)}, bf16[3,56,2048]{2,1,0:T(8,128)(2,1)}, u32[]{:S(2)}, u32[]{:S(2)}) collective-permute-start(bf16[3,56,2048]{2,1,0:T(8,128)(2,1)} %pad_maximum_fusion.4), channel_id=1, source_target_pairs={{5,0},{4,1},{7,2},{6,3},{13,8},{12,9},{15,10},{14,11},{21,16},{20,... | collective-permute-start | bytes 2064392 | tf_op jit(solution)/shard_map/ppermute | solution.py:27
  34.2 3.0 %convert_element_type.114 = bf16[3,56,4096]{2,1,0:T(8,128)(2,1)} convert(f32[3,56,4096]{2,1,0:T(8,128)} %param.11) | non-fusion elementwise | flops 688128 | bytes 4128768 | tf_op jit(solution)/shard_map/convert_element_type | solution.py:68
  37.2 2.0 collective-permute-start.3
  39.2 1.1 constant_dynamic-update-slice_fusion.1
  40.4 10.2 %collective-permute-done.3 = bf16[56,2048]{1,0:T(8,128)(2,1)S(1)} collective-permute-done((bf16[56,2048]{1,0:T(8,128)(2,1)S(1)}, bf16[56,2048]{1,0:T(8,128)(2,1)S(1)}, u32[]{:S(2)}, u32[]{:S(2)}) %collective-permute-start.3) | collective-permute-done | bytes 229408 | tf_op jit(solution)/shard_map/ppermute | solution.py:27
  50.6 7.4 %collective-permute-start.11 = (bf16[56,2048]{1,0:T(8,128)(2,1)}, bf16[56,2048]{1,0:T(8,128)(2,1)S(1)}, u32[]{:S(2)}, u32[]{:S(2)}) collective-permute-start(bf16[56,2048]{1,0:T(8,128)(2,1)} %collective-permute-done.10), channel_id=1, source_target_pairs={{12,4},{13,5},{14,6},{15,7},{20,12},{21,13},{22,14},{23,15},{28,20... | collective-permute-start | bytes 688136 | tf_op jit(solution)/shard_map/ppermute | solution.py:27
  58.0 1.9 collective-permute-start.7
  59.9 1.9 collective-permute-start.4
  61.8 1.1 constant_dynamic-update-slice_fusion.3
  63.0 2.1 collective-permute-start.20
  65.1 2.9 %collective-permute-done.7 = bf16[56,2048]{1,0:T(8,128)(2,1)S(1)} collective-permute-done((bf16[56,2048]{1,0:T(8,128)(2,1)}, bf16[56,2048]{1,0:T(8,128)(2,1)S(1)}, u32[]{:S(2)}, u32[]{:S(2)}) %collective-permute-start.7) | collective-permute-done | bytes 229408 | tf_op jit(solution)/shard_map/ppermute | solution.py:27
  68.0 2.3 %collective-permute-done.4 = bf16[56,2048]{1,0:T(8,128)(2,1)S(1)} collective-permute-done((bf16[56,2048]{1,0:T(8,128)(2,1)S(1)}, bf16[56,2048]{1,0:T(8,128)(2,1)S(1)}, u32[]{:S(2)}, u32[]{:S(2)}) %collective-permute-start.4) | collective-permute-done | bytes 229408 | tf_op jit(solution)/shard_map/ppermute | solution.py:27
  70.4 2.0 fusion.50
  72.4 1.9 fusion.45
  75.0 2.0 fusion.11
  78.6 1.9 fusion.14
  81.2 1.6 fusion.42
  84.6 1.1 copy.12
  85.7 2.1 collective-permute-start.16
  87.8 13.4 %collective-permute-done.16 = f32[320,504]{1,0:T(8,128)} collective-permute-done((f32[320,504]{1,0:T(8,128)}, f32[320,504]{1,0:T(8,128)}, u32[]{:S(2)}, u32[]{:S(2)}) %collective-permute-start.16) | collective-permute-done | bytes 645152 | tf_op jit(solution)/shard_map/ppermute | solution.py:27
  101.2 1.3 copy.13
  102.6 1.5 maximum_add_fusion.1
  104.3 1.8 collective-permute-start.17
  106.3 6.7 %collective-permute-done.17 = bf16[320,504]{0,1:T(8,128)(2,1)} collective-permute-done((bf16[320,504]{0,1:T(8,128)(2,1)S(1)}, bf16[320,504]{0,1:T(8,128)(2,1)}, u32[]{:S(2)}, u32[]{:S(2)}) %collective-permute-start.17) | collective-permute-done | bytes 322592 | tf_op jit(solution)/shard_map/ppermute | solution.py:27
  113.0 1.2 fusion.82
  114.8 1.9 fusion.10
  116.8 1.3 collective-permute-start.35
  118.1 1.9 collective-permute-start.33
  123.4 1.4 collective-permute-start.30
  124.9 1.9 collective-permute-start.28
  126.8 1.5 fusion.41
  128.4 2.1 convolution_add_fusion
  130.5 16.1 %collective-permute-done.33 = bf16[56,2048]{1,0:T(8,128)(2,1)S(1)} collective-permute-done((bf16[56,2048]{1,0:T(8,128)(2,1)S(1)}, bf16[56,2048]{1,0:T(8,128)(2,1)S(1)}, u32[]{:S(2)}, u32[]{:S(2)}) %collective-permute-start.33) | collective-permute-done | bytes 229408 | tf_op jit(solution)/shard_map/ppermute | solution.py:27
  146.7 1.3 collective-permute-start.25
  148.0 1.1 collective-permute-done.28
  149.1 1.9 collective-permute-start.23
  151.1 9.3 %collective-permute-done.23 = bf16[56,2048]{1,0:T(8,128)(2,1)S(1)} collective-permute-done((bf16[56,2048]{1,0:T(8,128)(2,1)S(1)}, bf16[56,2048]{1,0:T(8,128)(2,1)S(1)}, u32[]{:S(2)}, u32[]{:S(2)}) %collective-permute-start.23) | collective-permute-done | bytes 229408 | tf_op jit(solution)/shard_map/ppermute | solution.py:27
  160.5 9.2 %collective-permute-done.34 = bf16[56,2048]{1,0:T(8,128)(2,1)S(1)} collective-permute-done((bf16[56,2048]{1,0:T(8,128)(2,1)S(1)}, bf16[56,2048]{1,0:T(8,128)(2,1)S(1)}, u32[]{:S(2)}, u32[]{:S(2)}) %collective-permute-start.34) | collective-permute-done | bytes 229408 | tf_op jit(solution)/shard_map/ppermute | solution.py:27
  169.8 3.3 %collective-permute-start.24 = (bf16[56,2048]{1,0:T(8,128)(2,1)S(1)}, bf16[56,2048]{1,0:T(8,128)(2,1)S(1)}, u32[]{:S(2)}, u32[]{:S(2)}) collective-permute-start(bf16[56,2048]{1,0:T(8,128)(2,1)S(1)} %fusion.34), channel_id=1, source_target_pairs={{5,0},{4,1},{7,2},{6,3},{1,4},{0,5},{3,6},{2,7},{13,8},{12,9},{15,... | collective-permute-start | bytes 688136 | tf_op jit(solution)/shard_map/ppermute | solution.py:27
  173.3 3.7 %collective-permute-done.29 = bf16[56,2048]{1,0:T(8,128)(2,1)S(1)} collective-permute-done((bf16[56,2048]{1,0:T(8,128)(2,1)S(1)}, bf16[56,2048]{1,0:T(8,128)(2,1)S(1)}, u32[]{:S(2)}, u32[]{:S(2)}) %collective-permute-start.29) | collective-permute-done | bytes 229408 | tf_op jit(solution)/shard_map/ppermute | solution.py:27
  177.1 2.3 %collective-permute-done.24 = bf16[56,2048]{1,0:T(8,128)(2,1)S(1)} collective-permute-done((bf16[56,2048]{1,0:T(8,128)(2,1)S(1)}, bf16[56,2048]{1,0:T(8,128)(2,1)S(1)}, u32[]{:S(2)}, u32[]{:S(2)}) %collective-permute-start.24) | collective-permute-done | bytes 229408 | tf_op jit(solution)/shard_map/ppermute | solution.py:27
  179.6 9.3 %collective-permute-done.22 = bf16[3,56,2048]{2,1,0:T(8,128)(2,1)S(1)} collective-permute-done((bf16[3,56,2048]{2,1,0:T(8,128)(2,1)S(1)}, bf16[3,56,2048]{2,1,0:T(8,128)(2,1)S(1)}, u32[]{:S(2)}, u32[]{:S(2)}) %collective-permute-start.22) | collective-permute-done | bytes 688160 | tf_op jit(solution)/shard_map/ppermute | solution.py:27
  189.2 1.1 fusion.24
  190.3 1.8 collective-permute-start.37
  192.1 1.5 fusion.44
  193.9 1.8 collective-permute-start.27
  195.7 2.1 collective-permute-done.37
  197.8 1.0 broadcast_select_fusion.1
  198.8 1.4 collective-permute-done.32
  201.0 1.6 collective-permute-done.27
  202.6 1.0 broadcast_select_fusion.5
  203.6 2.5 %fusion = f32[320,2048]{1,0:T(8,128)S(1)} fusion(f32[320,2048]{1,0:T(8,128)} %collective-permute-done.18, f32[320,2048]{1,0:T(8,128)S(1)} %fusion.44, bf16[56,2048]{1,0:T(8,128)(2,1)S(1)} %copy-done.24, bf16[56,2048]{1,0:T(8,128)(2,1)S(1)} %copy-done.22, bf16[56,2048]{1,0:T(8,128)(2,1)S(1)} %copy-done.12, bf16[160,504]{0,1:T(8,128)(2,1)S(1)} %get-tuple-element.33, ...), kind=kOutput, calls=%fused_computation.6 | convolution fusion | flops 223791104 | bytes 8875008 | tf_op jit(solution)/shard_map/dot_general | solution.py:43
  208.6 8.6 %collective-permute-done.19 = bf16[160,2048]{1,0:T(8,128)(2,1)S(1)} collective-permute-done((bf16[160,2048]{1,0:T(8,128)(2,1)S(1)}, bf16[160,2048]{1,0:T(8,128)(2,1)S(1)}, u32[]{:S(2)}, u32[]{:S(2)}) %collective-permute-start.19) | collective-permute-done | bytes 655392 | tf_op jit(solution)/shard_map/ppermute | solution.py:27
  218.9 2.3 %fusion.7 = bf16[160,4096]{1,0:T(8,128)(2,1)} fusion(bf16[160,4096]{1,0:T(8,128)(2,1)S(1)} %copy-done, bf16[160,4096]{1,0:T(8,128)(2,1)S(1)} %copy-done.6, f32[160]{0:T(256)S(1)} %broadcast_multiply_fusion, f32[160]{0:T(256)S(1)} %get-tuple-element.53, f32[160]{0:T(256)S(1)} %get-tuple-element.54, f32[160,4096]{1,0:T(8,128)S(1)} %copy-done.1, ...), kind=kLoop, calls=%fused_computation.13 | loop fusion | flops 7208960 | bytes 9193344 | tf_op jit(solution)/shard_map/convert_element_type | solution.py:139
  (148 shorter events, 20.0 us)
Async XLA Ops:
  0.6 14.5 %copy-start = (bf16[160,4096]{1,0:T(8,128)(2,1)S(1)}, bf16[160,4096]{1,0:T(8,128)(2,1)}, u32[]{:S(2)}) copy-start(bf16[160,4096]{1,0:T(8,128)(2,1)} %param.8) | copy-start | bytes 3932164
  0.6 14.8 %copy-start.31 = (f32[4096]{0:T(1024)S(1)}, f32[4096]{0:T(1024)}, u32[]{:S(2)}) copy-start(f32[4096]{0:T(1024)} %param.12) | copy-start | bytes 49156
  2.4 16.6 %collective-permute-start.9 = (bf16[56,2048]{1,0:T(8,128)(2,1)}, bf16[56,2048]{1,0:T(8,128)(2,1)}, u32[]{:S(2)}, u32[]{:S(2)}) collective-permute-start(bf16[56,2048]{1,0:T(8,128)(2,1)} %constant_dynamic-slice_fusion.3), channel_id=1, source_target_pairs={{8,0},{9,1},{10,2},{11,3},{12,4},{13,5},{14,6},{15,7},{16,8},{17,9... | collective-permute-start | bytes 688136 | tf_op jit(solution)/shard_map/ppermute | solution.py:27
  12.1 9.6 %collective-permute-start.5 = (bf16[56,2048]{1,0:T(8,128)(2,1)}, bf16[56,2048]{1,0:T(8,128)(2,1)}, u32[]{:S(2)}, u32[]{:S(2)}) collective-permute-start(bf16[56,2048]{1,0:T(8,128)(2,1)} %constant_dynamic-slice_fusion.4), channel_id=1, source_target_pairs={{8,0},{9,1},{10,2},{11,3},{12,4},{13,5},{14,6},{15,7},{16,8},{17,9... | collective-permute-start | bytes 688136 | tf_op jit(solution)/shard_map/ppermute | solution.py:27
  14.6 10.9 %collective-permute-start.2 = (bf16[56,2048]{1,0:T(8,128)(2,1)}, bf16[56,2048]{1,0:T(8,128)(2,1)S(1)}, u32[]{:S(2)}, u32[]{:S(2)}) collective-permute-start(bf16[56,2048]{1,0:T(8,128)(2,1)} %constant_dynamic-slice_fusion.5), channel_id=1, source_target_pairs={{8,0},{9,1},{10,2},{11,3},{12,4},{13,5},{14,6},{15,7},{16,8},{17,9... | collective-permute-start | bytes 688136 | tf_op jit(solution)/shard_map/ppermute | solution.py:27
  15.9 1.8 copy-start.5
  16.9 2.1 copy-start.2
  16.9 41.0 %collective-permute-start = (bf16[160,2048]{1,0:T(8,128)(2,1)}, bf16[160,2048]{1,0:T(8,128)(2,1)S(1)}, u32[]{:S(2)}, u32[]{:S(2)}) collective-permute-start(bf16[160,2048]{1,0:T(8,128)(2,1)} %get-tuple-element.15), channel_id=1, source_target_pairs={{1,0},{0,1},{3,2},{2,3},{5,4},{4,5},{7,6},{6,7},{9,8},{8,9},{11,10... | collective-permute-start | bytes 1966088 | tf_op jit(solution)/shard_map/ppermute | solution.py:27
  17.7 19.5 %collective-permute-start.12 = (bf16[160,2048]{1,0:T(8,128)(2,1)S(1)}, bf16[160,2048]{1,0:T(8,128)(2,1)}, u32[]{:S(2)}, u32[]{:S(2)}) collective-permute-start(bf16[160,2048]{1,0:T(8,128)(2,1)S(1)} %get-tuple-element.16), channel_id=1, source_target_pairs={{2,0},{3,1},{0,2},{1,3},{6,4},{7,5},{4,6},{5,7},{10,8},{11,9},{8,1... | collective-permute-start | bytes 1966088 | tf_op jit(solution)/shard_map/ppermute | solution.py:27
  19.0 40.9 %collective-permute-start.14 = (bf16[160,2048]{1,0:T(8,128)(2,1)}, bf16[160,2048]{1,0:T(8,128)(2,1)}, u32[]{:S(2)}, u32[]{:S(2)}) collective-permute-start(bf16[160,2048]{1,0:T(8,128)(2,1)} %get-tuple-element.18), channel_id=1, source_target_pairs={{2,0},{3,1},{0,2},{1,3},{6,4},{7,5},{4,6},{5,7},{10,8},{11,9},{8,1... | collective-permute-start | bytes 1966088 | tf_op jit(solution)/shard_map/ppermute | solution.py:27
  21.7 8.2 %collective-permute-start.10 = (bf16[56,2048]{1,0:T(8,128)(2,1)}, bf16[56,2048]{1,0:T(8,128)(2,1)}, u32[]{:S(2)}, u32[]{:S(2)}) collective-permute-start(bf16[56,2048]{1,0:T(8,128)(2,1)} %collective-permute-done.9), channel_id=1, source_target_pairs={{5,0},{4,1},{7,2},{6,3},{1,4},{0,5},{3,6},{2,7},{13,8},{12,9},{15,... | collective-permute-start | bytes 688136 | tf_op jit(solution)/shard_map/ppermute | solution.py:27
  25.5 57.4 %copy-start.21 = (bf16[56,2048]{1,0:T(8,128)(2,1)}, bf16[56,2048]{1,0:T(8,128)(2,1)S(1)}, u32[]{:S(2)}) copy-start(bf16[56,2048]{1,0:T(8,128)(2,1)S(1)} %collective-permute-done.2) | copy-start | bytes 688132
  25.5 8.7 %collective-permute-start.6 = (bf16[56,2048]{1,0:T(8,128)(2,1)}, bf16[56,2048]{1,0:T(8,128)(2,1)}, u32[]{:S(2)}, u32[]{:S(2)}) collective-permute-start(bf16[56,2048]{1,0:T(8,128)(2,1)} %collective-permute-done.5), channel_id=1, source_target_pairs={{5,0},{4,1},{7,2},{6,3},{1,4},{0,5},{3,6},{2,7},{13,8},{12,9},{15,... | collective-permute-start | bytes 688136 | tf_op jit(solution)/shard_map/ppermute | solution.py:27
  29.9 40.5 %collective-permute-start.1 = (bf16[3,56,2048]{2,1,0:T(8,128)(2,1)}, bf16[3,56,2048]{2,1,0:T(8,128)(2,1)}, u32[]{:S(2)}, u32[]{:S(2)}) collective-permute-start(bf16[3,56,2048]{2,1,0:T(8,128)(2,1)} %pad_maximum_fusion.4), channel_id=1, source_target_pairs={{5,0},{4,1},{7,2},{6,3},{13,8},{12,9},{15,10},{14,11},{21,16},{20,... | collective-permute-start | bytes 2064392 | tf_op jit(solution)/shard_map/ppermute | solution.py:27
  34.2 28.8 %collective-permute-start.8 = (bf16[160,2048]{1,0:T(8,128)(2,1)}, bf16[160,2048]{1,0:T(8,128)(2,1)}, u32[]{:S(2)}, u32[]{:S(2)}) collective-permute-start(bf16[160,2048]{1,0:T(8,128)(2,1)} %get-tuple-element.17), channel_id=1, source_target_pairs={{1,0},{0,1},{3,2},{2,3},{5,4},{4,5},{7,6},{6,7},{9,8},{8,9},{11,10... | collective-permute-start | bytes 1966088 | tf_op jit(solution)/shard_map/ppermute | solution.py:27
  37.2 33.1 %copy-start.16 = (bf16[56,4096]{1,0:T(8,128)(2,1)S(1)}, bf16[56,4096]{1,0:T(8,128)(2,1)}, u32[]{:S(2)}) copy-start(bf16[56,4096]{1,0:T(8,128)(2,1)} %param.13) | copy-start | bytes 1376260
  37.2 33.1 %copy-start.18 = (bf16[56,4096]{1,0:T(8,128)(2,1)S(1)}, bf16[56,4096]{1,0:T(8,128)(2,1)}, u32[]{:S(2)}) copy-start(bf16[56,4096]{1,0:T(8,128)(2,1)} %param.15) | copy-start | bytes 1376260
  37.2 33.1 %copy-start.20 = (bf16[56,4096]{1,0:T(8,128)(2,1)S(1)}, bf16[56,4096]{1,0:T(8,128)(2,1)}, u32[]{:S(2)}) copy-start(bf16[56,4096]{1,0:T(8,128)(2,1)} %param.14) | copy-start | bytes 1376260
  37.2 13.4 %collective-permute-start.3 = (bf16[56,2048]{1,0:T(8,128)(2,1)S(1)}, bf16[56,2048]{1,0:T(8,128)(2,1)S(1)}, u32[]{:S(2)}, u32[]{:S(2)}) collective-permute-start(bf16[56,2048]{1,0:T(8,128)(2,1)S(1)} %collective-permute-done.2), channel_id=1, source_target_pairs={{5,0},{4,1},{7,2},{6,3},{1,4},{0,5},{3,6},{2,7},{13,8},{12,9},{15,... | collective-permute-start | bytes 688136 | tf_op jit(solution)/shard_map/ppermute | solution.py:27
  50.6 14.5 %collective-permute-start.11 = (bf16[56,2048]{1,0:T(8,128)(2,1)}, bf16[56,2048]{1,0:T(8,128)(2,1)S(1)}, u32[]{:S(2)}, u32[]{:S(2)}) collective-permute-start(bf16[56,2048]{1,0:T(8,128)(2,1)} %collective-permute-done.10), channel_id=1, source_target_pairs={{12,4},{13,5},{14,6},{15,7},{20,12},{21,13},{22,14},{23,15},{28,20... | collective-permute-start | bytes 688136 | tf_op jit(solution)/shard_map/ppermute | solution.py:27
  58.0 16.4 %copy-start.9 = (bf16[160,2048]{1,0:T(8,128)(2,1)}, bf16[160,2048]{1,0:T(8,128)(2,1)S(1)}, u32[]{:S(2)}) copy-start(bf16[160,2048]{1,0:T(8,128)(2,1)S(1)} %collective-permute-done) | copy-start | bytes 1966084
  58.0 10.0 %collective-permute-start.7 = (bf16[56,2048]{1,0:T(8,128)(2,1)}, bf16[56,2048]{1,0:T(8,128)(2,1)S(1)}, u32[]{:S(2)}, u32[]{:S(2)}) collective-permute-start(bf16[56,2048]{1,0:T(8,128)(2,1)} %collective-permute-done.6), channel_id=1, source_target_pairs={{12,4},{13,5},{14,6},{15,7},{20,12},{21,13},{22,14},{23,15},{28,20... | collective-permute-start | bytes 688136 | tf_op jit(solution)/shard_map/ppermute | solution.py:27
  59.9 10.4 %collective-permute-start.4 = (bf16[56,2048]{1,0:T(8,128)(2,1)S(1)}, bf16[56,2048]{1,0:T(8,128)(2,1)S(1)}, u32[]{:S(2)}, u32[]{:S(2)}) collective-permute-start(bf16[56,2048]{1,0:T(8,128)(2,1)S(1)} %collective-permute-done.3), channel_id=1, source_target_pairs={{12,4},{13,5},{14,6},{15,7},{20,12},{21,13},{22,14},{23,15},{28,20... | collective-permute-start | bytes 688136 | tf_op jit(solution)/shard_map/ppermute | solution.py:27
  63.0 9.4 %copy-start.3 = (bf16[160,2048]{1,0:T(8,128)(2,1)S(1)}, bf16[160,2048]{1,0:T(8,128)(2,1)}, u32[]{:S(2)}) copy-start(bf16[160,2048]{1,0:T(8,128)(2,1)} %copy-done.2) | copy-start | bytes 1966084
  63.0 43.1 %collective-permute-start.20 = (bf16[3,56,4096]{2,1,0:T(8,128)(2,1)}, bf16[3,56,4096]{2,1,0:T(8,128)(2,1)}, u32[]{:S(2)}, u32[]{:S(2)}) collective-permute-start(bf16[3,56,4096]{2,1,0:T(8,128)(2,1)} %convert_element_type.114), channel_id=1, source_target_pairs={{248,0},{249,1},{250,2},{251,3},{252,4},{253,5},{254,6},{255,7},{0... | collective-permute-start | bytes 4128776 | tf_op jit(solution)/shard_map/ppermute | solution.py:27
  65.1 16.1 %collective-permute-start.13 = (bf16[160,2048]{1,0:T(8,128)(2,1)S(1)}, bf16[160,2048]{1,0:T(8,128)(2,1)S(1)}, u32[]{:S(2)}, u32[]{:S(2)}) collective-permute-start(bf16[160,2048]{1,0:T(8,128)(2,1)S(1)} %collective-permute-done), channel_id=1, source_target_pairs={{2,0},{3,1},{0,2},{1,3},{6,4},{7,5},{4,6},{5,7},{10,8},{11,9},{8,1... | collective-permute-start | bytes 1966088 | tf_op jit(solution)/shard_map/ppermute | solution.py:27
  68.0 10.5 %collective-permute-start.15 = (bf16[160,2048]{1,0:T(8,128)(2,1)}, bf16[160,2048]{1,0:T(8,128)(2,1)S(1)}, u32[]{:S(2)}, u32[]{:S(2)}) collective-permute-start(bf16[160,2048]{1,0:T(8,128)(2,1)} %collective-permute-done.8), channel_id=1, source_target_pairs={{2,0},{3,1},{0,2},{1,3},{6,4},{7,5},{4,6},{5,7},{10,8},{11,9},{8,1... | collective-permute-start | bytes 1966088 | tf_op jit(solution)/shard_map/ppermute | solution.py:27
  72.4 2.0 copy-start.27
  72.4 2.0 copy-start.23
  72.4 8.9 %copy-start.13 = (bf16[56,2048]{1,0:T(8,128)(2,1)}, bf16[56,2048]{1,0:T(8,128)(2,1)S(1)}, u32[]{:S(2)}) copy-start(bf16[56,2048]{1,0:T(8,128)(2,1)S(1)} %get-tuple-element.24) | copy-start | bytes 688132
  72.4 8.9 %copy-start.29 = (bf16[56,2048]{1,0:T(8,128)(2,1)}, bf16[56,2048]{1,0:T(8,128)(2,1)S(1)}, u32[]{:S(2)}) copy-start(bf16[56,2048]{1,0:T(8,128)(2,1)S(1)} %get-tuple-element.47) | copy-start | bytes 688132
  72.4 10.5 %copy-start.11 = (bf16[56,2048]{1,0:T(8,128)(2,1)}, bf16[56,2048]{1,0:T(8,128)(2,1)S(1)}, u32[]{:S(2)}) copy-start(bf16[56,2048]{1,0:T(8,128)(2,1)S(1)} %get-tuple-element.22) | copy-start | bytes 688132
  72.4 10.5 %copy-start.25 = (bf16[56,2048]{1,0:T(8,128)(2,1)}, bf16[56,2048]{1,0:T(8,128)(2,1)S(1)}, u32[]{:S(2)}) copy-start(bf16[56,2048]{1,0:T(8,128)(2,1)S(1)} %get-tuple-element.51) | copy-start | bytes 688132
  78.6 1.9 copy-start.7
  85.7 15.5 %collective-permute-start.16 = (f32[320,504]{1,0:T(8,128)}, f32[320,504]{1,0:T(8,128)}, u32[]{:S(2)}, u32[]{:S(2)}) collective-permute-start(f32[320,504]{1,0:T(8,128)} %copy.12), channel_id=1, source_target_pairs={{1,0},{0,1},{3,2},{2,3},{5,4},{4,5},{7,6},{6,7},{9,8},{8,9},{11,10... | collective-permute-start | bytes 1935368 | tf_op jit(solution)/shard_map/ppermute | solution.py:27
  104.3 8.7 %collective-permute-start.17 = (bf16[320,504]{0,1:T(8,128)(2,1)S(1)}, bf16[320,504]{0,1:T(8,128)(2,1)}, u32[]{:S(2)}, u32[]{:S(2)}) collective-permute-start(bf16[320,504]{0,1:T(8,128)(2,1)S(1)} %pad_maximum_fusion.17), channel_id=1, source_target_pairs={{1,0},{0,1},{3,2},{2,3},{5,4},{4,5},{7,6},{6,7},{9,8},{8,9},{11,10... | collective-permute-start | bytes 967688 | tf_op jit(solution)/shard_map/ppermute | solution.py:27
  106.1 8.1 %copy-start.8 = (bf16[320,2048]{1,0:T(8,128)(2,1)S(1)}, bf16[320,2048]{1,0:T(8,128)(2,1)}, u32[]{:S(2)}) copy-start(bf16[320,2048]{1,0:T(8,128)(2,1)} %copy-done.7) | copy-start | bytes 3932164
  106.1 63.7 %collective-permute-start.21 = (bf16[3,56,4096]{2,1,0:T(8,128)(2,1)}, bf16[3,56,4096]{2,1,0:T(8,128)(2,1)S(1)}, u32[]{:S(2)}, u32[]{:S(2)}) collective-permute-start(bf16[3,56,4096]{2,1,0:T(8,128)(2,1)} %collective-permute-done.20), channel_id=1, source_target_pairs={{253,0},{252,1},{255,2},{254,3},{1,4},{0,5},{3,6},{2,7},{5,8},{4,9... | collective-permute-start | bytes 4128776 | tf_op jit(solution)/shard_map/ppermute | solution.py:27
  116.8 43.6 %collective-permute-start.35 = (bf16[56,2048]{1,0:T(8,128)(2,1)S(1)}, bf16[56,2048]{1,0:T(8,128)(2,1)S(1)}, u32[]{:S(2)}, u32[]{:S(2)}) collective-permute-start(bf16[56,2048]{1,0:T(8,128)(2,1)S(1)} %fusion.17), channel_id=1, source_target_pairs={{1,4},{0,5},{3,6},{2,7},{9,12},{8,13},{11,14},{10,15},{17,20},{16,... | collective-permute-start | bytes 688136 | tf_op jit(solution)/shard_map/ppermute | solution.py:27
  118.1 28.6 %collective-permute-start.33 = (bf16[56,2048]{1,0:T(8,128)(2,1)S(1)}, bf16[56,2048]{1,0:T(8,128)(2,1)S(1)}, u32[]{:S(2)}, u32[]{:S(2)}) collective-permute-start(bf16[56,2048]{1,0:T(8,128)(2,1)S(1)} %fusion.17), channel_id=1, source_target_pairs={{252,4},{253,5},{254,6},{255,7},{4,12},{5,13},{6,14},{7,15},{12,20... | collective-permute-start | bytes 688136 | tf_op jit(solution)/shard_map/ppermute | solution.py:27
  123.3 3.5 %copy-start.14 = (bf16[56,2048]{1,0:T(8,128)(2,1)S(1)}, bf16[56,2048]{1,0:T(8,128)(2,1)}, u32[]{:S(2)}) copy-start(bf16[56,2048]{1,0:T(8,128)(2,1)} %copy-done.13) | copy-start | bytes 688132
  123.3 3.5 %copy-start.30 = (bf16[56,2048]{1,0:T(8,128)(2,1)S(1)}, bf16[56,2048]{1,0:T(8,128)(2,1)}, u32[]{:S(2)}) copy-start(bf16[56,2048]{1,0:T(8,128)(2,1)} %copy-done.29) | copy-start | bytes 688132
  123.4 5.0 %copy-start.12 = (bf16[56,2048]{1,0:T(8,128)(2,1)S(1)}, bf16[56,2048]{1,0:T(8,128)(2,1)}, u32[]{:S(2)}) copy-start(bf16[56,2048]{1,0:T(8,128)(2,1)} %copy-done.11) | copy-start | bytes 688132
  123.4 5.0 %copy-start.22 = (bf16[56,2048]{1,0:T(8,128)(2,1)S(1)}, bf16[56,2048]{1,0:T(8,128)(2,1)}, u32[]{:S(2)}) copy-start(bf16[56,2048]{1,0:T(8,128)(2,1)} %copy-done.21) | copy-start | bytes 688132
  123.4 5.0 %copy-start.26 = (bf16[56,2048]{1,0:T(8,128)(2,1)S(1)}, bf16[56,2048]{1,0:T(8,128)(2,1)}, u32[]{:S(2)}) copy-start(bf16[56,2048]{1,0:T(8,128)(2,1)} %copy-done.25) | copy-start | bytes 688132
  123.4 49.8 %collective-permute-start.30 = (bf16[56,2048]{1,0:T(8,128)(2,1)S(1)}, bf16[56,2048]{1,0:T(8,128)(2,1)S(1)}, u32[]{:S(2)}, u32[]{:S(2)}) collective-permute-start(bf16[56,2048]{1,0:T(8,128)(2,1)S(1)} %fusion.25), channel_id=1, source_target_pairs={{1,4},{0,5},{3,6},{2,7},{9,12},{8,13},{11,14},{10,15},{17,20},{16,... | collective-permute-start | bytes 688136 | tf_op jit(solution)/shard_map/ppermute | solution.py:27
  124.9 24.3 %collective-permute-start.28 = (bf16[56,2048]{1,0:T(8,128)(2,1)S(1)}, bf16[56,2048]{1,0:T(8,128)(2,1)S(1)}, u32[]{:S(2)}, u32[]{:S(2)}) collective-permute-start(bf16[56,2048]{1,0:T(8,128)(2,1)S(1)} %fusion.25), channel_id=1, source_target_pairs={{252,4},{253,5},{254,6},{255,7},{4,12},{5,13},{6,14},{7,15},{12,20... | collective-permute-start | bytes 688136 | tf_op jit(solution)/shard_map/ppermute | solution.py:27
  146.7 30.4 %collective-permute-start.25 = (bf16[56,2048]{1,0:T(8,128)(2,1)S(1)}, bf16[56,2048]{1,0:T(8,128)(2,1)S(1)}, u32[]{:S(2)}, u32[]{:S(2)}) collective-permute-start(bf16[56,2048]{1,0:T(8,128)(2,1)S(1)} %fusion.33), channel_id=1, source_target_pairs={{1,4},{0,5},{3,6},{2,7},{9,12},{8,13},{11,14},{10,15},{17,20},{16,... | collective-permute-start | bytes 688136 | tf_op jit(solution)/shard_map/ppermute | solution.py:27
  149.1 11.2 %collective-permute-start.23 = (bf16[56,2048]{1,0:T(8,128)(2,1)S(1)}, bf16[56,2048]{1,0:T(8,128)(2,1)S(1)}, u32[]{:S(2)}, u32[]{:S(2)}) collective-permute-start(bf16[56,2048]{1,0:T(8,128)(2,1)S(1)} %fusion.33), channel_id=1, source_target_pairs={{252,4},{253,5},{254,6},{255,7},{4,12},{5,13},{6,14},{7,15},{12,20... | collective-permute-start | bytes 688136 | tf_op jit(solution)/shard_map/ppermute | solution.py:27
  160.4 9.4 %collective-permute-start.34 = (bf16[56,2048]{1,0:T(8,128)(2,1)S(1)}, bf16[56,2048]{1,0:T(8,128)(2,1)S(1)}, u32[]{:S(2)}, u32[]{:S(2)}) collective-permute-start(bf16[56,2048]{1,0:T(8,128)(2,1)S(1)} %fusion.18), channel_id=1, source_target_pairs={{5,0},{4,1},{7,2},{6,3},{1,4},{0,5},{3,6},{2,7},{13,8},{12,9},{15,... | collective-permute-start | bytes 688136 | tf_op jit(solution)/shard_map/ppermute | solution.py:27
  160.4 43.2 %collective-permute-start.18 = (f32[320,2048]{1,0:T(8,128)}, f32[320,2048]{1,0:T(8,128)}, u32[]{:S(2)}, u32[]{:S(2)}) collective-permute-start(f32[320,2048]{1,0:T(8,128)} %convolution_add_fusion), channel_id=1, source_target_pairs={{2,0},{3,1},{0,2},{1,3},{6,4},{7,5},{4,6},{5,7},{10,8},{11,9},{8,1... | collective-permute-start | bytes 7864328 | tf_op jit(solution)/shard_map/ppermute | solution.py:27
  169.7 7.2 %collective-permute-start.29 = (bf16[56,2048]{1,0:T(8,128)(2,1)S(1)}, bf16[56,2048]{1,0:T(8,128)(2,1)S(1)}, u32[]{:S(2)}, u32[]{:S(2)}) collective-permute-start(bf16[56,2048]{1,0:T(8,128)(2,1)S(1)} %fusion.26), channel_id=1, source_target_pairs={{5,0},{4,1},{7,2},{6,3},{1,4},{0,5},{3,6},{2,7},{13,8},{12,9},{15,... | collective-permute-start | bytes 688136 | tf_op jit(solution)/shard_map/ppermute | solution.py:27
  169.8 9.6 %collective-permute-start.24 = (bf16[56,2048]{1,0:T(8,128)(2,1)S(1)}, bf16[56,2048]{1,0:T(8,128)(2,1)S(1)}, u32[]{:S(2)}, u32[]{:S(2)}) collective-permute-start(bf16[56,2048]{1,0:T(8,128)(2,1)S(1)} %fusion.34), channel_id=1, source_target_pairs={{5,0},{4,1},{7,2},{6,3},{1,4},{0,5},{3,6},{2,7},{13,8},{12,9},{15,... | collective-permute-start | bytes 688136 | tf_op jit(solution)/shard_map/ppermute | solution.py:27
  173.2 15.9 %collective-permute-start.36 = (bf16[56,2048]{1,0:T(8,128)(2,1)S(1)}, bf16[56,2048]{1,0:T(8,128)(2,1)S(1)}, u32[]{:S(2)}, u32[]{:S(2)}) collective-permute-start(bf16[56,2048]{1,0:T(8,128)(2,1)S(1)} %fusion.19), channel_id=1, source_target_pairs={{248,0},{249,1},{250,2},{251,3},{252,4},{253,5},{254,6},{255,7},{0... | collective-permute-start | bytes 688136 | tf_op jit(solution)/shard_map/ppermute | solution.py:27
  177.0 12.0 %collective-permute-start.22 = (bf16[3,56,2048]{2,1,0:T(8,128)(2,1)S(1)}, bf16[3,56,2048]{2,1,0:T(8,128)(2,1)S(1)}, u32[]{:S(2)}, u32[]{:S(2)}) collective-permute-start(bf16[3,56,2048]{2,1,0:T(8,128)(2,1)S(1)} %constant_dynamic-slice_fusion), channel_id=1, source_target_pairs={{1,0},{0,1},{3,2},{2,3},{5,4},{4,5},{7,6},{6,7},{9,8},{8,9},{11,10... | collective-permute-start | bytes 2064392 | tf_op jit(solution)/shard_map/ppermute | solution.py:27
  177.1 12.1 %collective-permute-start.31 = (bf16[56,2048]{1,0:T(8,128)(2,1)S(1)}, bf16[56,2048]{1,0:T(8,128)(2,1)S(1)}, u32[]{:S(2)}, u32[]{:S(2)}) collective-permute-start(bf16[56,2048]{1,0:T(8,128)(2,1)S(1)} %fusion.27), channel_id=1, source_target_pairs={{248,0},{249,1},{250,2},{251,3},{252,4},{253,5},{254,6},{255,7},{0... | collective-permute-start | bytes 688136 | tf_op jit(solution)/shard_map/ppermute | solution.py:27
  179.5 9.6 %collective-permute-start.26 = (bf16[56,2048]{1,0:T(8,128)(2,1)S(1)}, bf16[56,2048]{1,0:T(8,128)(2,1)S(1)}, u32[]{:S(2)}, u32[]{:S(2)}) collective-permute-start(bf16[56,2048]{1,0:T(8,128)(2,1)S(1)} %fusion.35), channel_id=1, source_target_pairs={{248,0},{249,1},{250,2},{251,3},{252,4},{253,5},{254,6},{255,7},{0... | collective-permute-start | bytes 688136 | tf_op jit(solution)/shard_map/ppermute | solution.py:27
  189.1 3.0 %copy-start.28 = (bf16[56,2048]{1,0:T(8,128)(2,1)S(1)}, bf16[56,2048]{1,0:T(8,128)(2,1)}, u32[]{:S(2)}) copy-start(bf16[56,2048]{1,0:T(8,128)(2,1)} %copy-done.27) | copy-start | bytes 688132
  190.3 7.6 %collective-permute-start.37 = (bf16[56,2048]{1,0:T(8,128)(2,1)S(1)}, bf16[56,2048]{1,0:T(8,128)(2,1)}, u32[]{:S(2)}, u32[]{:S(2)}) collective-permute-start(bf16[56,2048]{1,0:T(8,128)(2,1)S(1)} %get-tuple-element.12), channel_id=1, source_target_pairs={{1,0},{0,1},{3,2},{2,3},{5,4},{4,5},{7,6},{6,7},{9,8},{8,9},{11,10... | collective-permute-start | bytes 688136 | tf_op jit(solution)/shard_map/ppermute | solution.py:27
  193.6 6.6 %collective-permute-start.32 = (bf16[56,2048]{1,0:T(8,128)(2,1)S(1)}, bf16[56,2048]{1,0:T(8,128)(2,1)S(1)}, u32[]{:S(2)}, u32[]{:S(2)}) collective-permute-start(bf16[56,2048]{1,0:T(8,128)(2,1)S(1)} %get-tuple-element.13), channel_id=1, source_target_pairs={{1,0},{0,1},{3,2},{2,3},{5,4},{4,5},{7,6},{6,7},{9,8},{8,9},{11,10... | collective-permute-start | bytes 688136 | tf_op jit(solution)/shard_map/ppermute | solution.py:27
  193.9 8.7 %collective-permute-start.27 = (bf16[56,2048]{1,0:T(8,128)(2,1)}, bf16[56,2048]{1,0:T(8,128)(2,1)S(1)}, u32[]{:S(2)}, u32[]{:S(2)}) collective-permute-start(bf16[56,2048]{1,0:T(8,128)(2,1)} %get-tuple-element.14), channel_id=1, source_target_pairs={{1,0},{0,1},{3,2},{2,3},{5,4},{4,5},{7,6},{6,7},{9,8},{8,9},{11,10... | collective-permute-start | bytes 688136 | tf_op jit(solution)/shard_map/ppermute | solution.py:27
  198.8 4.8 %copy-start.24 = (bf16[56,2048]{1,0:T(8,128)(2,1)S(1)}, bf16[56,2048]{1,0:T(8,128)(2,1)}, u32[]{:S(2)}) copy-start(bf16[56,2048]{1,0:T(8,128)(2,1)} %copy-done.23) | copy-start | bytes 688132
  206.2 11.0 %collective-permute-start.19 = (bf16[160,2048]{1,0:T(8,128)(2,1)S(1)}, bf16[160,2048]{1,0:T(8,128)(2,1)S(1)}, u32[]{:S(2)}, u32[]{:S(2)}) collective-permute-start(bf16[160,2048]{1,0:T(8,128)(2,1)S(1)} %slice.396), channel_id=1, source_target_pairs={{1,0},{0,1},{3,2},{2,3},{5,4},{4,5},{7,6},{6,7},{9,8},{8,9},{11,10... | collective-permute-start | bytes 1966088 | tf_op jit(solution)/shard_map/ppermute | solution.py:27
  208.6 8.9 %copy-start.1 = (f32[160,4096]{1,0:T(8,128)S(1)}, f32[160,4096]{1,0:T(8,128)}, u32[]{:S(2)}) copy-start(f32[160,4096]{1,0:T(8,128)} %param.10) | copy-start | bytes 7864324
  (6 other events, 8.5 us)

commit v2 on v1

v2 whole, which is shorter than its diff:
```python
import functools
import math

import jax
import jax.numpy as jnp
from jax import lax
from jax.experimental import pallas as pl
from jax.experimental.pallas import tpu as pltpu
from jax.sharding import PartitionSpec as P


AXES = ("blk", "rep")
BF, F32 = jnp.bfloat16, jnp.float32
epsilon = 1e-05


def hop(value, source_of):
    columns = lax.axis_size("blk") // 4
    pairs = []
    for c in range(columns):
        for q in range(2):
            for k in range(2):
                for r in range(2):
                    found = source_of(c, q, k, r)
                    if found is not None:
                        sc, sq, sk, sr = found
                        pairs.append(
                            (((sc % columns) * 4 + sq * 2 + sk) * 2 + sr, (c * 4 + q * 2 + k) * 2 + r)
                        )
    return lax.ppermute(value, AXES, pairs)


def core_swap(c, q, k, r):
    return c, q, 1 - k, r


def rep_swap(c, q, k, r):
    return c, q, k, 1 - r


def cross_swap(c, q, k, r):
    return c, 1 - q, k, 1 - r


def dot(a, b, contract):
    return lax.dot_general(a, b, (contract, ((), ())), preferred_element_type=F32)


def scores_kernel(count, core, x_own, x_par, *refs):
    first, second, third, held_here = (refs[count * i : count * (i + 1)] for i in range(4))
    rows, units = x_own.shape[0], first[0].shape[0]
    tokens = jnp.concatenate([x_own[...], x_par[...]], axis=0)
    got = []
    for f, s, t, w in zip(first, second, third, held_here):
        last = jnp.where(core[0] == 0, t[...], w[...])
        out = dot(tokens, jnp.concatenate([f[...], s[...], t[...], last], axis=0), ((1,), (1,)))
        got.append(out[:rows, : 3 * units])
        got += [out[rows:, : 2 * units], out[rows:, 3 * units :]]
    refs[-1][...] = jnp.concatenate(got, axis=1)


def in_vmem(count):
    return [pl.BlockSpec(memory_space=pltpu.VMEM)] * count


def scores(core, x_own, x_par, sets, picked):
    rows, half = x_own.shape
    columns = 6 * len(picked) * sets[0][0].shape[0]
    return pl.pallas_call(
        functools.partial(scores_kernel, len(picked)),
        out_shape=jax.ShapeDtypeStruct((rows, columns), F32),
        in_specs=[pl.BlockSpec(memory_space=pltpu.SMEM)] + in_vmem(2 + 4 * len(picked)),
        out_specs=in_vmem(1)[0],
        cost_estimate=pl.CostEstimate(
            flops=2 * rows * columns * half, bytes_accessed=4 * rows * half + 2 * columns * half, transcendentals=0
        ),
    )(core, x_own, x_par, *(group[i] for group in sets for i in picked))


def back_kernel(core, acts_mine, acts_other, *refs):
    sets, outs = [x[...] for x in refs[:8]], refs[8:]
    units = sets[0].shape[0]
    span = 3 * units
    last = [jnp.where(core[0] == 0, sets[4 + i], sets[6 + i]) for i in range(2)]
    for s, tail in enumerate((sets[4:6], last)):
        met = jnp.concatenate([x for i in range(2) for x in (sets[i], sets[2 + i], tail[i])], axis=0)
        for o, acts in enumerate((acts_other, acts_mine)):
            value = acts[...]
            lhs = jnp.concatenate(
                [value[:, span * s : span * (s + 1)], value[:, span * (2 + s) : span * (3 + s)]], axis=1
            )
            outs[2 * s + o][...] = dot(lhs, met, ((1,), (0,)))


def back_sums(core, acts_mine, acts_other, sets):
    rows = acts_mine.shape[0]
    units, half = sets[0][0].shape
    return pl.pallas_call(
        back_kernel,
        out_shape=[jax.ShapeDtypeStruct((rows, half), F32)] * 4,
        in_specs=[pl.BlockSpec(memory_space=pltpu.SMEM)] + in_vmem(10),
        out_specs=in_vmem(4),
        name="back",
        cost_estimate=pl.CostEstimate(
            flops=48 * rows * units * half, bytes_accessed=16 * rows * half + 16 * units * half, transcendentals=0
        ),
    )(core, acts_mine, acts_other, *(group[i] for group in sets for i in range(2)))


def gradient_kernel(i, core, acts_mine, acts_other, t_mine, t_other, t_mine_p, t_other_p, *outs):
    third_out, first_out, second_out, home_out = outs
    rows, half = t_mine.shape
    units = third_out.shape[0]
    even = core[0] == 0
    span = 3 * units
    lhs = []
    for acts in (acts_mine, acts_other):
        value = acts[...].astype(F32)[:, 2 * span * i : 2 * span * (i + 1)]
        none = jnp.zeros((rows, units), F32)
        lhs.append(jnp.concatenate([value[:, :span], none], axis=1))
        lhs.append(jnp.concatenate([value[:, span : span + 2 * units], none, value[:, span + 2 * units :]], axis=1))
    lhs = jnp.transpose(jnp.concatenate(lhs, axis=0)).astype(BF)
    step = 512
    for at in range(0, half, step):
        cols = slice(at, at + step)
        tokens = jnp.concatenate([t[:, cols] for t in (t_mine, t_mine_p, t_other, t_other_p)], axis=0)
        out = dot(lhs, tokens, ((1,), (0,)))
        first_out[:, cols] = out[:units]
        second_out[:, cols] = out[units : 2 * units]
        last = out[3 * units :]
        third_out[:, cols] = (out[2 * units : 3 * units] + jnp.where(even, last, 0.0)).astype(BF)
        home_out[:, cols] = jnp.where(even, 0.0, last)


def gradient(i, core, acts_mine, acts_other, tokens, units):
    rows, half = tokens[0].shape
    vmem = pl.BlockSpec(memory_space=pltpu.VMEM)
    return pl.pallas_call(
        functools.partial(gradient_kernel, i),
        out_shape=[jax.ShapeDtypeStruct((units, half), kind) for kind in (BF, F32, F32, F32)],
        in_specs=[pl.BlockSpec(memory_space=pltpu.SMEM)] + [vmem] * 6,
        out_specs=[vmem] * 4,
        cost_estimate=pl.CostEstimate(
            flops=24 * rows * units * half, bytes_accessed=8 * rows * half + 14 * units * half, transcendentals=0
        ),
    )(core, acts_mine, acts_other, *tokens)


def shards(block_inputs, out_cotangent, dnormed_in, carried_sums, norm_gain, w_gate, w_up, w_down):
    rows, width = block_inputs.shape
    units = w_gate.shape[0]
    half = width // 2
    blk, rep = lax.axis_index("blk"), lax.axis_index("rep")
    k, q = blk % 2, (blk // 2) % 2
    h = jnp.bitwise_xor(q, rep)
    scale = 1.0 / math.sqrt(lax.axis_size("blk") * rows * lax.axis_size("rep"))

    def mine(value):
        return lax.dynamic_slice_in_dim(value, h * half, half, value.ndim - 1)

    def other(value):
        return lax.dynamic_slice_in_dim(value, (1 - h) * half, half, value.ndim - 1)

    def joined(own, got):
        return jnp.concatenate([jnp.where(h == 0, own, got), jnp.where(h == 0, got, own)], axis=-1)

    cot_other = hop(other(out_cotangent), rep_swap)
    weights = [mine(w) for w in (w_gate, w_up, w_down)]
    weights = list(lax.optimization_barrier(tuple(weights)))
    second = [hop(w, lambda c, q, k, r: (c + 1, q, k, r)) for w in weights]
    held = hop(carried_sums.astype(BF), lambda c, q, k, r: (c - 1, q, k, r))
    values = block_inputs.astype(F32)
    rstd = lax.rsqrt(jnp.mean(values * values, axis=-1, keepdims=True) + epsilon)
    normed = (values * rstd * norm_gain).astype(BF)
    norm_other = hop(other(normed), rep_swap)
    cot_mine, norm_mine = mine(out_cotangent), mine(normed)
    cot_mine_p = hop(cot_mine, core_swap)
    norm_mine_p = hop(norm_mine, core_swap)
    first = [hop(jnp.where(q == 0, s, w), cross_swap) for s, w in zip(second, weights)]
    third = [hop(w, lambda c, q, k, r: (c + 1, q, k, r)) for w in first]
    cot_other_p = hop(cot_other, core_swap)
    norm_other_p = hop(norm_other, core_swap)
    held = hop(held, lambda c, q, k, r: (c, 0, k, 1 - r) if q == 1 else (c - 1, 1, k, 1 - r))
    held = mine(held).astype(F32) + hop(other(held), rep_swap).astype(F32)

    held_units = 3 * units
    core = jnp.full((1,), k, jnp.int32)
    sets = (first, second, third, weights)
    dhidden = scores(core, cot_other, cot_other_p, sets, (2,))
    got = hop(dhidden, rep_swap)
    dhidden = scores(core, cot_mine, cot_mine_p, sets, (2,)) + got
    pre = scores(core, norm_other, norm_other_p, sets, (0, 1))
    got = hop(pre, rep_swap)
    pre = scores(core, norm_mine, norm_mine_p, sets, (0, 1)) + got
    gate, upper = pre[:, : 2 * held_units], pre[:, 2 * held_units :]
    sigma = jax.nn.sigmoid(gate)
    act = gate * sigma
    hidden = (act * upper).astype(BF)
    hidden_other = hop(hidden, rep_swap)
    dgate = (dhidden * upper * sigma * (1.0 + gate * (1.0 - sigma))).astype(BF)
    dup = (dhidden * act).astype(BF)
    acts = jnp.concatenate([dgate, dup], axis=1)
    acts_other = hop(acts, rep_swap)

    norms = (norm_mine, norm_other, norm_mine_p, norm_other_p)
    cots = (cot_mine, cot_other, cot_mine_p, cot_other_p)
    finals = []
    for i in (2, 0, 1):
        third_sum, first_sum, second_sum, home_sum = gradient(
            *((i, core, acts, acts_other, norms) if i < 2 else (0, core, hidden, hidden_other, cots)), units
        )
        along = hop(third_sum, lambda c, q, k, r: (c - 1, q, k, r))
        swapped = hop((first_sum + along.astype(F32)).astype(BF), cross_swap).astype(F32)
        second_sum = second_sum + jnp.where(q == 0, swapped, 0.0)
        home = hop(second_sum.astype(BF), lambda c, q, k, r: (c - 1, q, k, r)).astype(F32)
        total = held[i] + home + home_sum + jnp.where(q == 1, swapped, 0.0)
        final = (total * scale).astype(BF)
        finals.append((final, hop(final, rep_swap)))

    own_other, own_mine, par_other, par_mine = back_sums(core, acts, acts_other, sets)
    back_other = own_other + hop(par_other, core_swap)
    back_got = hop(back_other.astype(BF), rep_swap).astype(F32)
    back_mine = own_mine + hop(par_mine, core_swap)
    dnormed = dnormed_in + joined(back_mine, back_got)
    scaled = norm_gain * dnormed
    dx = rstd * scaled - values * rstd**3 * jnp.mean(values * scaled, axis=-1, keepdims=True)
    input_grad = (out_cotangent.astype(F32) + dx).astype(BF)
    finals = [joined(final, lax.optimization_barrier((got, input_grad))[0]) for final, got in finals]
    return (input_grad, finals[1], finals[2], finals[0])


def solution(mesh):
    placed = (
        P(("blk", "rep"), None),
        P(("blk", "rep"), None),
        P(("blk", "rep"), None),
        P(None, ("blk", "rep"), None),
        P(),
        P("blk", None),
        P("blk", None),
        P("blk", None),
    )

    def step(*args):
        return shards(*args)

    step = jax.shard_map(
        step,
        mesh=mesh,
        in_specs=placed,
        out_specs=(P(("blk", "rep"), None), P("blk", None), P("blk", None), P("blk", None)),
        check_vma=False,
    )
    return step
```

time: 222 us -> 206 us (0.928)
  Pallas kernels: 0 us -> 29.6 us
  matrix products: 21 us -> 0 us
  starting transfers between devices: 52.2 us -> 32.7 us
  local copies, waits for them, and re-layouts: 18.2 us -> 9.41 us
  waiting for transfers between devices: 110 us -> 115 us
    pallas_call x0 -> x8, Pallas kernels: none -> 29.6 us  [the longest x4 12.9 us: scores(): pl.pallas_call(functools.partial(scores_kernel, len(picked)), out_shape=j...]
    dot_general x16 -> x0, matrix products: 21 us -> none  [dot(): lax.dot_general(a, b, (contract, ((), ())), preferred_element_type=F32)]
    ppermute x38 -> x37, starting transfers between devices: 52.2 us -> 32.7 us  [hop(): return lax.ppermute(value, AXES, pairs)]
    ppermute x38 -> x37, waiting for transfers between devices: 110 us -> 115 us  [hop(): return lax.ppermute(value, AXES, pairs)]
    slice x7 -> x0, local copies, waits for them, and re-layouts: 4.49 us -> none  [the longest x4 3.06 us: shards(): sums[i][s][:rows]]
    convert_element_type x6 -> x4, other arithmetic: 0.3 us -> 3.46 us  [the longest x3 3.28 us: shards(): (first_sum + along.astype(F32)).astype(BF)]
    dynamic_slice x3 -> x2, local copies, waits for them, and re-layouts: 5.02 us -> 1.88 us  [mine(): return lax.dynamic_slice_in_dim(value, h * half, half, value.ndim - 1)]
    unnamed x66 -> x64, local copies, waits for them, and re-layouts: 3.77 us -> 5.38 us
  transfers between devices with their start and end apart: 38 -> 37, of which waited for: 20 -> 17; matrix products, arithmetic and copies ran while one was open for 22% -> 8% of each run, Pallas kernels for 0% -> 14%
where the time goes in v2:
time: 206 us; the launch traced here: 205 us
  waiting for transfers between devices  115 us (56%)
  starting transfers between devices  32.7 us (16%)
  Pallas kernels  29.6 us (14%)
  other arithmetic  16.9 us (8%)
  local copies, waits for them, and re-layouts  9.41 us (5%)
    ppermute x37, waiting for transfers between devices, hop(): return lax.ppermute(value, AXES, pairs)  115 us
    ppermute x37, starting transfers between devices, hop(): return lax.ppermute(value, AXES, pairs)  32.7 us
    pallas_call x4, Pallas kernels, scores(): pl.pallas_call(functools.partial(scores_kernel, len(picked)), out_shape=j...  12.9 us
    pallas_call x3, Pallas kernels, gradient(): pl.pallas_call(functools.partial(gradient_kernel, i), out_shape=[jax.Shap...  12.1 us
    unnamed x64, local copies, waits for them, and re-layouts  5.38 us
    pallas_call x1, Pallas kernels, back_sums(): pl.pallas_call(back_kernel, out_shape=[jax.ShapeDtypeStruct((rows, half),...  4.62 us
  transfers between devices with their start and end apart: 37, of which 17 were waited for; matrix products, arithmetic and copies ran while one was open for 8% of the time, Pallas kernels for 14%

profile of v2, /device:TPU:24, one launch (start us, length us, event | category | flops | bytes accessed | tf_op | source)
XLA Modules:
  0.0 205.2 jit_solution(6150985948483258495)
XLA Ops:
  0.7 1.0 copy-done
  1.7 1.9 constant_dynamic-slice_fusion.4
  3.6 8.1 %collective-permute-start.1 = (bf16[56,2048]{1,0:T(8,128)(2,1)}, bf16[56,2048]{1,0:T(8,128)(2,1)}, u32[]{:S(2)}, u32[]{:S(2)}) collective-permute-start(bf16[56,2048]{1,0:T(8,128)(2,1)} %get-tuple-element.26.refs_3_), channel_id=1, source_target_pairs={{8,0},{9,1},{10,2},{11,3},{12,4},{13,5},{14,6},{15,7},{16,8},{17,9... | collective-permute-start | bytes 688136 | tf_op jit(solution)/shard_map/ppermute | solution.py:30
  11.6 1.1 constant_dynamic-slice_fusion.3
  12.7 0.7 collective-permute-start.4
  13.5 0.8 collective-permute-start.10
  14.3 0.5 collective-permute-start.8
  15.2 0.6 multiply_multiply_fusion
  16.2 1.0 constant_dynamic-slice_fusion.1
  17.1 1.3 collective-permute-start.14
  18.4 4.3 %collective-permute-done.10.refs_3_ = bf16[56,2048]{1,0:T(8,128)(2,1)} collective-permute-done((bf16[56,2048]{1,0:T(8,128)(2,1)S(1)}, bf16[56,2048]{1,0:T(8,128)(2,1)}, u32[]{:S(2)}, u32[]{:S(2)}) %collective-permute-start.10) | collective-permute-done | bytes 229408 | tf_op jit(solution)/shard_map/ppermute | solution.py:30
  22.8 1.4 collective-permute-start.11
  24.2 2.3 %collective-permute-done.8.refs_2_ = bf16[56,2048]{1,0:T(8,128)(2,1)} collective-permute-done((bf16[56,2048]{1,0:T(8,128)(2,1)S(1)}, bf16[56,2048]{1,0:T(8,128)(2,1)}, u32[]{:S(2)}, u32[]{:S(2)}) %collective-permute-start.8) | collective-permute-done | bytes 229408 | tf_op jit(solution)/shard_map/ppermute | solution.py:30
  26.5 1.2 collective-permute-start.9
  27.8 15.4 %collective-permute-done.14.x_own.t_other = bf16[160,2048]{1,0:T(8,128)(2,1)S(1)} collective-permute-done((bf16[160,2048]{1,0:T(8,128)(2,1)}, bf16[160,2048]{1,0:T(8,128)(2,1)S(1)}, u32[]{:S(2)}, u32[]{:S(2)}) %collective-permute-start.14) | collective-permute-done | bytes 655392 | tf_op jit(solution)/shard_map/ppermute | solution.py:30
  43.2 1.2 broadcast_select_fusion.8
  44.7 0.8 collective-permute-start.13
  45.6 0.5 collective-permute-start.12
  46.1 3.0 %convert_element_type.98 = bf16[3,56,4096]{2,1,0:T(8,128)(2,1)} convert(f32[3,56,4096]{2,1,0:T(8,128)} %param.11) | non-fusion elementwise | flops 688128 | bytes 4128768 | tf_op jit(solution)/shard_map/convert_element_type | solution.py:171
  49.2 4.4 %collective-permute-done.2.refs_0_ = bf16[56,2048]{1,0:T(8,128)(2,1)} collective-permute-done((bf16[56,2048]{1,0:T(8,128)(2,1)S(1)}, bf16[56,2048]{1,0:T(8,128)(2,1)}, u32[]{:S(2)}, u32[]{:S(2)}) %collective-permute-start.2) | collective-permute-done | bytes 229408 | tf_op jit(solution)/shard_map/ppermute | solution.py:30
  53.7 3.6 %collective-permute-done.12.refs_4_ = bf16[56,2048]{1,0:T(8,128)(2,1)S(1)} collective-permute-done((bf16[56,2048]{1,0:T(8,128)(2,1)S(1)}, bf16[56,2048]{1,0:T(8,128)(2,1)S(1)}, u32[]{:S(2)}, u32[]{:S(2)}) %collective-permute-start.12) | collective-permute-done | bytes 229408 | tf_op jit(solution)/shard_map/ppermute | solution.py:30
  57.3 0.7 copy-done.17
  58.0 0.9 copy-done.5
  58.9 4.1 %collective-permute-start.3 = (bf16[56,2048]{1,0:T(8,128)(2,1)}, bf16[56,2048]{1,0:T(8,128)(2,1)S(1)}, u32[]{:S(2)}, u32[]{:S(2)}) collective-permute-start(bf16[56,2048]{1,0:T(8,128)(2,1)} %collective-permute-done.2.refs_0_), channel_id=1, source_target_pairs={{8,0},{9,1},{10,2},{11,3},{12,4},{13,5},{14,6},{15,7},{16,8},{17,9... | collective-permute-start | bytes 688136 | tf_op jit(solution)/shard_map/ppermute | solution.py:30
  63.0 3.6 %shard_map.114 = f32[160,672]{1,0:T(8,128)} custom-call(s32[1]{0:T(128)} %bitcast.core, bf16[160,2048]{1,0:T(8,128)(2,1)} %copy-done.4, bf16[160,2048]{1,0:T(8,128)(2,1)} %copy-done.5, bf16[56,2048]{1,0:T(8,128)(2,1)} %copy-done.15, bf16[56,2048]{1,0:T(8,128)(2,1)} %copy-done.14, bf16[56,2048]{1,0:T(8,128)(2,1)} %collective-permute-done.8.refs_2_, ...), custom_call_target="tpu_custom_call" | custom-call | flops 440401920 | bytes 4063232 | tf_op jit(solution)/shard_map/pallas_call | solution.py:69
  66.6 1.6 collective-permute-done.3.refs_2_
  68.2 0.8 collective-permute-start.16
  69.0 2.8 %shard_map.112 = f32[160,336]{1,0:T(8,128)} custom-call(s32[1]{0:T(128)} %bitcast.core, bf16[160,2048]{1,0:T(8,128)(2,1)} %collective-permute-done.4.x_own.t_other, bf16[160,2048]{1,0:T(8,128)(2,1)} %collective-permute-done.5.x_par.t_other_p, bf16[56,2048]{1,0:T(8,128)(2,1)} %collective-permute-done.2.refs_0_, ...), custom_call_target="tpu_custom_call" | custom-call | flops 220200960 | bytes 2686976 | tf_op jit(solution)/shard_map/pallas_call | solution.py:69
  71.9 1.2 collective-permute-start.6
  73.1 2.8 %shard_map.111 = f32[160,336]{1,0:T(8,128)} custom-call(s32[1]{0:T(128)} %bitcast.core, bf16[160,2048]{1,0:T(8,128)(2,1)} %get-tuple-element.56.x_own.t_mine, bf16[160,2048]{1,0:T(8,128)(2,1)} %collective-permute-done.x_par.t_mine_p, bf16[56,2048]{1,0:T(8,128)(2,1)} %collective-permute-done.2.refs_0_, bf16[56,2048]{1,0:T(8,128)(2,1)} %collective-permute-done.1.refs_1_, ...), custom_call_target="tpu_custom_call" | custom-call | flops 220200960 | bytes 2686976 | tf_op jit(solution)/shard_map/pallas_call | solution.py:69
  75.9 3.6 %shard_map.113 = f32[160,672]{1,0:T(8,128)} custom-call(s32[1]{0:T(128)} %bitcast.core, bf16[160,2048]{1,0:T(8,128)(2,1)} %copy-done.3, bf16[160,2048]{1,0:T(8,128)(2,1)} %collective-permute-done.7.x_par.t_mine_p, bf16[56,2048]{1,0:T(8,128)(2,1)} %copy-done.15, bf16[56,2048]{1,0:T(8,128)(2,1)} %copy-done.14, ...), custom_call_target="tpu_custom_call" | custom-call | flops 440401920 | bytes 4063232 | tf_op jit(solution)/shard_map/pallas_call | solution.py:69
  79.5 3.0 %collective-permute-done.16 = f32[160,672]{1,0:T(8,128)S(1)} collective-permute-done((f32[160,672]{1,0:T(8,128)}, f32[160,672]{1,0:T(8,128)S(1)}, u32[]{:S(2)}, u32[]{:S(2)}) %collective-permute-start.16) | collective-permute-done | bytes 430112 | tf_op jit(solution)/shard_map/ppermute | solution.py:30
  82.5 1.1 add.114
  83.6 2.2 %collective-permute-done.6 = f32[160,336]{1,0:T(8,128)S(1)} collective-permute-done((f32[160,336]{1,0:T(8,128)}, f32[160,336]{1,0:T(8,128)S(1)}, u32[]{:S(2)}, u32[]{:S(2)}) %collective-permute-start.6) | collective-permute-done | bytes 215072 | tf_op jit(solution)/shard_map/ppermute | solution.py:30
  86.1 0.9 collective-permute-start.17
  87.0 1.2 collective-permute-start.32
  88.3 6.7 %collective-permute-done.32.acts_other = bf16[160,336]{1,0:T(8,128)(2,1)S(1)} collective-permute-done((bf16[160,336]{1,0:T(8,128)(2,1)S(1)}, bf16[160,336]{1,0:T(8,128)(2,1)S(1)}, u32[]{:S(2)}, u32[]{:S(2)}) %collective-permute-start.32) | collective-permute-done | bytes 107552 | tf_op jit(solution)/shard_map/ppermute | solution.py:30
  95.0 0.7 copy-done.28
  95.6 3.9 %shard_map.117 = (bf16[56,2048]{1,0:T(8,128)(2,1)}, f32[56,2048]{1,0:T(8,128)}, f32[56,2048]{1,0:T(8,128)}, f32[56,2048]{1,0:T(8,128)}) custom-call(s32[1]{0:T(128)} %bitcast.core, bf16[160,336]{1,0:T(8,128)(2,1)} %copy-done.19, bf16[160,336]{1,0:T(8,128)(2,1)} %copy-done.28, bf16[160,2048]{1,0:T(8,128)(2,1)} %get-tuple-element.56.x_own.t_mine, ...), custom_call_target="tpu_custom_call" | custom-call | flops 440401920 | bytes 4227072 | tf_op jit(solution)/shard_map/pallas_call | solution.py:138
  99.8 4.0 %shard_map.115 = (bf16[56,2048]{1,0:T(8,128)(2,1)}, f32[56,2048]{1,0:T(8,128)}, f32[56,2048]{1,0:T(8,128)}, f32[56,2048]{1,0:T(8,128)}) custom-call(s32[1]{0:T(128)} %bitcast.core, bf16[160,672]{1,0:T(8,128)(2,1)} %copy-done.10, bf16[160,672]{1,0:T(8,128)(2,1)} %collective-permute-done.17.acts_other, bf16[160,2048]{1,0:T(8,128)(2,1)} %copy-done.3, ...), custom_call_target="tpu_custom_call" | custom-call | flops 440401920 | bytes 4227072 | tf_op jit(solution)/shard_map/pallas_call | solution.py:138
  103.9 1.4 collective-permute-start.24
  105.3 4.2 %shard_map.116 = (bf16[56,2048]{1,0:T(8,128)(2,1)}, f32[56,2048]{1,0:T(8,128)}, f32[56,2048]{1,0:T(8,128)}, f32[56,2048]{1,0:T(8,128)}) custom-call(s32[1]{0:T(128)} %bitcast.core, bf16[160,672]{1,0:T(8,128)(2,1)} %copy-done.10, bf16[160,672]{1,0:T(8,128)(2,1)} %collective-permute-done.17.acts_other, bf16[160,2048]{1,0:T(8,128)(2,1)} %copy-done.3, ...), custom_call_target="tpu_custom_call" | custom-call | flops 440401920 | bytes 4227072 | tf_op jit(solution)/shard_map/pallas_call | solution.py:138
  109.5 4.6 %back.1 = (f32[160,2048]{1,0:T(8,128)}, f32[160,2048]{1,0:T(8,128)}, f32[160,2048]{1,0:T(8,128)}, f32[160,2048]{1,0:T(8,128)}) custom-call(s32[1]{0:T(128)} %bitcast.core, bf16[160,672]{1,0:T(8,128)(2,1)} %copy-done.10, bf16[160,672]{1,0:T(8,128)(2,1)} %collective-permute-done.17.acts_other, bf16[56,2048]{1,0:T(8,128)(2,1)} %copy-done.15, ...), custom_call_target="tpu_custom_call" | custom-call | flops 880803840 | bytes 7077888 | tf_op jit(solution)/shard_map/back/pallas_call | solution.py:98
  114.7 1.2 add_convert_fusion.1
  115.9 29.5 %collective-permute-done.24 = bf16[56,2048]{1,0:T(8,128)(2,1)S(1)} collective-permute-done((bf16[56,2048]{1,0:T(8,128)(2,1)}, bf16[56,2048]{1,0:T(8,128)(2,1)S(1)}, u32[]{:S(2)}, u32[]{:S(2)}) %collective-permute-start.24) | collective-permute-done | bytes 229408 | tf_op jit(solution)/shard_map/ppermute | solution.py:30
  145.4 1.1 add_convert_fusion.3
  146.5 1.4 collective-permute-done.28
  147.9 1.9 collective-permute-start.25
  149.8 1.0 add_convert_fusion.2
  150.8 4.2 %collective-permute-done.34 = bf16[56,2048]{1,0:T(8,128)(2,1)S(1)} collective-permute-done((bf16[56,2048]{1,0:T(8,128)(2,1)S(1)}, bf16[56,2048]{1,0:T(8,128)(2,1)S(1)}, u32[]{:S(2)}, u32[]{:S(2)}) %collective-permute-start.34) | collective-permute-done | bytes 229408 | tf_op jit(solution)/shard_map/ppermute | solution.py:30
  155.1 3.1 %collective-permute-done.25 = bf16[56,2048]{1,0:T(8,128)(2,1)S(1)} collective-permute-done((bf16[56,2048]{1,0:T(8,128)(2,1)S(1)}, bf16[56,2048]{1,0:T(8,128)(2,1)S(1)}, u32[]{:S(2)}, u32[]{:S(2)}) %collective-permute-start.25) | collective-permute-done | bytes 229408 | tf_op jit(solution)/shard_map/ppermute | solution.py:30
  158.5 3.8 %collective-permute-done.29 = bf16[56,2048]{1,0:T(8,128)(2,1)S(1)} collective-permute-done((bf16[56,2048]{1,0:T(8,128)(2,1)S(1)}, bf16[56,2048]{1,0:T(8,128)(2,1)S(1)}, u32[]{:S(2)}, u32[]{:S(2)}) %collective-permute-start.29) | collective-permute-done | bytes 229408 | tf_op jit(solution)/shard_map/ppermute | solution.py:30
  162.7 15.2 %collective-permute-done.23 = bf16[3,56,2048]{2,1,0:T(8,128)(2,1)S(1)} collective-permute-done((bf16[3,56,2048]{2,1,0:T(8,128)(2,1)S(1)}, bf16[3,56,2048]{2,1,0:T(8,128)(2,1)S(1)}, u32[]{:S(2)}, u32[]{:S(2)}) %collective-permute-start.23) | collective-permute-done | bytes 688160 | tf_op jit(solution)/shard_map/ppermute | solution.py:30
  178.6 2.1 %collective-permute-start.36 = (bf16[56,2048]{1,0:T(8,128)(2,1)S(1)}, bf16[56,2048]{1,0:T(8,128)(2,1)S(1)}, u32[]{:S(2)}, u32[]{:S(2)}) collective-permute-start(bf16[56,2048]{1,0:T(8,128)(2,1)S(1)} %get-tuple-element.50), channel_id=1, source_target_pairs={{1,0},{0,1},{3,2},{2,3},{5,4},{4,5},{7,6},{6,7},{9,8},{8,9},{11,10... | collective-permute-start | bytes 688136 | tf_op jit(solution)/shard_map/ppermute | solution.py:30
  180.8 1.9 collective-permute-start.27
  182.7 12.7 %collective-permute-done.20 = bf16[160,2048]{1,0:T(8,128)(2,1)S(1)} collective-permute-done((bf16[160,2048]{1,0:T(8,128)(2,1)S(1)}, bf16[160,2048]{1,0:T(8,128)(2,1)S(1)}, u32[]{:S(2)}, u32[]{:S(2)}) %collective-permute-start.20) | collective-permute-done | bytes 655392 | tf_op jit(solution)/shard_map/ppermute | solution.py:30
  195.7 1.4 copy-done.2
  197.2 0.6 fusion.7
  197.8 0.7 copy-done.7
  198.5 2.3 %fusion.6 = bf16[160,4096]{1,0:T(8,128)(2,1)} fusion(bf16[160,4096]{1,0:T(8,128)(2,1)S(1)} %copy-done.1, bf16[160,4096]{1,0:T(8,128)(2,1)S(1)} %copy-done.7, f32[160]{0:T(256)S(1)} %broadcast_multiply_fusion, f32[160]{0:T(256)S(1)} %copy-done.31, f32[160]{0:T(256)S(1)} %copy-done.30, f32[160,4096]{1,0:T(8,128)S(1)} %copy-done.2, ...), kind=kLoop, calls=%fused_computation.10 | loop fusion | flops 7208960 | bytes 9193344 | tf_op jit(solution)/shard_map/convert_element_type | solution.py:227
  200.9 1.9 collective-permute-done.27
  202.8 0.8 pad_maximum_fusion.2
  203.6 0.8 pad_maximum_fusion.1
  204.4 0.8 pad_maximum_fusion
  (116 shorter events, 4.3 us)
Async XLA Ops:
  0.6 11.0 %copy-start.6 = (bf16[160,4096]{1,0:T(8,128)(2,1)S(1)}, bf16[160,4096]{1,0:T(8,128)(2,1)}, u32[]{:S(2)}) copy-start(bf16[160,4096]{1,0:T(8,128)(2,1)} %param.9) | copy-start | bytes 3932164
  1.7 24.8 %copy-start.8 = (bf16[56,2048]{1,0:T(8,128)(2,1)}, bf16[56,2048]{1,0:T(8,128)(2,1)S(1)}, u32[]{:S(2)}) copy-start(bf16[56,2048]{1,0:T(8,128)(2,1)S(1)} %constant_dynamic-slice_fusion.6.refs_6_) | copy-start | bytes 688132
  3.5 19.2 %copy-start.9 = (bf16[56,2048]{1,0:T(8,128)(2,1)}, bf16[56,2048]{1,0:T(8,128)(2,1)S(1)}, u32[]{:S(2)}) copy-start(bf16[56,2048]{1,0:T(8,128)(2,1)S(1)} %get-tuple-element.28.refs_7_) | copy-start | bytes 688132
  3.5 11.3 %copy-start.1 = (bf16[160,4096]{1,0:T(8,128)(2,1)S(1)}, bf16[160,4096]{1,0:T(8,128)(2,1)}, u32[]{:S(2)}) copy-start(bf16[160,4096]{1,0:T(8,128)(2,1)} %param.8) | copy-start | bytes 3932164
  3.6 39.7 %collective-permute-start.1 = (bf16[56,2048]{1,0:T(8,128)(2,1)}, bf16[56,2048]{1,0:T(8,128)(2,1)}, u32[]{:S(2)}, u32[]{:S(2)}) collective-permute-start(bf16[56,2048]{1,0:T(8,128)(2,1)} %get-tuple-element.26.refs_3_), channel_id=1, source_target_pairs={{8,0},{9,1},{10,2},{11,3},{12,4},{13,5},{14,6},{15,7},{16,8},{17,9... | collective-permute-start | bytes 688136 | tf_op jit(solution)/shard_map/ppermute | solution.py:30
  11.6 4.2 %copy-start.27 = (f32[4096]{0:T(1024)S(1)}, f32[4096]{0:T(1024)}, u32[]{:S(2)}) copy-start(f32[4096]{0:T(1024)} %param.12) | copy-start | bytes 49156
  12.7 33.4 %collective-permute-start.4 = (bf16[160,2048]{1,0:T(8,128)(2,1)}, bf16[160,2048]{1,0:T(8,128)(2,1)}, u32[]{:S(2)}, u32[]{:S(2)}) collective-permute-start(bf16[160,2048]{1,0:T(8,128)(2,1)} %get-tuple-element.55), channel_id=1, source_target_pairs={{1,0},{0,1},{3,2},{2,3},{5,4},{4,5},{7,6},{6,7},{9,8},{8,9},{11,10... | collective-permute-start | bytes 1966088 | tf_op jit(solution)/shard_map/ppermute | solution.py:30
  13.5 9.2 %collective-permute-start.10 = (bf16[56,2048]{1,0:T(8,128)(2,1)S(1)}, bf16[56,2048]{1,0:T(8,128)(2,1)}, u32[]{:S(2)}, u32[]{:S(2)}) collective-permute-start(bf16[56,2048]{1,0:T(8,128)(2,1)S(1)} %get-tuple-element.28.refs_7_), channel_id=1, source_target_pairs={{8,0},{9,1},{10,2},{11,3},{12,4},{13,5},{14,6},{15,7},{16,8},{17,9... | collective-permute-start | bytes 688136 | tf_op jit(solution)/shard_map/ppermute | solution.py:30
  14.3 12.2 %collective-permute-start.8 = (bf16[56,2048]{1,0:T(8,128)(2,1)S(1)}, bf16[56,2048]{1,0:T(8,128)(2,1)}, u32[]{:S(2)}, u32[]{:S(2)}) collective-permute-start(bf16[56,2048]{1,0:T(8,128)(2,1)S(1)} %constant_dynamic-slice_fusion.6.refs_6_), channel_id=1, source_target_pairs={{8,0},{9,1},{10,2},{11,3},{12,4},{13,5},{14,6},{15,7},{16,8},{17,9... | collective-permute-start | bytes 688136 | tf_op jit(solution)/shard_map/ppermute | solution.py:30
  15.8 1.4 copy-start.29
  17.1 40.2 %copy-start.3 = (bf16[160,2048]{1,0:T(8,128)(2,1)}, bf16[160,2048]{1,0:T(8,128)(2,1)S(1)}, u32[]{:S(2)}) copy-start(bf16[160,2048]{1,0:T(8,128)(2,1)S(1)} %get-tuple-element.54.x_own.t_mine) | copy-start | bytes 1966084
  17.1 26.1 %collective-permute-start.14 = (bf16[160,2048]{1,0:T(8,128)(2,1)}, bf16[160,2048]{1,0:T(8,128)(2,1)S(1)}, u32[]{:S(2)}, u32[]{:S(2)}) collective-permute-start(bf16[160,2048]{1,0:T(8,128)(2,1)} %get-tuple-element.53), channel_id=1, source_target_pairs={{1,0},{0,1},{3,2},{2,3},{5,4},{4,5},{7,6},{6,7},{9,8},{8,9},{11,10... | collective-permute-start | bytes 1966088 | tf_op jit(solution)/shard_map/ppermute | solution.py:30
  22.8 22.0 %collective-permute-start.11 = (bf16[56,2048]{1,0:T(8,128)(2,1)S(1)}, bf16[56,2048]{1,0:T(8,128)(2,1)S(1)}, u32[]{:S(2)}, u32[]{:S(2)}) collective-permute-start(bf16[56,2048]{1,0:T(8,128)(2,1)S(1)} %broadcast_select_fusion.6), channel_id=1, source_target_pairs={{5,0},{4,1},{7,2},{6,3},{1,4},{0,5},{3,6},{2,7},{13,8},{12,9},{15,... | collective-permute-start | bytes 688136 | tf_op jit(solution)/shard_map/ppermute | solution.py:30
  26.5 19.0 %collective-permute-start.9 = (bf16[56,2048]{1,0:T(8,128)(2,1)S(1)}, bf16[56,2048]{1,0:T(8,128)(2,1)S(1)}, u32[]{:S(2)}, u32[]{:S(2)}) collective-permute-start(bf16[56,2048]{1,0:T(8,128)(2,1)S(1)} %broadcast_select_fusion.7), channel_id=1, source_target_pairs={{5,0},{4,1},{7,2},{6,3},{1,4},{0,5},{3,6},{2,7},{13,8},{12,9},{15,... | collective-permute-start | bytes 688136 | tf_op jit(solution)/shard_map/ppermute | solution.py:30
  43.2 6.0 %copy-start.4 = (bf16[160,2048]{1,0:T(8,128)(2,1)}, bf16[160,2048]{1,0:T(8,128)(2,1)S(1)}, u32[]{:S(2)}) copy-start(bf16[160,2048]{1,0:T(8,128)(2,1)S(1)} %collective-permute-done.14.x_own.t_other) | copy-start | bytes 1966084
  43.2 14.1 %collective-permute-start.15 = (bf16[160,2048]{1,0:T(8,128)(2,1)S(1)}, bf16[160,2048]{1,0:T(8,128)(2,1)S(1)}, u32[]{:S(2)}, u32[]{:S(2)}) collective-permute-start(bf16[160,2048]{1,0:T(8,128)(2,1)S(1)} %collective-permute-done.14.x_own.t_other), channel_id=1, source_target_pairs={{2,0},{3,1},{0,2},{1,3},{6,4},{7,5},{4,6},{5,7},{10,8},{11,9},{8,1... | collective-permute-start | bytes 1966088 | tf_op jit(solution)/shard_map/ppermute | solution.py:30
  44.4 9.2 %collective-permute-start.2 = (bf16[56,2048]{1,0:T(8,128)(2,1)S(1)}, bf16[56,2048]{1,0:T(8,128)(2,1)}, u32[]{:S(2)}, u32[]{:S(2)}) collective-permute-start(bf16[56,2048]{1,0:T(8,128)(2,1)S(1)} %broadcast_select_fusion.8), channel_id=1, source_target_pairs={{5,0},{4,1},{7,2},{6,3},{1,4},{0,5},{3,6},{2,7},{13,8},{12,9},{15,... | collective-permute-start | bytes 688136 | tf_op jit(solution)/shard_map/ppermute | solution.py:30
  44.7 4.4 %copy-start.14 = (bf16[56,2048]{1,0:T(8,128)(2,1)}, bf16[56,2048]{1,0:T(8,128)(2,1)S(1)}, u32[]{:S(2)}) copy-start(bf16[56,2048]{1,0:T(8,128)(2,1)S(1)} %collective-permute-done.11.refs_1_) | copy-start | bytes 688132
  44.7 8.9 %collective-permute-start.13 = (bf16[56,2048]{1,0:T(8,128)(2,1)S(1)}, bf16[56,2048]{1,0:T(8,128)(2,1)S(1)}, u32[]{:S(2)}, u32[]{:S(2)}) collective-permute-start(bf16[56,2048]{1,0:T(8,128)(2,1)S(1)} %collective-permute-done.11.refs_1_), channel_id=1, source_target_pairs={{8,0},{9,1},{10,2},{11,3},{12,4},{13,5},{14,6},{15,7},{16,8},{17,9... | collective-permute-start | bytes 688136 | tf_op jit(solution)/shard_map/ppermute | solution.py:30
  45.6 3.6 %copy-start.15 = (bf16[56,2048]{1,0:T(8,128)(2,1)}, bf16[56,2048]{1,0:T(8,128)(2,1)S(1)}, u32[]{:S(2)}) copy-start(bf16[56,2048]{1,0:T(8,128)(2,1)S(1)} %collective-permute-done.9.refs_0_) | copy-start | bytes 688132
  45.6 11.7 %collective-permute-start.12 = (bf16[56,2048]{1,0:T(8,128)(2,1)S(1)}, bf16[56,2048]{1,0:T(8,128)(2,1)S(1)}, u32[]{:S(2)}, u32[]{:S(2)}) collective-permute-start(bf16[56,2048]{1,0:T(8,128)(2,1)S(1)} %collective-permute-done.9.refs_0_), channel_id=1, source_target_pairs={{8,0},{9,1},{10,2},{11,3},{12,4},{13,5},{14,6},{15,7},{16,8},{17,9... | collective-permute-start | bytes 688136 | tf_op jit(solution)/shard_map/ppermute | solution.py:30
  46.1 22.9 %collective-permute-start.5 = (bf16[160,2048]{1,0:T(8,128)(2,1)}, bf16[160,2048]{1,0:T(8,128)(2,1)}, u32[]{:S(2)}, u32[]{:S(2)}) collective-permute-start(bf16[160,2048]{1,0:T(8,128)(2,1)} %collective-permute-done.4.x_own.t_other), channel_id=1, source_target_pairs={{2,0},{3,1},{0,2},{1,3},{6,4},{7,5},{4,6},{5,7},{10,8},{11,9},{8,1... | collective-permute-start | bytes 1966088 | tf_op jit(solution)/shard_map/ppermute | solution.py:30
  53.6 46.0 %collective-permute-start.21 = (bf16[3,56,4096]{2,1,0:T(8,128)(2,1)}, bf16[3,56,4096]{2,1,0:T(8,128)(2,1)}, u32[]{:S(2)}, u32[]{:S(2)}) collective-permute-start(bf16[3,56,4096]{2,1,0:T(8,128)(2,1)} %convert_element_type.98), channel_id=1, source_target_pairs={{248,0},{249,1},{250,2},{251,3},{252,4},{253,5},{254,6},{255,7},{0... | collective-permute-start | bytes 4128776 | tf_op jit(solution)/shard_map/ppermute | solution.py:30
  53.6 3.7 %copy-start.16 = (bf16[56,2048]{1,0:T(8,128)(2,1)}, bf16[56,2048]{1,0:T(8,128)(2,1)S(1)}, u32[]{:S(2)}) copy-start(bf16[56,2048]{1,0:T(8,128)(2,1)S(1)} %collective-permute-done.13.refs_5_) | copy-start | bytes 688132
  53.6 19.5 %collective-permute-start = (bf16[160,2048]{1,0:T(8,128)(2,1)}, bf16[160,2048]{1,0:T(8,128)(2,1)}, u32[]{:S(2)}, u32[]{:S(2)}) collective-permute-start(bf16[160,2048]{1,0:T(8,128)(2,1)} %get-tuple-element.56.x_own.t_mine), channel_id=1, source_target_pairs={{2,0},{3,1},{0,2},{1,3},{6,4},{7,5},{4,6},{5,7},{10,8},{11,9},{8,1... | collective-permute-start | bytes 1966088 | tf_op jit(solution)/shard_map/ppermute | solution.py:30
  57.3 18.6 %collective-permute-start.7 = (bf16[160,2048]{1,0:T(8,128)(2,1)S(1)}, bf16[160,2048]{1,0:T(8,128)(2,1)}, u32[]{:S(2)}, u32[]{:S(2)}) collective-permute-start(bf16[160,2048]{1,0:T(8,128)(2,1)S(1)} %get-tuple-element.54.x_own.t_mine), channel_id=1, source_target_pairs={{2,0},{3,1},{0,2},{1,3},{6,4},{7,5},{4,6},{5,7},{10,8},{11,9},{8,1... | collective-permute-start | bytes 1966088 | tf_op jit(solution)/shard_map/ppermute | solution.py:30
  58.9 9.3 %collective-permute-start.3 = (bf16[56,2048]{1,0:T(8,128)(2,1)}, bf16[56,2048]{1,0:T(8,128)(2,1)S(1)}, u32[]{:S(2)}, u32[]{:S(2)}) collective-permute-start(bf16[56,2048]{1,0:T(8,128)(2,1)} %collective-permute-done.2.refs_0_), channel_id=1, source_target_pairs={{8,0},{9,1},{10,2},{11,3},{12,4},{13,5},{14,6},{15,7},{16,8},{17,9... | collective-permute-start | bytes 688136 | tf_op jit(solution)/shard_map/ppermute | solution.py:30
  68.2 14.3 %collective-permute-start.16 = (f32[160,672]{1,0:T(8,128)}, f32[160,672]{1,0:T(8,128)S(1)}, u32[]{:S(2)}, u32[]{:S(2)}) collective-permute-start(f32[160,672]{1,0:T(8,128)} %shard_map.114), channel_id=1, source_target_pairs={{1,0},{0,1},{3,2},{2,3},{5,4},{4,5},{7,6},{6,7},{9,8},{8,9},{11,10... | collective-permute-start | bytes 1290248 | tf_op jit(solution)/shard_map/ppermute | solution.py:30
  71.9 13.9 %collective-permute-start.6 = (f32[160,336]{1,0:T(8,128)}, f32[160,336]{1,0:T(8,128)S(1)}, u32[]{:S(2)}, u32[]{:S(2)}) collective-permute-start(f32[160,336]{1,0:T(8,128)} %shard_map.112), channel_id=1, source_target_pairs={{1,0},{0,1},{3,2},{2,3},{5,4},{4,5},{7,6},{6,7},{9,8},{8,9},{11,10... | collective-permute-start | bytes 645128 | tf_op jit(solution)/shard_map/ppermute | solution.py:30
  79.5 6.3 %copy-start.13 = (f32[160,336]{1,0:T(8,128)S(1)}, f32[160,336]{1,0:T(8,128)}, u32[]{:S(2)}) copy-start(f32[160,336]{1,0:T(8,128)} %shard_map.111) | copy-start | bytes 645124
  86.0 9.0 %copy-start.19 = (bf16[160,336]{1,0:T(8,128)(2,1)}, bf16[160,336]{1,0:T(8,128)(2,1)S(1)}, u32[]{:S(2)}) copy-start(bf16[160,336]{1,0:T(8,128)(2,1)S(1)} %get-tuple-element.59.acts_mine) | copy-start | bytes 322564
  86.1 13.4 %copy-start.10 = (bf16[160,672]{1,0:T(8,128)(2,1)}, bf16[160,672]{1,0:T(8,128)(2,1)S(1)}, u32[]{:S(2)}) copy-start(bf16[160,672]{1,0:T(8,128)(2,1)S(1)} %pad_maximum_fusion.3.acts_mine) | copy-start | bytes 645124
  86.1 13.7 %collective-permute-start.17 = (bf16[160,672]{1,0:T(8,128)(2,1)S(1)}, bf16[160,672]{1,0:T(8,128)(2,1)}, u32[]{:S(2)}, u32[]{:S(2)}) collective-permute-start(bf16[160,672]{1,0:T(8,128)(2,1)S(1)} %pad_maximum_fusion.3.acts_mine), channel_id=1, source_target_pairs={{1,0},{0,1},{3,2},{2,3},{5,4},{4,5},{7,6},{6,7},{9,8},{8,9},{11,10... | collective-permute-start | bytes 645128 | tf_op jit(solution)/shard_map/ppermute | solution.py:30
  87.0 7.9 %collective-permute-start.32 = (bf16[160,336]{1,0:T(8,128)(2,1)S(1)}, bf16[160,336]{1,0:T(8,128)(2,1)S(1)}, u32[]{:S(2)}, u32[]{:S(2)}) collective-permute-start(bf16[160,336]{1,0:T(8,128)(2,1)S(1)} %get-tuple-element.59.acts_mine), channel_id=1, source_target_pairs={{1,0},{0,1},{3,2},{2,3},{5,4},{4,5},{7,6},{6,7},{9,8},{8,9},{11,10... | collective-permute-start | bytes 322568 | tf_op jit(solution)/shard_map/ppermute | solution.py:30
  99.5 14.7 %collective-permute-start.33 = (bf16[56,2048]{1,0:T(8,128)(2,1)}, bf16[56,2048]{1,0:T(8,128)(2,1)}, u32[]{:S(2)}, u32[]{:S(2)}) collective-permute-start(bf16[56,2048]{1,0:T(8,128)(2,1)} %get-tuple-element.45), channel_id=1, source_target_pairs={{248,0},{249,1},{250,2},{251,3},{252,4},{253,5},{254,6},{255,7},{0... | collective-permute-start | bytes 688136 | tf_op jit(solution)/shard_map/ppermute | solution.py:30
  99.6 58.8 %collective-permute-start.22 = (bf16[3,56,4096]{2,1,0:T(8,128)(2,1)}, bf16[3,56,4096]{2,1,0:T(8,128)(2,1)S(1)}, u32[]{:S(2)}, u32[]{:S(2)}) collective-permute-start(bf16[3,56,4096]{2,1,0:T(8,128)(2,1)} %collective-permute-done.21), channel_id=1, source_target_pairs={{253,0},{252,1},{255,2},{254,3},{1,4},{0,5},{3,6},{2,7},{5,8},{4,9... | collective-permute-start | bytes 4128776 | tf_op jit(solution)/shard_map/ppermute | solution.py:30
  103.9 41.5 %collective-permute-start.24 = (bf16[56,2048]{1,0:T(8,128)(2,1)}, bf16[56,2048]{1,0:T(8,128)(2,1)S(1)}, u32[]{:S(2)}, u32[]{:S(2)}) collective-permute-start(bf16[56,2048]{1,0:T(8,128)(2,1)} %get-tuple-element.35), channel_id=1, source_target_pairs={{248,0},{249,1},{250,2},{251,3},{252,4},{253,5},{254,6},{255,7},{0... | collective-permute-start | bytes 688136 | tf_op jit(solution)/shard_map/ppermute | solution.py:30
  109.4 38.5 %collective-permute-start.28 = (bf16[56,2048]{1,0:T(8,128)(2,1)}, bf16[56,2048]{1,0:T(8,128)(2,1)}, u32[]{:S(2)}, u32[]{:S(2)}) collective-permute-start(bf16[56,2048]{1,0:T(8,128)(2,1)} %get-tuple-element.40), channel_id=1, source_target_pairs={{248,0},{249,1},{250,2},{251,3},{252,4},{253,5},{254,6},{255,7},{0... | collective-permute-start | bytes 688136 | tf_op jit(solution)/shard_map/ppermute | solution.py:30
  114.2 35.7 %copy-start.26 = (f32[56,2048]{1,0:T(8,128)S(1)}, f32[56,2048]{1,0:T(8,128)}, u32[]{:S(2)}) copy-start(f32[56,2048]{1,0:T(8,128)} %get-tuple-element.39) | copy-start | bytes 1376260
  114.2 48.2 %collective-permute-start.19 = (f32[160,2048]{1,0:T(8,128)}, f32[160,2048]{1,0:T(8,128)S(1)}, u32[]{:S(2)}, u32[]{:S(2)}) collective-permute-start(f32[160,2048]{1,0:T(8,128)} %get-tuple-element.32), channel_id=1, source_target_pairs={{2,0},{3,1},{0,2},{1,3},{6,4},{7,5},{4,6},{5,7},{10,8},{11,9},{8,1... | collective-permute-start | bytes 3932168 | tf_op jit(solution)/shard_map/ppermute | solution.py:30
  114.2 68.5 %collective-permute-start.18 = (f32[160,2048]{1,0:T(8,128)}, f32[160,2048]{1,0:T(8,128)S(1)}, u32[]{:S(2)}, u32[]{:S(2)}) collective-permute-start(f32[160,2048]{1,0:T(8,128)} %get-tuple-element.30), channel_id=1, source_target_pairs={{2,0},{3,1},{0,2},{1,3},{6,4},{7,5},{4,6},{5,7},{10,8},{11,9},{8,1... | collective-permute-start | bytes 3932168 | tf_op jit(solution)/shard_map/ppermute | solution.py:30
  114.7 40.4 %copy-start.23 = (f32[56,2048]{1,0:T(8,128)S(1)}, f32[56,2048]{1,0:T(8,128)}, u32[]{:S(2)}) copy-start(f32[56,2048]{1,0:T(8,128)} %get-tuple-element.43) | copy-start | bytes 1376260
  145.4 9.7 %collective-permute-start.34 = (bf16[56,2048]{1,0:T(8,128)(2,1)S(1)}, bf16[56,2048]{1,0:T(8,128)(2,1)S(1)}, u32[]{:S(2)}, u32[]{:S(2)}) collective-permute-start(bf16[56,2048]{1,0:T(8,128)(2,1)S(1)} %add_convert_fusion.1), channel_id=1, source_target_pairs={{5,0},{4,1},{7,2},{6,3},{1,4},{0,5},{3,6},{2,7},{13,8},{12,9},{15,... | collective-permute-start | bytes 688136 | tf_op jit(solution)/shard_map/ppermute | solution.py:30
  145.4 12.9 %copy-start.25 = (f32[56,2048]{1,0:T(8,128)S(1)}, f32[56,2048]{1,0:T(8,128)}, u32[]{:S(2)}) copy-start(f32[56,2048]{1,0:T(8,128)} %get-tuple-element.33) | copy-start | bytes 1376260
  147.9 10.3 %collective-permute-start.25 = (bf16[56,2048]{1,0:T(8,128)(2,1)S(1)}, bf16[56,2048]{1,0:T(8,128)(2,1)S(1)}, u32[]{:S(2)}, u32[]{:S(2)}) collective-permute-start(bf16[56,2048]{1,0:T(8,128)(2,1)S(1)} %add_convert_fusion.3), channel_id=1, source_target_pairs={{5,0},{4,1},{7,2},{6,3},{1,4},{0,5},{3,6},{2,7},{13,8},{12,9},{15,... | collective-permute-start | bytes 688136 | tf_op jit(solution)/shard_map/ppermute | solution.py:30
  155.1 7.2 %collective-permute-start.29 = (bf16[56,2048]{1,0:T(8,128)(2,1)S(1)}, bf16[56,2048]{1,0:T(8,128)(2,1)S(1)}, u32[]{:S(2)}, u32[]{:S(2)}) collective-permute-start(bf16[56,2048]{1,0:T(8,128)(2,1)S(1)} %add_convert_fusion.2), channel_id=1, source_target_pairs={{5,0},{4,1},{7,2},{6,3},{1,4},{0,5},{3,6},{2,7},{13,8},{12,9},{15,... | collective-permute-start | bytes 688136 | tf_op jit(solution)/shard_map/ppermute | solution.py:30
  155.1 7.2 %copy-start.24 = (f32[56,2048]{1,0:T(8,128)S(1)}, f32[56,2048]{1,0:T(8,128)}, u32[]{:S(2)}) copy-start(f32[56,2048]{1,0:T(8,128)} %get-tuple-element.38) | copy-start | bytes 1376260
  158.3 19.8 %collective-permute-start.35 = (bf16[56,2048]{1,0:T(8,128)(2,1)S(1)}, bf16[56,2048]{1,0:T(8,128)(2,1)S(1)}, u32[]{:S(2)}, u32[]{:S(2)}) collective-permute-start(bf16[56,2048]{1,0:T(8,128)(2,1)S(1)} %fusion.20), channel_id=1, source_target_pairs={{248,0},{249,1},{250,2},{251,3},{252,4},{253,5},{254,6},{255,7},{0... | collective-permute-start | bytes 688136 | tf_op jit(solution)/shard_map/ppermute | solution.py:30
  158.3 4.1 %copy-start.11 = (f32[160,2048]{1,0:T(8,128)S(1)}, f32[160,2048]{1,0:T(8,128)}, u32[]{:S(2)}) copy-start(f32[160,2048]{1,0:T(8,128)} %get-tuple-element.31) | copy-start | bytes 3932164
  158.4 19.7 %collective-permute-start.26 = (bf16[56,2048]{1,0:T(8,128)(2,1)S(1)}, bf16[56,2048]{1,0:T(8,128)(2,1)S(1)}, u32[]{:S(2)}, u32[]{:S(2)}) collective-permute-start(bf16[56,2048]{1,0:T(8,128)(2,1)S(1)} %fusion.10), channel_id=1, source_target_pairs={{248,0},{249,1},{250,2},{251,3},{252,4},{253,5},{254,6},{255,7},{0... | collective-permute-start | bytes 688136 | tf_op jit(solution)/shard_map/ppermute | solution.py:30
  162.3 15.6 %collective-permute-start.23 = (bf16[3,56,2048]{2,1,0:T(8,128)(2,1)S(1)}, bf16[3,56,2048]{2,1,0:T(8,128)(2,1)S(1)}, u32[]{:S(2)}, u32[]{:S(2)}) collective-permute-start(bf16[3,56,2048]{2,1,0:T(8,128)(2,1)S(1)} %constant_dynamic-slice_fusion), channel_id=1, source_target_pairs={{1,0},{0,1},{3,2},{2,3},{5,4},{4,5},{7,6},{6,7},{9,8},{8,9},{11,10... | collective-permute-start | bytes 2064392 | tf_op jit(solution)/shard_map/ppermute | solution.py:30
  162.4 15.7 %collective-permute-start.30 = (bf16[56,2048]{1,0:T(8,128)(2,1)S(1)}, bf16[56,2048]{1,0:T(8,128)(2,1)S(1)}, u32[]{:S(2)}, u32[]{:S(2)}) collective-permute-start(bf16[56,2048]{1,0:T(8,128)(2,1)S(1)} %fusion.15), channel_id=1, source_target_pairs={{248,0},{249,1},{250,2},{251,3},{252,4},{253,5},{254,6},{255,7},{0... | collective-permute-start | bytes 688136 | tf_op jit(solution)/shard_map/ppermute | solution.py:30
  162.7 15.4 %copy-start.20 = (f32[56,2048]{1,0:T(8,128)S(1)}, f32[56,2048]{1,0:T(8,128)}, u32[]{:S(2)}) copy-start(f32[56,2048]{1,0:T(8,128)} %get-tuple-element.46) | copy-start | bytes 1376260
  162.7 15.4 %copy-start.21 = (f32[56,2048]{1,0:T(8,128)S(1)}, f32[56,2048]{1,0:T(8,128)}, u32[]{:S(2)}) copy-start(f32[56,2048]{1,0:T(8,128)} %get-tuple-element.36) | copy-start | bytes 1376260
  162.7 15.4 %copy-start.22 = (f32[56,2048]{1,0:T(8,128)S(1)}, f32[56,2048]{1,0:T(8,128)}, u32[]{:S(2)}) copy-start(f32[56,2048]{1,0:T(8,128)} %get-tuple-element.41) | copy-start | bytes 1376260
  177.9 17.5 %collective-permute-start.20 = (bf16[160,2048]{1,0:T(8,128)(2,1)S(1)}, bf16[160,2048]{1,0:T(8,128)(2,1)S(1)}, u32[]{:S(2)}, u32[]{:S(2)}) collective-permute-start(bf16[160,2048]{1,0:T(8,128)(2,1)S(1)} %add_convert_fusion), channel_id=1, source_target_pairs={{1,0},{0,1},{3,2},{2,3},{5,4},{4,5},{7,6},{6,7},{9,8},{8,9},{11,10... | collective-permute-start | bytes 1966088 | tf_op jit(solution)/shard_map/ppermute | solution.py:30
  178.1 17.3 %copy-start.12 = (f32[160,2048]{1,0:T(8,128)S(1)}, f32[160,2048]{1,0:T(8,128)}, u32[]{:S(2)}) copy-start(f32[160,2048]{1,0:T(8,128)} %get-tuple-element.29) | copy-start | bytes 3932164
  178.6 22.2 %collective-permute-start.36 = (bf16[56,2048]{1,0:T(8,128)(2,1)S(1)}, bf16[56,2048]{1,0:T(8,128)(2,1)S(1)}, u32[]{:S(2)}, u32[]{:S(2)}) collective-permute-start(bf16[56,2048]{1,0:T(8,128)(2,1)S(1)} %get-tuple-element.50), channel_id=1, source_target_pairs={{1,0},{0,1},{3,2},{2,3},{5,4},{4,5},{7,6},{6,7},{9,8},{8,9},{11,10... | collective-permute-start | bytes 688136 | tf_op jit(solution)/shard_map/ppermute | solution.py:30
  180.7 20.1 %collective-permute-start.31 = (bf16[56,2048]{1,0:T(8,128)(2,1)S(1)}, bf16[56,2048]{1,0:T(8,128)(2,1)S(1)}, u32[]{:S(2)}, u32[]{:S(2)}) collective-permute-start(bf16[56,2048]{1,0:T(8,128)(2,1)S(1)} %get-tuple-element.51), channel_id=1, source_target_pairs={{1,0},{0,1},{3,2},{2,3},{5,4},{4,5},{7,6},{6,7},{9,8},{8,9},{11,10... | collective-permute-start | bytes 688136 | tf_op jit(solution)/shard_map/ppermute | solution.py:30
  180.8 22.0 %collective-permute-start.27 = (bf16[56,2048]{1,0:T(8,128)(2,1)S(1)}, bf16[56,2048]{1,0:T(8,128)(2,1)S(1)}, u32[]{:S(2)}, u32[]{:S(2)}) collective-permute-start(bf16[56,2048]{1,0:T(8,128)(2,1)S(1)} %get-tuple-element.52), channel_id=1, source_target_pairs={{1,0},{0,1},{3,2},{2,3},{5,4},{4,5},{7,6},{6,7},{9,8},{8,9},{11,10... | collective-permute-start | bytes 688136 | tf_op jit(solution)/shard_map/ppermute | solution.py:30
  195.4 1.7 copy-start.2
  197.2 1.3 copy-start.7
  197.2 1.3 copy-start.30
  197.2 1.3 copy-start.31
  (5 other events, 4.1 us)

commit v3 on v2

--- a/solution.py
+++ b/solution.py
@@ -89,7 +89,11 @@
             lhs = jnp.concatenate(
                 [value[:, span * s : span * (s + 1)], value[:, span * (2 + s) : span * (3 + s)]], axis=1
             )
-            outs[2 * s + o][...] = dot(lhs, met, ((1,), (0,)))
+            got = dot(lhs, met, ((1,), (0,)))
+            if s == 0:
+                outs[o][...] = got
+            else:
+                outs[2][o * lhs.shape[0] : (o + 1) * lhs.shape[0], :] = got.astype(BF)
 
 
 def back_sums(core, acts_mine, acts_other, sets):
@@ -97,9 +101,9 @@
     units, half = sets[0][0].shape
     return pl.pallas_call(
         back_kernel,
-        out_shape=[jax.ShapeDtypeStruct((rows, half), F32)] * 4,
+        out_shape=[jax.ShapeDtypeStruct((rows, half), F32)] * 2 + [jax.ShapeDtypeStruct((2 * rows, half), BF)],
         in_specs=[pl.BlockSpec(memory_space=pltpu.SMEM)] + in_vmem(10),
-        out_specs=in_vmem(4),
+        out_specs=in_vmem(3),
         name="back",
         cost_estimate=pl.CostEstimate(
             flops=48 * rows * units * half, bytes_accessed=16 * rows * half + 16 * units * half, transcendentals=0
@@ -213,19 +217,22 @@
         swapped = hop((first_sum + along.astype(F32)).astype(BF), cross_swap).astype(F32)
         second_sum = second_sum + jnp.where(q == 0, swapped, 0.0)
         home = hop(second_sum.astype(BF), lambda c, q, k, r: (c - 1, q, k, r)).astype(F32)
+        if finals:
+            home = lax.optimization_barrier((home, finals[-1][0]))[0]
         total = held[i] + home + home_sum + jnp.where(q == 1, swapped, 0.0)
         final = (total * scale).astype(BF)
         finals.append((final, hop(final, rep_swap)))
 
-    own_other, own_mine, par_other, par_mine = back_sums(core, acts, acts_other, sets)
-    back_other = own_other + hop(par_other, core_swap)
-    back_got = hop(back_other.astype(BF), rep_swap).astype(F32)
-    back_mine = own_mine + hop(par_mine, core_swap)
+    own_other, own_mine, partner = back_sums(core, acts, acts_other, sets)
+    partner = hop(partner, core_swap)
+    back_got = hop((own_other + partner[:rows].astype(F32)).astype(BF), rep_swap).astype(F32)
+    back_mine = own_mine + partner[rows:].astype(F32)
     dnormed = dnormed_in + joined(back_mine, back_got)
     scaled = norm_gain * dnormed
     dx = rstd * scaled - values * rstd**3 * jnp.mean(values * scaled, axis=-1, keepdims=True)
     input_grad = (out_cotangent.astype(F32) + dx).astype(BF)
-    finals = [joined(final, lax.optimization_barrier((got, input_grad))[0]) for final, got in finals]
+    for n, (final, got) in enumerate(finals):
+        finals[n] = joined(final, lax.optimization_barrier((got, input_grad))[0])
     return (input_grad, finals[1], finals[2], finals[0])
 
 

time: 206 us -> 198 us (0.961)
  waiting for transfers between devices: 115 us -> 99.7 us
  starting transfers between devices: 32.7 us -> 39.8 us
    ppermute x37 -> x36, waiting for transfers between devices: 115 us -> 99.7 us  [hop(): return lax.ppermute(value, AXES, pairs)]
    ppermute x37 -> x36, starting transfers between devices: 32.7 us -> 39.8 us  [hop(): return lax.ppermute(value, AXES, pairs)]
  transfers between devices with their start and end apart: 37 -> 36, of which waited for: 17 -> 17; matrix products, arithmetic and copies ran while one was open for 8% -> 9% of each run, Pallas kernels for 14% -> 15%
where the time goes in v3:
time: 198 us; the launch traced here: 197 us
  waiting for transfers between devices  99.7 us (50%)
  starting transfers between devices  39.8 us (20%)
  Pallas kernels  29.3 us (15%)
  other arithmetic  17 us (9%)
  local copies, waits for them, and re-layouts  10.3 us (5%)
    ppermute x36, waiting for transfers between devices, hop(): return lax.ppermute(value, AXES, pairs)  99.7 us
    ppermute x36, starting transfers between devices, hop(): return lax.ppermute(value, AXES, pairs)  39.8 us
    pallas_call x4, Pallas kernels, scores(): pl.pallas_call(functools.partial(scores_kernel, len(picked)), out_shape=j...  12.9 us
    pallas_call x3, Pallas kernels, gradient(): pl.pallas_call(functools.partial(gradient_kernel, i), out_shape=[jax.Shap...  12.1 us
    unnamed x64, local copies, waits for them, and re-layouts  6.17 us
    pallas_call x1, Pallas kernels, back_sums(): pl.pallas_call(back_kernel, out_shape=[jax.ShapeDtypeStruct((rows, half),...  4.36 us
  transfers between devices with their start and end apart: 36, of which 17 were waited for; matrix products, arithmetic and copies ran while one was open for 9% of the time, Pallas kernels for 15%

profile of v3, /device:TPU:24, one launch (start us, length us, event | category | flops | bytes accessed | tf_op | source)
XLA Modules:
  0.0 197.3 jit_solution(13365149837693473846)
XLA Ops:
  0.7 1.0 copy-done
  1.7 1.9 constant_dynamic-slice_fusion.4
  3.5 8.1 %collective-permute-start.1 = (bf16[56,2048]{1,0:T(8,128)(2,1)}, bf16[56,2048]{1,0:T(8,128)(2,1)}, u32[]{:S(2)}, u32[]{:S(2)}) collective-permute-start(bf16[56,2048]{1,0:T(8,128)(2,1)} %get-tuple-element.27.refs_3_), channel_id=1, source_target_pairs={{8,0},{9,1},{10,2},{11,3},{12,4},{13,5},{14,6},{15,7},{16,8},{17,9... | collective-permute-start | bytes 688136 | tf_op jit(solution)/shard_map/ppermute | solution.py:30
  11.6 0.8 collective-permute-start.8
  14.8 1.0 constant_dynamic-slice_fusion.1
  15.8 0.7 collective-permute-start.14
  16.5 1.2 constant_dynamic-slice_fusion.3
  17.7 1.3 collective-permute-start.4
  19.0 3.7 %collective-permute-done.8.refs_2_ = bf16[56,2048]{1,0:T(8,128)(2,1)} collective-permute-done((bf16[56,2048]{1,0:T(8,128)(2,1)S(1)}, bf16[56,2048]{1,0:T(8,128)(2,1)}, u32[]{:S(2)}, u32[]{:S(2)}) %collective-permute-start.8) | collective-permute-done | bytes 229408 | tf_op jit(solution)/shard_map/ppermute | solution.py:30
  22.8 1.2 collective-permute-start.9
  24.0 2.5 %collective-permute-done.10.refs_3_ = bf16[56,2048]{1,0:T(8,128)(2,1)} collective-permute-done((bf16[56,2048]{1,0:T(8,128)(2,1)S(1)}, bf16[56,2048]{1,0:T(8,128)(2,1)}, u32[]{:S(2)}, u32[]{:S(2)}) %collective-permute-start.10) | collective-permute-done | bytes 229408 | tf_op jit(solution)/shard_map/ppermute | solution.py:30
  26.5 1.2 collective-permute-start.11
  27.8 5.8 %collective-permute-done.14.x_own.t_other = bf16[160,2048]{1,0:T(8,128)(2,1)S(1)} collective-permute-done((bf16[160,2048]{1,0:T(8,128)(2,1)}, bf16[160,2048]{1,0:T(8,128)(2,1)S(1)}, u32[]{:S(2)}, u32[]{:S(2)}) %collective-permute-start.14) | collective-permute-done | bytes 655392 | tf_op jit(solution)/shard_map/ppermute | solution.py:30
  33.6 1.2 broadcast_select_fusion.8
  35.1 2.0 %collective-permute-start.12 = (bf16[56,2048]{1,0:T(8,128)(2,1)S(1)}, bf16[56,2048]{1,0:T(8,128)(2,1)S(1)}, u32[]{:S(2)}, u32[]{:S(2)}) collective-permute-start(bf16[56,2048]{1,0:T(8,128)(2,1)S(1)} %collective-permute-done.9.refs_0_), channel_id=1, source_target_pairs={{8,0},{9,1},{10,2},{11,3},{12,4},{13,5},{14,6},{15,7},{16,8},{17,9... | collective-permute-start | bytes 688136 | tf_op jit(solution)/shard_map/ppermute | solution.py:30
  37.1 5.1 %collective-permute-start.13 = (bf16[56,2048]{1,0:T(8,128)(2,1)S(1)}, bf16[56,2048]{1,0:T(8,128)(2,1)S(1)}, u32[]{:S(2)}, u32[]{:S(2)}) collective-permute-start(bf16[56,2048]{1,0:T(8,128)(2,1)S(1)} %collective-permute-done.11.refs_1_), channel_id=1, source_target_pairs={{8,0},{9,1},{10,2},{11,3},{12,4},{13,5},{14,6},{15,7},{16,8},{17,9... | collective-permute-start | bytes 688136 | tf_op jit(solution)/shard_map/ppermute | solution.py:30
  42.2 3.5 %collective-permute-done.4.x_own.t_other = bf16[160,2048]{1,0:T(8,128)(2,1)} collective-permute-done((bf16[160,2048]{1,0:T(8,128)(2,1)}, bf16[160,2048]{1,0:T(8,128)(2,1)}, u32[]{:S(2)}, u32[]{:S(2)}) %collective-permute-start.4) | collective-permute-done | bytes 655392 | tf_op jit(solution)/shard_map/ppermute | solution.py:30
  45.8 3.0 %convert_element_type.106 = bf16[3,56,4096]{2,1,0:T(8,128)(2,1)} convert(f32[3,56,4096]{2,1,0:T(8,128)} %param.11) | non-fusion elementwise | flops 688128 | bytes 4128768 | tf_op jit(solution)/shard_map/convert_element_type | solution.py:175
  48.8 1.6 collective-permute-start.20
  51.3 0.9 copy-done.5
  52.2 3.9 %collective-permute-start.3 = (bf16[56,2048]{1,0:T(8,128)(2,1)}, bf16[56,2048]{1,0:T(8,128)(2,1)S(1)}, u32[]{:S(2)}, u32[]{:S(2)}) collective-permute-start(bf16[56,2048]{1,0:T(8,128)(2,1)} %collective-permute-done.2.refs_0_), channel_id=1, source_target_pairs={{8,0},{9,1},{10,2},{11,3},{12,4},{13,5},{14,6},{15,7},{16,8},{17,9... | collective-permute-start | bytes 688136 | tf_op jit(solution)/shard_map/ppermute | solution.py:30
  56.0 3.6 %shard_map.114 = f32[160,672]{1,0:T(8,128)} custom-call(s32[1]{0:T(128)} %bitcast.core, bf16[160,2048]{1,0:T(8,128)(2,1)} %copy-done.4, bf16[160,2048]{1,0:T(8,128)(2,1)} %copy-done.5, bf16[56,2048]{1,0:T(8,128)(2,1)} %copy-done.14, bf16[56,2048]{1,0:T(8,128)(2,1)} %copy-done.15, bf16[56,2048]{1,0:T(8,128)(2,1)} %collective-permute-done.8.refs_2_, ...), custom_call_target="tpu_custom_call" | custom-call | flops 440401920 | bytes 4063232 | tf_op jit(solution)/shard_map/pallas_call | solution.py:69
  59.6 2.0 %collective-permute-done.3.refs_2_ = bf16[56,2048]{1,0:T(8,128)(2,1)S(1)} collective-permute-done((bf16[56,2048]{1,0:T(8,128)(2,1)}, bf16[56,2048]{1,0:T(8,128)(2,1)S(1)}, u32[]{:S(2)}, u32[]{:S(2)}) %collective-permute-start.3) | collective-permute-done | bytes 229408 | tf_op jit(solution)/shard_map/ppermute | solution.py:30
  61.7 0.7 collective-permute-start.16
  62.4 2.8 %shard_map.112 = f32[160,336]{1,0:T(8,128)} custom-call(s32[1]{0:T(128)} %bitcast.core, bf16[160,2048]{1,0:T(8,128)(2,1)} %collective-permute-done.4.x_own.t_other, bf16[160,2048]{1,0:T(8,128)(2,1)} %collective-permute-done.5.x_par.t_other_p, bf16[56,2048]{1,0:T(8,128)(2,1)} %collective-permute-done.2.refs_0_, ...), custom_call_target="tpu_custom_call" | custom-call | flops 220200960 | bytes 2686976 | tf_op jit(solution)/shard_map/pallas_call | solution.py:69
  65.2 1.3 collective-permute-start.6
  66.5 2.8 %shard_map.111 = f32[160,336]{1,0:T(8,128)} custom-call(s32[1]{0:T(128)} %bitcast.core, bf16[160,2048]{1,0:T(8,128)(2,1)} %get-tuple-element.55.x_own.t_mine, bf16[160,2048]{1,0:T(8,128)(2,1)} %collective-permute-done.x_par.t_mine_p, bf16[56,2048]{1,0:T(8,128)(2,1)} %collective-permute-done.2.refs_0_, bf16[56,2048]{1,0:T(8,128)(2,1)} %collective-permute-done.1.refs_1_, ...), custom_call_target="tpu_custom_call" | custom-call | flops 220200960 | bytes 2686976 | tf_op jit(solution)/shard_map/pallas_call | solution.py:69
  69.4 3.6 %shard_map.113 = f32[160,672]{1,0:T(8,128)} custom-call(s32[1]{0:T(128)} %bitcast.core, bf16[160,2048]{1,0:T(8,128)(2,1)} %copy-done.3, bf16[160,2048]{1,0:T(8,128)(2,1)} %collective-permute-done.7.x_par.t_mine_p, bf16[56,2048]{1,0:T(8,128)(2,1)} %copy-done.14, bf16[56,2048]{1,0:T(8,128)(2,1)} %copy-done.15, ...), custom_call_target="tpu_custom_call" | custom-call | flops 440401920 | bytes 4063232 | tf_op jit(solution)/shard_map/pallas_call | solution.py:69
  73.0 3.0 %collective-permute-done.16 = f32[160,672]{1,0:T(8,128)S(1)} collective-permute-done((f32[160,672]{1,0:T(8,128)}, f32[160,672]{1,0:T(8,128)S(1)}, u32[]{:S(2)}, u32[]{:S(2)}) %collective-permute-start.16) | collective-permute-done | bytes 430112 | tf_op jit(solution)/shard_map/ppermute | solution.py:30
  76.0 1.1 add.114
  77.1 2.6 %collective-permute-done.6 = f32[160,336]{1,0:T(8,128)S(1)} collective-permute-done((f32[160,336]{1,0:T(8,128)}, f32[160,336]{1,0:T(8,128)S(1)}, u32[]{:S(2)}, u32[]{:S(2)}) %collective-permute-start.6) | collective-permute-done | bytes 215072 | tf_op jit(solution)/shard_map/ppermute | solution.py:30
  80.0 0.8 collective-permute-start.17
  80.9 1.3 collective-permute-start.26
  82.2 7.1 %collective-permute-done.26.acts_other = bf16[160,336]{1,0:T(8,128)(2,1)S(1)} collective-permute-done((bf16[160,336]{1,0:T(8,128)(2,1)S(1)}, bf16[160,336]{1,0:T(8,128)(2,1)S(1)}, u32[]{:S(2)}, u32[]{:S(2)}) %collective-permute-start.26) | collective-permute-done | bytes 107552 | tf_op jit(solution)/shard_map/ppermute | solution.py:30
  89.3 0.6 copy-done.28
  89.9 3.9 %shard_map.116 = (bf16[56,2048]{1,0:T(8,128)(2,1)}, f32[56,2048]{1,0:T(8,128)}, f32[56,2048]{1,0:T(8,128)}, f32[56,2048]{1,0:T(8,128)}) custom-call(s32[1]{0:T(128)} %bitcast.core, bf16[160,336]{1,0:T(8,128)(2,1)} %copy-done.19, bf16[160,336]{1,0:T(8,128)(2,1)} %copy-done.28, bf16[160,2048]{1,0:T(8,128)(2,1)} %get-tuple-element.55.x_own.t_mine, ...), custom_call_target="tpu_custom_call" | custom-call | flops 440401920 | bytes 4227072 | tf_op jit(solution)/shard_map/pallas_call | solution.py:142
  94.1 4.2 %shard_map.117 = (bf16[56,2048]{1,0:T(8,128)(2,1)}, f32[56,2048]{1,0:T(8,128)}, f32[56,2048]{1,0:T(8,128)}, f32[56,2048]{1,0:T(8,128)}) custom-call(s32[1]{0:T(128)} %bitcast.core, bf16[160,672]{1,0:T(8,128)(2,1)} %copy-done.10, bf16[160,672]{1,0:T(8,128)(2,1)} %collective-permute-done.17.acts_other, bf16[160,2048]{1,0:T(8,128)(2,1)} %copy-done.3, ...), custom_call_target="tpu_custom_call" | custom-call | flops 440401920 | bytes 4227072 | tf_op jit(solution)/shard_map/pallas_call | solution.py:142
  98.3 0.8 collective-permute-start.31
  99.0 4.0 %shard_map.115 = (bf16[56,2048]{1,0:T(8,128)(2,1)}, f32[56,2048]{1,0:T(8,128)}, f32[56,2048]{1,0:T(8,128)}, f32[56,2048]{1,0:T(8,128)}) custom-call(s32[1]{0:T(128)} %bitcast.core, bf16[160,672]{1,0:T(8,128)(2,1)} %copy-done.10, bf16[160,672]{1,0:T(8,128)(2,1)} %collective-permute-done.17.acts_other, bf16[160,2048]{1,0:T(8,128)(2,1)} %copy-done.3, ...), custom_call_target="tpu_custom_call" | custom-call | flops 440401920 | bytes 4227072 | tf_op jit(solution)/shard_map/pallas_call | solution.py:142
  103.1 4.4 %back.1 = (f32[160,2048]{1,0:T(8,128)}, f32[160,2048]{1,0:T(8,128)}, bf16[320,2048]{1,0:T(8,128)(2,1)}) custom-call(s32[1]{0:T(128)} %bitcast.core, bf16[160,672]{1,0:T(8,128)(2,1)} %copy-done.10, bf16[160,672]{1,0:T(8,128)(2,1)} %collective-permute-done.17.acts_other, bf16[56,2048]{1,0:T(8,128)(2,1)} %copy-done.14, bf16[56,2048]{1,0:T(8,128)(2,1)} %copy-done.15, ...), custom_call_target="tpu_custom_call" | custom-call | flops 880803840 | bytes 7077888 | tf_op jit(solution)/shard_map/back/pallas_call | solution.py:102
  107.5 1.2 add_convert_fusion.2
  108.7 2.5 %collective-permute-start.28 = (bf16[56,2048]{1,0:T(8,128)(2,1)S(1)}, bf16[56,2048]{1,0:T(8,128)(2,1)S(1)}, u32[]{:S(2)}, u32[]{:S(2)}) collective-permute-start(bf16[56,2048]{1,0:T(8,128)(2,1)S(1)} %add_convert_fusion.2), channel_id=1, source_target_pairs={{5,0},{4,1},{7,2},{6,3},{1,4},{0,5},{3,6},{2,7},{13,8},{12,9},{15,... | collective-permute-start | bytes 688136 | tf_op jit(solution)/shard_map/ppermute | solution.py:30
  111.2 29.1 %collective-permute-done.31 = bf16[56,2048]{1,0:T(8,128)(2,1)S(1)} collective-permute-done((bf16[56,2048]{1,0:T(8,128)(2,1)}, bf16[56,2048]{1,0:T(8,128)(2,1)S(1)}, u32[]{:S(2)}, u32[]{:S(2)}) %collective-permute-start.31) | collective-permute-done | bytes 229408 | tf_op jit(solution)/shard_map/ppermute | solution.py:30
  140.3 1.1 add_convert_fusion.1
  141.5 1.3 collective-permute-done.23
  142.8 1.0 add_convert_fusion.3
  143.8 2.0 collective-permute-start.24
  145.8 3.9 %collective-permute-done.32 = bf16[56,2048]{1,0:T(8,128)(2,1)S(1)} collective-permute-done((bf16[56,2048]{1,0:T(8,128)(2,1)S(1)}, bf16[56,2048]{1,0:T(8,128)(2,1)S(1)}, u32[]{:S(2)}, u32[]{:S(2)}) %collective-permute-start.32) | collective-permute-done | bytes 229408 | tf_op jit(solution)/shard_map/ppermute | solution.py:30
  149.9 2.3 %collective-permute-done.24 = bf16[56,2048]{1,0:T(8,128)(2,1)S(1)} collective-permute-done((bf16[56,2048]{1,0:T(8,128)(2,1)S(1)}, bf16[56,2048]{1,0:T(8,128)(2,1)S(1)}, u32[]{:S(2)}, u32[]{:S(2)}) %collective-permute-start.24) | collective-permute-done | bytes 229408 | tf_op jit(solution)/shard_map/ppermute | solution.py:30
  152.7 9.0 %collective-permute-done.33 = bf16[56,2048]{1,0:T(8,128)(2,1)S(1)} collective-permute-done((bf16[56,2048]{1,0:T(8,128)(2,1)S(1)}, bf16[56,2048]{1,0:T(8,128)(2,1)S(1)}, u32[]{:S(2)}, u32[]{:S(2)}) %collective-permute-start.33) | collective-permute-done | bytes 229408 | tf_op jit(solution)/shard_map/ppermute | solution.py:30
  161.7 2.6 %collective-permute-done.25 = bf16[56,2048]{1,0:T(8,128)(2,1)S(1)} collective-permute-done((bf16[56,2048]{1,0:T(8,128)(2,1)S(1)}, bf16[56,2048]{1,0:T(8,128)(2,1)S(1)}, u32[]{:S(2)}, u32[]{:S(2)}) %collective-permute-start.25) | collective-permute-done | bytes 229408 | tf_op jit(solution)/shard_map/ppermute | solution.py:30
  164.6 6.2 %collective-permute-done.22 = bf16[3,56,2048]{2,1,0:T(8,128)(2,1)S(1)} collective-permute-done((bf16[3,56,2048]{2,1,0:T(8,128)(2,1)S(1)}, bf16[3,56,2048]{2,1,0:T(8,128)(2,1)S(1)}, u32[]{:S(2)}, u32[]{:S(2)}) %collective-permute-start.22) | collective-permute-done | bytes 688160 | tf_op jit(solution)/shard_map/ppermute | solution.py:30
  171.3 0.7 copy-done.26
  172.1 1.4 collective-permute-start.30
  173.6 0.8 collective-permute-start.34
  174.5 10.4 %collective-permute-done.19 = bf16[160,2048]{1,0:T(8,128)(2,1)S(1)} collective-permute-done((bf16[160,2048]{1,0:T(8,128)(2,1)S(1)}, bf16[160,2048]{1,0:T(8,128)(2,1)S(1)}, u32[]{:S(2)}, u32[]{:S(2)}) %collective-permute-start.19) | collective-permute-done | bytes 655392 | tf_op jit(solution)/shard_map/ppermute | solution.py:30
  185.2 1.4 copy-done.2
  186.6 0.6 fusion.7
  187.2 0.7 copy-done.7
  187.9 2.3 %fusion.6 = bf16[160,4096]{1,0:T(8,128)(2,1)} fusion(bf16[160,4096]{1,0:T(8,128)(2,1)S(1)} %copy-done.1, bf16[160,4096]{1,0:T(8,128)(2,1)S(1)} %copy-done.7, f32[160]{0:T(256)S(1)} %broadcast_multiply_fusion, f32[160]{0:T(256)S(1)} %copy-done.31, f32[160]{0:T(256)S(1)} %copy-done.30, f32[160,4096]{1,0:T(8,128)S(1)} %copy-done.2, ...), kind=kLoop, calls=%fused_computation.10 | loop fusion | flops 7208960 | bytes 9193344 | tf_op jit(solution)/shard_map/convert_element_type | solution.py:233
  190.2 4.6 %collective-permute-done.34 = bf16[56,2048]{1,0:T(8,128)(2,1)S(1)} collective-permute-done((bf16[56,2048]{1,0:T(8,128)(2,1)S(1)}, bf16[56,2048]{1,0:T(8,128)(2,1)S(1)}, u32[]{:S(2)}, u32[]{:S(2)}) %collective-permute-start.34) | collective-permute-done | bytes 229408 | tf_op jit(solution)/shard_map/ppermute | solution.py:30
  194.9 0.8 pad_maximum_fusion.2
  195.7 0.8 pad_maximum_fusion.1
  196.5 0.8 pad_maximum_fusion
  (118 shorter events, 6.5 us)
Async XLA Ops:
  0.6 1.0 copy-start
  0.6 12.3 %copy-start.1 = (bf16[160,4096]{1,0:T(8,128)(2,1)S(1)}, bf16[160,4096]{1,0:T(8,128)(2,1)}, u32[]{:S(2)}) copy-start(bf16[160,4096]{1,0:T(8,128)(2,1)} %param.8) | copy-start | bytes 3932164
  0.7 13.7 %copy-start.27 = (f32[4096]{0:T(1024)S(1)}, f32[4096]{0:T(1024)}, u32[]{:S(2)}) copy-start(f32[4096]{0:T(1024)} %param.12) | copy-start | bytes 49156
  1.7 21.0 %copy-start.8 = (bf16[56,2048]{1,0:T(8,128)(2,1)}, bf16[56,2048]{1,0:T(8,128)(2,1)S(1)}, u32[]{:S(2)}) copy-start(bf16[56,2048]{1,0:T(8,128)(2,1)S(1)} %constant_dynamic-slice_fusion.6.refs_6_) | copy-start | bytes 688132
  3.5 23.0 %copy-start.9 = (bf16[56,2048]{1,0:T(8,128)(2,1)}, bf16[56,2048]{1,0:T(8,128)(2,1)S(1)}, u32[]{:S(2)}) copy-start(bf16[56,2048]{1,0:T(8,128)(2,1)S(1)} %get-tuple-element.29.refs_7_) | copy-start | bytes 688132
  3.5 30.0 %collective-permute-start.1 = (bf16[56,2048]{1,0:T(8,128)(2,1)}, bf16[56,2048]{1,0:T(8,128)(2,1)}, u32[]{:S(2)}, u32[]{:S(2)}) collective-permute-start(bf16[56,2048]{1,0:T(8,128)(2,1)} %get-tuple-element.27.refs_3_), channel_id=1, source_target_pairs={{8,0},{9,1},{10,2},{11,3},{12,4},{13,5},{14,6},{15,7},{16,8},{17,9... | collective-permute-start | bytes 688136 | tf_op jit(solution)/shard_map/ppermute | solution.py:30
  11.6 11.1 %collective-permute-start.8 = (bf16[56,2048]{1,0:T(8,128)(2,1)S(1)}, bf16[56,2048]{1,0:T(8,128)(2,1)}, u32[]{:S(2)}, u32[]{:S(2)}) collective-permute-start(bf16[56,2048]{1,0:T(8,128)(2,1)S(1)} %constant_dynamic-slice_fusion.6.refs_6_), channel_id=1, source_target_pairs={{8,0},{9,1},{10,2},{11,3},{12,4},{13,5},{14,6},{15,7},{16,8},{17,9... | collective-permute-start | bytes 688136 | tf_op jit(solution)/shard_map/ppermute | solution.py:30
  12.4 14.1 %collective-permute-start.10 = (bf16[56,2048]{1,0:T(8,128)(2,1)S(1)}, bf16[56,2048]{1,0:T(8,128)(2,1)}, u32[]{:S(2)}, u32[]{:S(2)}) collective-permute-start(bf16[56,2048]{1,0:T(8,128)(2,1)S(1)} %get-tuple-element.29.refs_7_), channel_id=1, source_target_pairs={{8,0},{9,1},{10,2},{11,3},{12,4},{13,5},{14,6},{15,7},{16,8},{17,9... | collective-permute-start | bytes 688136 | tf_op jit(solution)/shard_map/ppermute | solution.py:30
  14.8 1.7 copy-start.6
  15.8 34.9 %copy-start.3 = (bf16[160,2048]{1,0:T(8,128)(2,1)}, bf16[160,2048]{1,0:T(8,128)(2,1)S(1)}, u32[]{:S(2)}) copy-start(bf16[160,2048]{1,0:T(8,128)(2,1)S(1)} %get-tuple-element.53.x_own.t_mine) | copy-start | bytes 1966084
  15.8 17.8 %collective-permute-start.14 = (bf16[160,2048]{1,0:T(8,128)(2,1)}, bf16[160,2048]{1,0:T(8,128)(2,1)S(1)}, u32[]{:S(2)}, u32[]{:S(2)}) collective-permute-start(bf16[160,2048]{1,0:T(8,128)(2,1)} %get-tuple-element.52), channel_id=1, source_target_pairs={{1,0},{0,1},{3,2},{2,3},{5,4},{4,5},{7,6},{6,7},{9,8},{8,9},{11,10... | collective-permute-start | bytes 1966088 | tf_op jit(solution)/shard_map/ppermute | solution.py:30
  17.7 28.0 %collective-permute-start.4 = (bf16[160,2048]{1,0:T(8,128)(2,1)}, bf16[160,2048]{1,0:T(8,128)(2,1)}, u32[]{:S(2)}, u32[]{:S(2)}) collective-permute-start(bf16[160,2048]{1,0:T(8,128)(2,1)} %get-tuple-element.54), channel_id=1, source_target_pairs={{1,0},{0,1},{3,2},{2,3},{5,4},{4,5},{7,6},{6,7},{9,8},{8,9},{11,10... | collective-permute-start | bytes 1966088 | tf_op jit(solution)/shard_map/ppermute | solution.py:30
  22.8 12.4 %collective-permute-start.9 = (bf16[56,2048]{1,0:T(8,128)(2,1)S(1)}, bf16[56,2048]{1,0:T(8,128)(2,1)S(1)}, u32[]{:S(2)}, u32[]{:S(2)}) collective-permute-start(bf16[56,2048]{1,0:T(8,128)(2,1)S(1)} %broadcast_select_fusion.7), channel_id=1, source_target_pairs={{5,0},{4,1},{7,2},{6,3},{1,4},{0,5},{3,6},{2,7},{13,8},{12,9},{15,... | collective-permute-start | bytes 688136 | tf_op jit(solution)/shard_map/ppermute | solution.py:30
  26.5 10.6 %collective-permute-start.11 = (bf16[56,2048]{1,0:T(8,128)(2,1)S(1)}, bf16[56,2048]{1,0:T(8,128)(2,1)S(1)}, u32[]{:S(2)}, u32[]{:S(2)}) collective-permute-start(bf16[56,2048]{1,0:T(8,128)(2,1)S(1)} %broadcast_select_fusion.6), channel_id=1, source_target_pairs={{5,0},{4,1},{7,2},{6,3},{1,4},{0,5},{3,6},{2,7},{13,8},{12,9},{15,... | collective-permute-start | bytes 688136 | tf_op jit(solution)/shard_map/ppermute | solution.py:30
  33.6 15.2 %copy-start.4 = (bf16[160,2048]{1,0:T(8,128)(2,1)}, bf16[160,2048]{1,0:T(8,128)(2,1)S(1)}, u32[]{:S(2)}) copy-start(bf16[160,2048]{1,0:T(8,128)(2,1)S(1)} %collective-permute-done.14.x_own.t_other) | copy-start | bytes 1966084
  33.6 17.4 %collective-permute-start.15 = (bf16[160,2048]{1,0:T(8,128)(2,1)S(1)}, bf16[160,2048]{1,0:T(8,128)(2,1)S(1)}, u32[]{:S(2)}, u32[]{:S(2)}) collective-permute-start(bf16[160,2048]{1,0:T(8,128)(2,1)S(1)} %collective-permute-done.14.x_own.t_other), channel_id=1, source_target_pairs={{2,0},{3,1},{0,2},{1,3},{6,4},{7,5},{4,6},{5,7},{10,8},{11,9},{8,1... | collective-permute-start | bytes 1966088 | tf_op jit(solution)/shard_map/ppermute | solution.py:30
  34.8 14.0 %collective-permute-start.2 = (bf16[56,2048]{1,0:T(8,128)(2,1)S(1)}, bf16[56,2048]{1,0:T(8,128)(2,1)}, u32[]{:S(2)}, u32[]{:S(2)}) collective-permute-start(bf16[56,2048]{1,0:T(8,128)(2,1)S(1)} %broadcast_select_fusion.8), channel_id=1, source_target_pairs={{5,0},{4,1},{7,2},{6,3},{1,4},{0,5},{3,6},{2,7},{13,8},{12,9},{15,... | collective-permute-start | bytes 688136 | tf_op jit(solution)/shard_map/ppermute | solution.py:30
  35.1 13.7 %copy-start.14 = (bf16[56,2048]{1,0:T(8,128)(2,1)}, bf16[56,2048]{1,0:T(8,128)(2,1)S(1)}, u32[]{:S(2)}) copy-start(bf16[56,2048]{1,0:T(8,128)(2,1)S(1)} %collective-permute-done.9.refs_0_) | copy-start | bytes 688132
  35.1 15.3 %collective-permute-start.12 = (bf16[56,2048]{1,0:T(8,128)(2,1)S(1)}, bf16[56,2048]{1,0:T(8,128)(2,1)S(1)}, u32[]{:S(2)}, u32[]{:S(2)}) collective-permute-start(bf16[56,2048]{1,0:T(8,128)(2,1)S(1)} %collective-permute-done.9.refs_0_), channel_id=1, source_target_pairs={{8,0},{9,1},{10,2},{11,3},{12,4},{13,5},{14,6},{15,7},{16,8},{17,9... | collective-permute-start | bytes 688136 | tf_op jit(solution)/shard_map/ppermute | solution.py:30
  37.1 11.7 %copy-start.15 = (bf16[56,2048]{1,0:T(8,128)(2,1)}, bf16[56,2048]{1,0:T(8,128)(2,1)S(1)}, u32[]{:S(2)}) copy-start(bf16[56,2048]{1,0:T(8,128)(2,1)S(1)} %collective-permute-done.11.refs_1_) | copy-start | bytes 688132
  37.1 13.5 %collective-permute-start.13 = (bf16[56,2048]{1,0:T(8,128)(2,1)S(1)}, bf16[56,2048]{1,0:T(8,128)(2,1)S(1)}, u32[]{:S(2)}, u32[]{:S(2)}) collective-permute-start(bf16[56,2048]{1,0:T(8,128)(2,1)S(1)} %collective-permute-done.11.refs_1_), channel_id=1, source_target_pairs={{8,0},{9,1},{10,2},{11,3},{12,4},{13,5},{14,6},{15,7},{16,8},{17,9... | collective-permute-start | bytes 688136 | tf_op jit(solution)/shard_map/ppermute | solution.py:30
  45.8 16.7 %collective-permute-start.5 = (bf16[160,2048]{1,0:T(8,128)(2,1)}, bf16[160,2048]{1,0:T(8,128)(2,1)}, u32[]{:S(2)}, u32[]{:S(2)}) collective-permute-start(bf16[160,2048]{1,0:T(8,128)(2,1)} %collective-permute-done.4.x_own.t_other), channel_id=1, source_target_pairs={{2,0},{3,1},{0,2},{1,3},{6,4},{7,5},{4,6},{5,7},{10,8},{11,9},{8,1... | collective-permute-start | bytes 1966088 | tf_op jit(solution)/shard_map/ppermute | solution.py:30
  48.8 45.2 %collective-permute-start.20 = (bf16[3,56,4096]{2,1,0:T(8,128)(2,1)}, bf16[3,56,4096]{2,1,0:T(8,128)(2,1)}, u32[]{:S(2)}, u32[]{:S(2)}) collective-permute-start(bf16[3,56,4096]{2,1,0:T(8,128)(2,1)} %convert_element_type.106), channel_id=1, source_target_pairs={{248,0},{249,1},{250,2},{251,3},{252,4},{253,5},{254,6},{255,7},{0... | collective-permute-start | bytes 4128776 | tf_op jit(solution)/shard_map/ppermute | solution.py:30
  50.4 16.1 %collective-permute-start = (bf16[160,2048]{1,0:T(8,128)(2,1)}, bf16[160,2048]{1,0:T(8,128)(2,1)}, u32[]{:S(2)}, u32[]{:S(2)}) collective-permute-start(bf16[160,2048]{1,0:T(8,128)(2,1)} %get-tuple-element.55.x_own.t_mine), channel_id=1, source_target_pairs={{2,0},{3,1},{0,2},{1,3},{6,4},{7,5},{4,6},{5,7},{10,8},{11,9},{8,1... | collective-permute-start | bytes 1966088 | tf_op jit(solution)/shard_map/ppermute | solution.py:30
  50.6 18.8 %collective-permute-start.7 = (bf16[160,2048]{1,0:T(8,128)(2,1)S(1)}, bf16[160,2048]{1,0:T(8,128)(2,1)}, u32[]{:S(2)}, u32[]{:S(2)}) collective-permute-start(bf16[160,2048]{1,0:T(8,128)(2,1)S(1)} %get-tuple-element.53.x_own.t_mine), channel_id=1, source_target_pairs={{2,0},{3,1},{0,2},{1,3},{6,4},{7,5},{4,6},{5,7},{10,8},{11,9},{8,1... | collective-permute-start | bytes 1966088 | tf_op jit(solution)/shard_map/ppermute | solution.py:30
  51.3 0.9 copy-start.5
  52.2 9.5 %collective-permute-start.3 = (bf16[56,2048]{1,0:T(8,128)(2,1)}, bf16[56,2048]{1,0:T(8,128)(2,1)S(1)}, u32[]{:S(2)}, u32[]{:S(2)}) collective-permute-start(bf16[56,2048]{1,0:T(8,128)(2,1)} %collective-permute-done.2.refs_0_), channel_id=1, source_target_pairs={{8,0},{9,1},{10,2},{11,3},{12,4},{13,5},{14,6},{15,7},{16,8},{17,9... | collective-permute-start | bytes 688136 | tf_op jit(solution)/shard_map/ppermute | solution.py:30
  61.7 0.8 copy-start.18
  61.7 14.3 %collective-permute-start.16 = (f32[160,672]{1,0:T(8,128)}, f32[160,672]{1,0:T(8,128)S(1)}, u32[]{:S(2)}, u32[]{:S(2)}) collective-permute-start(f32[160,672]{1,0:T(8,128)} %shard_map.114), channel_id=1, source_target_pairs={{1,0},{0,1},{3,2},{2,3},{5,4},{4,5},{7,6},{6,7},{9,8},{8,9},{11,10... | collective-permute-start | bytes 1290248 | tf_op jit(solution)/shard_map/ppermute | solution.py:30
  65.2 14.4 %collective-permute-start.6 = (f32[160,336]{1,0:T(8,128)}, f32[160,336]{1,0:T(8,128)S(1)}, u32[]{:S(2)}, u32[]{:S(2)}) collective-permute-start(f32[160,336]{1,0:T(8,128)} %shard_map.112), channel_id=1, source_target_pairs={{1,0},{0,1},{3,2},{2,3},{5,4},{4,5},{7,6},{6,7},{9,8},{8,9},{11,10... | collective-permute-start | bytes 645128 | tf_op jit(solution)/shard_map/ppermute | solution.py:30
  73.0 6.7 %copy-start.13 = (f32[160,336]{1,0:T(8,128)S(1)}, f32[160,336]{1,0:T(8,128)}, u32[]{:S(2)}) copy-start(f32[160,336]{1,0:T(8,128)} %shard_map.111) | copy-start | bytes 645124
  79.9 9.4 %copy-start.19 = (bf16[160,336]{1,0:T(8,128)(2,1)}, bf16[160,336]{1,0:T(8,128)(2,1)S(1)}, u32[]{:S(2)}) copy-start(bf16[160,336]{1,0:T(8,128)(2,1)S(1)} %get-tuple-element.58.acts_mine) | copy-start | bytes 322564
  80.0 13.8 %copy-start.10 = (bf16[160,672]{1,0:T(8,128)(2,1)}, bf16[160,672]{1,0:T(8,128)(2,1)S(1)}, u32[]{:S(2)}) copy-start(bf16[160,672]{1,0:T(8,128)(2,1)S(1)} %pad_maximum_fusion.3.acts_mine) | copy-start | bytes 645124
  80.0 14.0 %collective-permute-start.17 = (bf16[160,672]{1,0:T(8,128)(2,1)S(1)}, bf16[160,672]{1,0:T(8,128)(2,1)}, u32[]{:S(2)}, u32[]{:S(2)}) collective-permute-start(bf16[160,672]{1,0:T(8,128)(2,1)S(1)} %pad_maximum_fusion.3.acts_mine), channel_id=1, source_target_pairs={{1,0},{0,1},{3,2},{2,3},{5,4},{4,5},{7,6},{6,7},{9,8},{8,9},{11,10... | collective-permute-start | bytes 645128 | tf_op jit(solution)/shard_map/ppermute | solution.py:30
  80.9 8.4 %collective-permute-start.26 = (bf16[160,336]{1,0:T(8,128)(2,1)S(1)}, bf16[160,336]{1,0:T(8,128)(2,1)S(1)}, u32[]{:S(2)}, u32[]{:S(2)}) collective-permute-start(bf16[160,336]{1,0:T(8,128)(2,1)S(1)} %get-tuple-element.58.acts_mine), channel_id=1, source_target_pairs={{1,0},{0,1},{3,2},{2,3},{5,4},{4,5},{7,6},{6,7},{9,8},{8,9},{11,10... | collective-permute-start | bytes 322568 | tf_op jit(solution)/shard_map/ppermute | solution.py:30
  93.9 13.6 %collective-permute-start.27 = (bf16[56,2048]{1,0:T(8,128)(2,1)}, bf16[56,2048]{1,0:T(8,128)(2,1)}, u32[]{:S(2)}, u32[]{:S(2)}) collective-permute-start(bf16[56,2048]{1,0:T(8,128)(2,1)} %get-tuple-element.38), channel_id=1, source_target_pairs={{248,0},{249,1},{250,2},{251,3},{252,4},{253,5},{254,6},{255,7},{0... | collective-permute-start | bytes 688136 | tf_op jit(solution)/shard_map/ppermute | solution.py:30
  94.0 58.3 %collective-permute-start.21 = (bf16[3,56,4096]{2,1,0:T(8,128)(2,1)}, bf16[3,56,4096]{2,1,0:T(8,128)(2,1)S(1)}, u32[]{:S(2)}, u32[]{:S(2)}) collective-permute-start(bf16[3,56,4096]{2,1,0:T(8,128)(2,1)} %collective-permute-done.20), channel_id=1, source_target_pairs={{253,0},{252,1},{255,2},{254,3},{1,4},{0,5},{3,6},{2,7},{5,8},{4,9... | collective-permute-start | bytes 4128776 | tf_op jit(solution)/shard_map/ppermute | solution.py:30
  98.3 42.0 %collective-permute-start.31 = (bf16[56,2048]{1,0:T(8,128)(2,1)}, bf16[56,2048]{1,0:T(8,128)(2,1)S(1)}, u32[]{:S(2)}, u32[]{:S(2)}) collective-permute-start(bf16[56,2048]{1,0:T(8,128)(2,1)} %get-tuple-element.45), channel_id=1, source_target_pairs={{248,0},{249,1},{250,2},{251,3},{252,4},{253,5},{254,6},{255,7},{0... | collective-permute-start | bytes 688136 | tf_op jit(solution)/shard_map/ppermute | solution.py:30
  103.0 39.8 %collective-permute-start.23 = (bf16[56,2048]{1,0:T(8,128)(2,1)}, bf16[56,2048]{1,0:T(8,128)(2,1)}, u32[]{:S(2)}, u32[]{:S(2)}) collective-permute-start(bf16[56,2048]{1,0:T(8,128)(2,1)} %get-tuple-element.35), channel_id=1, source_target_pairs={{248,0},{249,1},{250,2},{251,3},{252,4},{253,5},{254,6},{255,7},{0... | collective-permute-start | bytes 688136 | tf_op jit(solution)/shard_map/ppermute | solution.py:30
  107.5 35.3 %copy-start.23 = (f32[56,2048]{1,0:T(8,128)S(1)}, f32[56,2048]{1,0:T(8,128)}, u32[]{:S(2)}) copy-start(f32[56,2048]{1,0:T(8,128)} %get-tuple-element.34) | copy-start | bytes 1376260
  107.5 56.8 %collective-permute-start.18 = (bf16[320,2048]{1,0:T(8,128)(2,1)}, bf16[320,2048]{1,0:T(8,128)(2,1)S(1)}, u32[]{:S(2)}, u32[]{:S(2)}) collective-permute-start(bf16[320,2048]{1,0:T(8,128)(2,1)} %get-tuple-element.31), channel_id=1, source_target_pairs={{2,0},{3,1},{0,2},{1,3},{6,4},{7,5},{4,6},{5,7},{10,8},{11,9},{8,1... | collective-permute-start | bytes 3932168 | tf_op jit(solution)/shard_map/ppermute | solution.py:30
  107.5 42.2 %copy-start.22 = (f32[56,2048]{1,0:T(8,128)S(1)}, f32[56,2048]{1,0:T(8,128)}, u32[]{:S(2)}) copy-start(f32[56,2048]{1,0:T(8,128)} %get-tuple-element.43) | copy-start | bytes 1376260
  108.7 43.8 %collective-permute-start.28 = (bf16[56,2048]{1,0:T(8,128)(2,1)S(1)}, bf16[56,2048]{1,0:T(8,128)(2,1)S(1)}, u32[]{:S(2)}, u32[]{:S(2)}) collective-permute-start(bf16[56,2048]{1,0:T(8,128)(2,1)S(1)} %add_convert_fusion.2), channel_id=1, source_target_pairs={{5,0},{4,1},{7,2},{6,3},{1,4},{0,5},{3,6},{2,7},{13,8},{12,9},{15,... | collective-permute-start | bytes 688136 | tf_op jit(solution)/shard_map/ppermute | solution.py:30
  140.3 11.9 %copy-start.21 = (f32[56,2048]{1,0:T(8,128)S(1)}, f32[56,2048]{1,0:T(8,128)}, u32[]{:S(2)}) copy-start(f32[56,2048]{1,0:T(8,128)} %get-tuple-element.33) | copy-start | bytes 1376260
  141.4 8.3 %collective-permute-start.32 = (bf16[56,2048]{1,0:T(8,128)(2,1)S(1)}, bf16[56,2048]{1,0:T(8,128)(2,1)S(1)}, u32[]{:S(2)}, u32[]{:S(2)}) collective-permute-start(bf16[56,2048]{1,0:T(8,128)(2,1)S(1)} %add_convert_fusion.1), channel_id=1, source_target_pairs={{5,0},{4,1},{7,2},{6,3},{1,4},{0,5},{3,6},{2,7},{13,8},{12,9},{15,... | collective-permute-start | bytes 688136 | tf_op jit(solution)/shard_map/ppermute | solution.py:30
  143.8 8.4 %collective-permute-start.24 = (bf16[56,2048]{1,0:T(8,128)(2,1)S(1)}, bf16[56,2048]{1,0:T(8,128)(2,1)S(1)}, u32[]{:S(2)}, u32[]{:S(2)}) collective-permute-start(bf16[56,2048]{1,0:T(8,128)(2,1)S(1)} %add_convert_fusion.3), channel_id=1, source_target_pairs={{5,0},{4,1},{7,2},{6,3},{1,4},{0,5},{3,6},{2,7},{13,8},{12,9},{15,... | collective-permute-start | bytes 688136 | tf_op jit(solution)/shard_map/ppermute | solution.py:30
  149.8 2.7 %copy-start.20 = (f32[56,2048]{1,0:T(8,128)S(1)}, f32[56,2048]{1,0:T(8,128)}, u32[]{:S(2)}) copy-start(f32[56,2048]{1,0:T(8,128)} %get-tuple-element.36) | copy-start | bytes 1376260
  149.8 11.9 %collective-permute-start.33 = (bf16[56,2048]{1,0:T(8,128)(2,1)S(1)}, bf16[56,2048]{1,0:T(8,128)(2,1)S(1)}, u32[]{:S(2)}, u32[]{:S(2)}) collective-permute-start(bf16[56,2048]{1,0:T(8,128)(2,1)S(1)} %fusion.20), channel_id=1, source_target_pairs={{248,0},{249,1},{250,2},{251,3},{252,4},{253,5},{254,6},{255,7},{0... | collective-permute-start | bytes 688136 | tf_op jit(solution)/shard_map/ppermute | solution.py:30
  152.2 12.0 %collective-permute-start.25 = (bf16[56,2048]{1,0:T(8,128)(2,1)S(1)}, bf16[56,2048]{1,0:T(8,128)(2,1)S(1)}, u32[]{:S(2)}, u32[]{:S(2)}) collective-permute-start(bf16[56,2048]{1,0:T(8,128)(2,1)S(1)} %fusion.10), channel_id=1, source_target_pairs={{248,0},{249,1},{250,2},{251,3},{252,4},{253,5},{254,6},{255,7},{0... | collective-permute-start | bytes 688136 | tf_op jit(solution)/shard_map/ppermute | solution.py:30
  152.4 11.9 %copy-start.11 = (f32[160,2048]{1,0:T(8,128)S(1)}, f32[160,2048]{1,0:T(8,128)}, u32[]{:S(2)}) copy-start(f32[160,2048]{1,0:T(8,128)} %get-tuple-element.32) | copy-start | bytes 3932164
  152.4 18.4 %collective-permute-start.22 = (bf16[3,56,2048]{2,1,0:T(8,128)(2,1)S(1)}, bf16[3,56,2048]{2,1,0:T(8,128)(2,1)S(1)}, u32[]{:S(2)}, u32[]{:S(2)}) collective-permute-start(bf16[3,56,2048]{2,1,0:T(8,128)(2,1)S(1)} %constant_dynamic-slice_fusion), channel_id=1, source_target_pairs={{1,0},{0,1},{3,2},{2,3},{5,4},{4,5},{7,6},{6,7},{9,8},{8,9},{11,10... | collective-permute-start | bytes 2064392 | tf_op jit(solution)/shard_map/ppermute | solution.py:30
  152.6 18.4 %collective-permute-start.29 = (bf16[56,2048]{1,0:T(8,128)(2,1)S(1)}, bf16[56,2048]{1,0:T(8,128)(2,1)S(1)}, u32[]{:S(2)}, u32[]{:S(2)}) collective-permute-start(bf16[56,2048]{1,0:T(8,128)(2,1)S(1)} %fusion.15), channel_id=1, source_target_pairs={{248,0},{249,1},{250,2},{251,3},{252,4},{253,5},{254,6},{255,7},{0... | collective-permute-start | bytes 688136 | tf_op jit(solution)/shard_map/ppermute | solution.py:30
  164.5 6.5 %copy-start.24 = (f32[56,2048]{1,0:T(8,128)S(1)}, f32[56,2048]{1,0:T(8,128)}, u32[]{:S(2)}) copy-start(f32[56,2048]{1,0:T(8,128)} %get-tuple-element.39) | copy-start | bytes 1376260
  164.5 20.4 %collective-permute-start.19 = (bf16[160,2048]{1,0:T(8,128)(2,1)S(1)}, bf16[160,2048]{1,0:T(8,128)(2,1)S(1)}, u32[]{:S(2)}, u32[]{:S(2)}) collective-permute-start(bf16[160,2048]{1,0:T(8,128)(2,1)S(1)} %add_convert_fusion), channel_id=1, source_target_pairs={{1,0},{0,1},{3,2},{2,3},{5,4},{4,5},{7,6},{6,7},{9,8},{8,9},{11,10... | collective-permute-start | bytes 1966088 | tf_op jit(solution)/shard_map/ppermute | solution.py:30
  171.0 1.0 copy-start.26
  171.0 2.5 %copy-start.25 = (f32[56,2048]{1,0:T(8,128)S(1)}, f32[56,2048]{1,0:T(8,128)}, u32[]{:S(2)}) copy-start(f32[56,2048]{1,0:T(8,128)} %get-tuple-element.47) | copy-start | bytes 1376260
  171.2 19.0 %collective-permute-start.35 = (bf16[56,2048]{1,0:T(8,128)(2,1)S(1)}, bf16[56,2048]{1,0:T(8,128)(2,1)S(1)}, u32[]{:S(2)}, u32[]{:S(2)}) collective-permute-start(bf16[56,2048]{1,0:T(8,128)(2,1)S(1)} %fusion.18), channel_id=1, source_target_pairs={{1,0},{0,1},{3,2},{2,3},{5,4},{4,5},{7,6},{6,7},{9,8},{8,9},{11,10... | collective-permute-start | bytes 688136 | tf_op jit(solution)/shard_map/ppermute | solution.py:30
  172.1 12.7 %copy-start.12 = (f32[160,2048]{1,0:T(8,128)S(1)}, f32[160,2048]{1,0:T(8,128)}, u32[]{:S(2)}) copy-start(f32[160,2048]{1,0:T(8,128)} %get-tuple-element.30) | copy-start | bytes 3932164
  172.1 22.7 %collective-permute-start.30 = (bf16[56,2048]{1,0:T(8,128)(2,1)S(1)}, bf16[56,2048]{1,0:T(8,128)(2,1)S(1)}, u32[]{:S(2)}, u32[]{:S(2)}) collective-permute-start(bf16[56,2048]{1,0:T(8,128)(2,1)S(1)} %fusion.13), channel_id=1, source_target_pairs={{1,0},{0,1},{3,2},{2,3},{5,4},{4,5},{7,6},{6,7},{9,8},{8,9},{11,10... | collective-permute-start | bytes 688136 | tf_op jit(solution)/shard_map/ppermute | solution.py:30
  173.6 21.2 %collective-permute-start.34 = (bf16[56,2048]{1,0:T(8,128)(2,1)S(1)}, bf16[56,2048]{1,0:T(8,128)(2,1)S(1)}, u32[]{:S(2)}, u32[]{:S(2)}) collective-permute-start(bf16[56,2048]{1,0:T(8,128)(2,1)S(1)} %fusion.23), channel_id=1, source_target_pairs={{1,0},{0,1},{3,2},{2,3},{5,4},{4,5},{7,6},{6,7},{9,8},{8,9},{11,10... | collective-permute-start | bytes 688136 | tf_op jit(solution)/shard_map/ppermute | solution.py:30
  184.8 1.7 copy-start.2
  186.6 1.3 copy-start.7
  186.6 1.3 copy-start.30
  186.6 1.3 copy-start.31
  (4 other events, 2.5 us)

commit v4 on v3

--- a/solution.py
+++ b/solution.py
@@ -111,41 +111,49 @@
     )(core, acts_mine, acts_other, *(group[i] for group in sets for i in range(2)))
 
 
-def gradient_kernel(i, core, acts_mine, acts_other, t_mine, t_other, t_mine_p, t_other_p, *outs):
-    third_out, first_out, second_out, home_out = outs
-    rows, half = t_mine.shape
-    units = third_out.shape[0]
+def gradient_kernel(core, acts_mine, acts_other, t_mine, t_other, t_mine_p, t_other_p, *outs):
+    units, half = outs[0].shape
+    rows, span = t_mine.shape[0], 3 * units
+    arrays = len(outs) // 4
     even = core[0] == 0
-    span = 3 * units
+    none = jnp.zeros((rows, units), F32)
     lhs = []
     for acts in (acts_mine, acts_other):
-        value = acts[...].astype(F32)[:, 2 * span * i : 2 * span * (i + 1)]
-        none = jnp.zeros((rows, units), F32)
-        lhs.append(jnp.concatenate([value[:, :span], none], axis=1))
-        lhs.append(jnp.concatenate([value[:, span : span + 2 * units], none, value[:, span + 2 * units :]], axis=1))
+        value = acts[...].astype(F32)
+        own, partner = [], []
+        for i in range(arrays):
+            part = value[:, 2 * span * i : 2 * span * (i + 1)]
+            own += [part[:, :span], none]
+            partner += [part[:, span : span + 2 * units], none, part[:, span + 2 * units :]]
+        lhs += [jnp.concatenate(own, axis=1), jnp.concatenate(partner, axis=1)]
     lhs = jnp.transpose(jnp.concatenate(lhs, axis=0)).astype(BF)
-    step = 512
+    step = 512 // arrays
     for at in range(0, half, step):
         cols = slice(at, at + step)
         tokens = jnp.concatenate([t[:, cols] for t in (t_mine, t_mine_p, t_other, t_other_p)], axis=0)
-        out = dot(lhs, tokens, ((1,), (0,)))
-        first_out[:, cols] = out[:units]
-        second_out[:, cols] = out[units : 2 * units]
-        last = out[3 * units :]
-        third_out[:, cols] = (out[2 * units : 3 * units] + jnp.where(even, last, 0.0)).astype(BF)
-        home_out[:, cols] = jnp.where(even, 0.0, last)
-
-
-def gradient(i, core, acts_mine, acts_other, tokens, units):
+        both = dot(lhs, tokens, ((1,), (0,)))
+        for i in range(arrays):
+            third_out, first_out, second_out, home_out = outs[4 * i : 4 * i + 4]
+            out = both[4 * units * i : 4 * units * (i + 1)]
+            first_out[:, cols] = out[:units]
+            second_out[:, cols] = out[units : 2 * units]
+            last = out[3 * units :]
+            third_out[:, cols] = (out[2 * units : 3 * units] + jnp.where(even, last, 0.0)).astype(BF)
+            home_out[:, cols] = jnp.where(even, 0.0, last)
+
+
+def gradient(core, acts_mine, acts_other, tokens, units):
     rows, half = tokens[0].shape
-    vmem = pl.BlockSpec(memory_space=pltpu.VMEM)
+    arrays = acts_mine.shape[1] // (6 * units)
     return pl.pallas_call(
-        functools.partial(gradient_kernel, i),
-        out_shape=[jax.ShapeDtypeStruct((units, half), kind) for kind in (BF, F32, F32, F32)],
-        in_specs=[pl.BlockSpec(memory_space=pltpu.SMEM)] + [vmem] * 6,
-        out_specs=[vmem] * 4,
+        gradient_kernel,
+        out_shape=[jax.ShapeDtypeStruct((units, half), kind) for kind in (BF, F32, F32, F32)] * arrays,
+        in_specs=[pl.BlockSpec(memory_space=pltpu.SMEM)] + in_vmem(6),
+        out_specs=in_vmem(4 * arrays),
         cost_estimate=pl.CostEstimate(
-            flops=24 * rows * units * half, bytes_accessed=8 * rows * half + 14 * units * half, transcendentals=0
+            flops=32 * arrays * rows * units * half,
+            bytes_accessed=8 * rows * half + 14 * arrays * units * half,
+            transcendentals=0,
         ),
     )(core, acts_mine, acts_other, *tokens)
 
@@ -209,11 +217,13 @@
     norms = (norm_mine, norm_other, norm_mine_p, norm_other_p)
     cots = (cot_mine, cot_other, cot_mine_p, cot_other_p)
     finals = []
-    for i in (2, 0, 1):
-        third_sum, first_sum, second_sum, home_sum = gradient(
-            *((i, core, acts, acts_other, norms) if i < 2 else (0, core, hidden, hidden_other, cots)), units
-        )
+    sums = gradient(core, hidden, hidden_other, cots, units)
+    sums += gradient(core, acts, acts_other, norms, units)
+    for n, i in enumerate((2, 0, 1)):
+        third_sum, first_sum, second_sum, home_sum = sums[4 * n : 4 * n + 4]
         along = hop(third_sum, lambda c, q, k, r: (c - 1, q, k, r))
+        if i == 2:
+            along = lax.optimization_barrier((along, sums[4]))[0]
         swapped = hop((first_sum + along.astype(F32)).astype(BF), cross_swap).astype(F32)
         second_sum = second_sum + jnp.where(q == 0, swapped, 0.0)
         home = hop(second_sum.astype(BF), lambda c, q, k, r: (c - 1, q, k, r)).astype(F32)

time: 198 us -> 195 us (0.985)
  Pallas kernels: 29.3 us -> 26.7 us
  other arithmetic: 17 us -> 14.6 us
  waiting for transfers between devices: 99.7 us -> 102 us
    pallas_call x3 -> x2, Pallas kernels: 12.1 us -> 9.53 us  [gradient(): pl.pallas_call(gradient_kernel, out_shape=[jax.ShapeDtypeStruct((units, h...]
    ppermute x36, waiting for transfers between devices: 99.7 us -> 102 us  [hop(): return lax.ppermute(value, AXES, pairs)]
    unnamed x64 -> x60, local copies, waits for them, and re-layouts: 6.17 us -> 6.37 us
  transfers between devices with their start and end apart: 36 -> 36, of which waited for: 17 -> 18; matrix products, arithmetic and copies ran while one was open for 9% -> 7% of each run, Pallas kernels for 15% -> 14%
where the time goes in v4:
time: 195 us; the launch traced here: 194 us
  waiting for transfers between devices  102 us (52%)
  starting transfers between devices  39.9 us (20%)
  Pallas kernels  26.7 us (14%)
  other arithmetic  14.6 us (7%)
  local copies, waits for them, and re-layouts  9.73 us (5%)
    ppermute x36, waiting for transfers between devices, hop(): return lax.ppermute(value, AXES, pairs)  102 us
    ppermute x36, starting transfers between devices, hop(): return lax.ppermute(value, AXES, pairs)  39.9 us
    pallas_call x4, Pallas kernels, scores(): pl.pallas_call(functools.partial(scores_kernel, len(picked)), out_shape=j...  12.8 us
    pallas_call x2, Pallas kernels, gradient(): pl.pallas_call(gradient_kernel, out_shape=[jax.ShapeDtypeStruct((units, h...  9.53 us
    unnamed x60, local copies, waits for them, and re-layouts  6.37 us
    pallas_call x1, Pallas kernels, back_sums(): pl.pallas_call(back_kernel, out_shape=[jax.ShapeDtypeStruct((rows, half),...  4.35 us
  transfers between devices with their start and end apart: 36, of which 18 were waited for; matrix products, arithmetic and copies ran while one was open for 7% of the time, Pallas kernels for 14%

profile of v4, /device:TPU:24, one launch (start us, length us, event | category | flops | bytes accessed | tf_op | source)
XLA Modules:
  0.0 194.3 jit_solution(8634252729460090735)
XLA Ops:
  0.7 1.0 copy-done
  1.7 1.2 constant_dynamic-slice_fusion.4
  2.9 8.1 %collective-permute-start.1 = (bf16[56,2048]{1,0:T(8,128)(2,1)S(1)}, bf16[56,2048]{1,0:T(8,128)(2,1)}, u32[]{:S(2)}, u32[]{:S(2)}) collective-permute-start(bf16[56,2048]{1,0:T(8,128)(2,1)S(1)} %get-tuple-element.28.refs_3_), channel_id=1, source_target_pairs={{8,0},{9,1},{10,2},{11,3},{12,4},{13,5},{14,6},{15,7},{16,8},{17,9... | collective-permute-start | bytes 688136 | tf_op jit(solution)/shard_map/ppermute | solution.py:30
  11.0 0.8 collective-permute-start.8
  11.8 0.5 collective-permute-start.10
  13.2 1.1 constant_dynamic-slice_fusion.1
  14.3 0.7 collective-permute-start.14
  15.0 1.0 constant_dynamic-slice_fusion.3
  16.0 1.3 collective-permute-start.4
  17.3 4.6 %collective-permute-done.8.refs_2_ = bf16[56,2048]{1,0:T(8,128)(2,1)S(1)} collective-permute-done((bf16[56,2048]{1,0:T(8,128)(2,1)S(1)}, bf16[56,2048]{1,0:T(8,128)(2,1)S(1)}, u32[]{:S(2)}, u32[]{:S(2)}) %collective-permute-start.8) | collective-permute-done | bytes 229408 | tf_op jit(solution)/shard_map/ppermute | solution.py:30
  22.3 3.4 %collective-permute-done.10.refs_3_ = bf16[56,2048]{1,0:T(8,128)(2,1)} collective-permute-done((bf16[56,2048]{1,0:T(8,128)(2,1)S(1)}, bf16[56,2048]{1,0:T(8,128)(2,1)}, u32[]{:S(2)}, u32[]{:S(2)}) %collective-permute-start.10) | collective-permute-done | bytes 229408 | tf_op jit(solution)/shard_map/ppermute | solution.py:30
  25.7 1.2 collective-permute-start.11
  27.0 5.2 %collective-permute-done.14.x_own.t_other = bf16[160,2048]{1,0:T(8,128)(2,1)} collective-permute-done((bf16[160,2048]{1,0:T(8,128)(2,1)}, bf16[160,2048]{1,0:T(8,128)(2,1)}, u32[]{:S(2)}, u32[]{:S(2)}) %collective-permute-start.14) | collective-permute-done | bytes 655392 | tf_op jit(solution)/shard_map/ppermute | solution.py:30
  32.3 1.2 collective-permute-start.2
  33.5 2.5 %collective-permute-start.12 = (bf16[56,2048]{1,0:T(8,128)(2,1)S(1)}, bf16[56,2048]{1,0:T(8,128)(2,1)S(1)}, u32[]{:S(2)}, u32[]{:S(2)}) collective-permute-start(bf16[56,2048]{1,0:T(8,128)(2,1)S(1)} %collective-permute-done.9.refs_0_), channel_id=1, source_target_pairs={{8,0},{9,1},{10,2},{11,3},{12,4},{13,5},{14,6},{15,7},{16,8},{17,9... | collective-permute-start | bytes 688136 | tf_op jit(solution)/shard_map/ppermute | solution.py:30
  36.1 5.4 %collective-permute-start.13 = (bf16[56,2048]{1,0:T(8,128)(2,1)S(1)}, bf16[56,2048]{1,0:T(8,128)(2,1)S(1)}, u32[]{:S(2)}, u32[]{:S(2)}) collective-permute-start(bf16[56,2048]{1,0:T(8,128)(2,1)S(1)} %collective-permute-done.11.refs_1_), channel_id=1, source_target_pairs={{8,0},{9,1},{10,2},{11,3},{12,4},{13,5},{14,6},{15,7},{16,8},{17,9... | collective-permute-start | bytes 688136 | tf_op jit(solution)/shard_map/ppermute | solution.py:30
  41.4 2.9 %collective-permute-done.4.x_own.t_other = bf16[160,2048]{1,0:T(8,128)(2,1)} collective-permute-done((bf16[160,2048]{1,0:T(8,128)(2,1)}, bf16[160,2048]{1,0:T(8,128)(2,1)}, u32[]{:S(2)}, u32[]{:S(2)}) %collective-permute-start.4) | collective-permute-done | bytes 655392 | tf_op jit(solution)/shard_map/ppermute | solution.py:30
  44.3 3.1 %convert_element_type.106 = bf16[3,56,4096]{2,1,0:T(8,128)(2,1)} convert(f32[3,56,4096]{2,1,0:T(8,128)} %param.11) | non-fusion elementwise | flops 688128 | bytes 4128768 | tf_op jit(solution)/shard_map/convert_element_type | solution.py:183
  47.4 1.6 collective-permute-start.20
  49.6 0.7 copy-done.17
  50.5 3.9 %collective-permute-start.3 = (bf16[56,2048]{1,0:T(8,128)(2,1)}, bf16[56,2048]{1,0:T(8,128)(2,1)S(1)}, u32[]{:S(2)}, u32[]{:S(2)}) collective-permute-start(bf16[56,2048]{1,0:T(8,128)(2,1)} %collective-permute-done.2.refs_0_), channel_id=1, source_target_pairs={{8,0},{9,1},{10,2},{11,3},{12,4},{13,5},{14,6},{15,7},{16,8},{17,9... | collective-permute-start | bytes 688136 | tf_op jit(solution)/shard_map/ppermute | solution.py:30
  54.4 3.6 %shard_map.114 = f32[160,672]{1,0:T(8,128)} custom-call(s32[1]{0:T(128)} %bitcast.core, bf16[160,2048]{1,0:T(8,128)(2,1)} %collective-permute-done.14.x_own.t_other, bf16[160,2048]{1,0:T(8,128)(2,1)} %collective-permute-done.15.x_par.t_other_p, bf16[56,2048]{1,0:T(8,128)(2,1)} %copy-done.14, bf16[56,2048]{1,0:T(8,128)(2,1)} %copy-done.15, ...), custom_call_target="tpu_custom_call" | custom-call | flops 440401920 | bytes 4063232 | tf_op jit(solution)/shard_map/pallas_call | solution.py:69
  58.0 2.0 %collective-permute-done.3.refs_2_ = bf16[56,2048]{1,0:T(8,128)(2,1)S(1)} collective-permute-done((bf16[56,2048]{1,0:T(8,128)(2,1)}, bf16[56,2048]{1,0:T(8,128)(2,1)S(1)}, u32[]{:S(2)}, u32[]{:S(2)}) %collective-permute-start.3) | collective-permute-done | bytes 229408 | tf_op jit(solution)/shard_map/ppermute | solution.py:30
  60.0 0.7 collective-permute-start.16
  60.8 0.8 copy-done.9
  61.6 2.8 %shard_map.112 = f32[160,336]{1,0:T(8,128)} custom-call(s32[1]{0:T(128)} %bitcast.core, bf16[160,2048]{1,0:T(8,128)(2,1)} %collective-permute-done.4.x_own.t_other, bf16[160,2048]{1,0:T(8,128)(2,1)} %copy-done.9, bf16[56,2048]{1,0:T(8,128)(2,1)} %collective-permute-done.2.refs_0_, bf16[56,2048]{1,0:T(8,128)(2,1)} %collective-permute-done.1.refs_1_, ...), custom_call_target="tpu_custom_call" | custom-call | flops 220200960 | bytes 2686976 | tf_op jit(solution)/shard_map/pallas_call | solution.py:69
  64.4 1.3 collective-permute-start.6
  65.7 2.8 %shard_map.111 = f32[160,336]{1,0:T(8,128)} custom-call(s32[1]{0:T(128)} %bitcast.core, bf16[160,2048]{1,0:T(8,128)(2,1)} %copy-done.3, bf16[160,2048]{1,0:T(8,128)(2,1)} %collective-permute-done.x_par.t_mine_p, bf16[56,2048]{1,0:T(8,128)(2,1)} %collective-permute-done.2.refs_0_, bf16[56,2048]{1,0:T(8,128)(2,1)} %collective-permute-done.1.refs_1_, ...), custom_call_target="tpu_custom_call" | custom-call | flops 220200960 | bytes 2686976 | tf_op jit(solution)/shard_map/pallas_call | solution.py:69
  68.6 3.6 %shard_map.113 = f32[160,672]{1,0:T(8,128)} custom-call(s32[1]{0:T(128)} %bitcast.core, bf16[160,2048]{1,0:T(8,128)(2,1)} %get-tuple-element.55.x_own.t_mine, bf16[160,2048]{1,0:T(8,128)(2,1)} %collective-permute-done.7.x_par.t_mine_p, bf16[56,2048]{1,0:T(8,128)(2,1)} %copy-done.14, bf16[56,2048]{1,0:T(8,128)(2,1)} %copy-done.15, ...), custom_call_target="tpu_custom_call" | custom-call | flops 440401920 | bytes 4063232 | tf_op jit(solution)/shard_map/pallas_call | solution.py:69
  72.1 2.3 %collective-permute-done.16 = f32[160,672]{1,0:T(8,128)} collective-permute-done((f32[160,672]{1,0:T(8,128)}, f32[160,672]{1,0:T(8,128)}, u32[]{:S(2)}, u32[]{:S(2)}) %collective-permute-start.16) | collective-permute-done | bytes 430112 | tf_op jit(solution)/shard_map/ppermute | solution.py:30
  74.4 1.2 add.114
  75.7 2.4 %collective-permute-done.6 = f32[160,336]{1,0:T(8,128)S(1)} collective-permute-done((f32[160,336]{1,0:T(8,128)}, f32[160,336]{1,0:T(8,128)S(1)}, u32[]{:S(2)}, u32[]{:S(2)}) %collective-permute-start.6) | collective-permute-done | bytes 215072 | tf_op jit(solution)/shard_map/ppermute | solution.py:30
  78.4 0.8 collective-permute-start.17
  79.2 1.3 collective-permute-start.26
  80.5 7.1 %collective-permute-done.26.acts_other = bf16[160,336]{1,0:T(8,128)(2,1)S(1)} collective-permute-done((bf16[160,336]{1,0:T(8,128)(2,1)S(1)}, bf16[160,336]{1,0:T(8,128)(2,1)S(1)}, u32[]{:S(2)}, u32[]{:S(2)}) %collective-permute-start.26) | collective-permute-done | bytes 107552 | tf_op jit(solution)/shard_map/ppermute | solution.py:30
  87.7 0.6 copy-done.29
  88.3 3.9 %shard_map.116 = (bf16[56,2048]{1,0:T(8,128)(2,1)}, f32[56,2048]{1,0:T(8,128)}, f32[56,2048]{1,0:T(8,128)}, f32[56,2048]{1,0:T(8,128)}) custom-call(s32[1]{0:T(128)} %bitcast.core, bf16[160,336]{1,0:T(8,128)(2,1)} %copy-done.19, bf16[160,336]{1,0:T(8,128)(2,1)} %copy-done.29, bf16[160,2048]{1,0:T(8,128)(2,1)} %copy-done.3, ...), custom_call_target="tpu_custom_call" | custom-call | flops 587202560 | bytes 4227072 | tf_op jit(solution)/shard_map/pallas_call | solution.py:148
  92.5 5.6 %shard_map.115 = (bf16[56,2048]{1,0:T(8,128)(2,1)}, f32[56,2048]{1,0:T(8,128)}, f32[56,2048]{1,0:T(8,128)}, f32[56,2048]{1,0:T(8,128)}, bf16[56,2048]{1,0:T(8,12...) custom-call(s32[1]{0:T(128)} %bitcast.core, bf16[160,672]{1,0:T(8,128)(2,1)} %copy-done.27, ...), custom_call_target="tpu_custom_call" | custom-call | flops 1174405120 | bytes 5832704 | tf_op jit(solution)/shard_map/pallas_call | solution.py:148
  98.1 1.2 collective-permute-start.31
  99.4 4.4 %back.1 = (f32[160,2048]{1,0:T(8,128)}, f32[160,2048]{1,0:T(8,128)}, bf16[320,2048]{1,0:T(8,128)(2,1)}) custom-call(s32[1]{0:T(128)} %bitcast.core, bf16[160,672]{1,0:T(8,128)(2,1)} %copy-done.27, bf16[160,672]{1,0:T(8,128)(2,1)} %collective-permute-done.17.acts_other, bf16[56,2048]{1,0:T(8,128)(2,1)} %copy-done.14, bf16[56,2048]{1,0:T(8,128)(2,1)} %copy-done.15, ...), custom_call_target="tpu_custom_call" | custom-call | flops 880803840 | bytes 7077888 | tf_op jit(solution)/shard_map/back/pallas_call | solution.py:102
  103.8 1.0 collective-permute-done.27
  104.8 1.2 add_convert_fusion.2
  106.0 1.1 collective-permute-start.28
  107.1 31.9 %collective-permute-done.31 = bf16[56,2048]{1,0:T(8,128)(2,1)} collective-permute-done((bf16[56,2048]{1,0:T(8,128)(2,1)}, bf16[56,2048]{1,0:T(8,128)(2,1)}, u32[]{:S(2)}, u32[]{:S(2)}) %collective-permute-start.31) | collective-permute-done | bytes 229408 | tf_op jit(solution)/shard_map/ppermute | solution.py:30
  138.9 1.2 add_convert_fusion.1
  140.2 1.1 collective-permute-done.23
  141.4 2.2 %collective-permute-start.24 = (bf16[56,2048]{1,0:T(8,128)(2,1)S(1)}, bf16[56,2048]{1,0:T(8,128)(2,1)S(1)}, u32[]{:S(2)}, u32[]{:S(2)}) collective-permute-start(bf16[56,2048]{1,0:T(8,128)(2,1)S(1)} %add_convert_fusion.3), channel_id=1, source_target_pairs={{5,0},{4,1},{7,2},{6,3},{1,4},{0,5},{3,6},{2,7},{13,8},{12,9},{15,... | collective-permute-start | bytes 688136 | tf_op jit(solution)/shard_map/ppermute | solution.py:30
  143.6 4.0 %collective-permute-done.32 = bf16[56,2048]{1,0:T(8,128)(2,1)S(1)} collective-permute-done((bf16[56,2048]{1,0:T(8,128)(2,1)S(1)}, bf16[56,2048]{1,0:T(8,128)(2,1)S(1)}, u32[]{:S(2)}, u32[]{:S(2)}) %collective-permute-start.32) | collective-permute-done | bytes 229408 | tf_op jit(solution)/shard_map/ppermute | solution.py:30
  147.7 2.3 %collective-permute-done.24 = bf16[56,2048]{1,0:T(8,128)(2,1)S(1)} collective-permute-done((bf16[56,2048]{1,0:T(8,128)(2,1)S(1)}, bf16[56,2048]{1,0:T(8,128)(2,1)S(1)}, u32[]{:S(2)}, u32[]{:S(2)}) %collective-permute-start.24) | collective-permute-done | bytes 229408 | tf_op jit(solution)/shard_map/ppermute | solution.py:30
  150.5 8.2 %collective-permute-done.33 = bf16[56,2048]{1,0:T(8,128)(2,1)S(1)} collective-permute-done((bf16[56,2048]{1,0:T(8,128)(2,1)S(1)}, bf16[56,2048]{1,0:T(8,128)(2,1)S(1)}, u32[]{:S(2)}, u32[]{:S(2)}) %collective-permute-start.33) | collective-permute-done | bytes 229408 | tf_op jit(solution)/shard_map/ppermute | solution.py:30
  158.8 2.4 %collective-permute-done.25 = bf16[56,2048]{1,0:T(8,128)(2,1)S(1)} collective-permute-done((bf16[56,2048]{1,0:T(8,128)(2,1)S(1)}, bf16[56,2048]{1,0:T(8,128)(2,1)S(1)}, u32[]{:S(2)}, u32[]{:S(2)}) %collective-permute-start.25) | collective-permute-done | bytes 229408 | tf_op jit(solution)/shard_map/ppermute | solution.py:30
  161.6 7.1 %collective-permute-done.22 = bf16[3,56,2048]{2,1,0:T(8,128)(2,1)S(1)} collective-permute-done((bf16[3,56,2048]{2,1,0:T(8,128)(2,1)S(1)}, bf16[3,56,2048]{2,1,0:T(8,128)(2,1)S(1)}, u32[]{:S(2)}, u32[]{:S(2)}) %collective-permute-start.22) | collective-permute-done | bytes 688160 | tf_op jit(solution)/shard_map/ppermute | solution.py:30
  169.1 0.7 copy-done.26
  170.0 1.4 collective-permute-start.30
  171.5 0.8 collective-permute-start.34
  172.3 10.4 %collective-permute-done.19 = bf16[160,2048]{1,0:T(8,128)(2,1)S(1)} collective-permute-done((bf16[160,2048]{1,0:T(8,128)(2,1)S(1)}, bf16[160,2048]{1,0:T(8,128)(2,1)S(1)}, u32[]{:S(2)}, u32[]{:S(2)}) %collective-permute-start.19) | collective-permute-done | bytes 655392 | tf_op jit(solution)/shard_map/ppermute | solution.py:30
  183.1 1.4 copy-done.2
  184.5 0.6 fusion.7
  185.1 0.7 copy-done.5
  185.8 2.3 %fusion.6 = bf16[160,4096]{1,0:T(8,128)(2,1)} fusion(bf16[160,4096]{1,0:T(8,128)(2,1)S(1)} %copy-done.1, bf16[160,4096]{1,0:T(8,128)(2,1)S(1)} %copy-done.5, f32[160]{0:T(256)S(1)} %broadcast_multiply_fusion, f32[160]{0:T(256)S(1)} %get-tuple-element.67, f32[160]{0:T(256)S(1)} %get-tuple-element.68, f32[160,4096]{1,0:T(8,128)S(1)} %copy-done.2, ...), kind=kLoop, calls=%fused_computation.10 | loop fusion | flops 7208960 | bytes 9193344 | tf_op jit(solution)/shard_map/convert_element_type | solution.py:243
  188.1 3.7 %collective-permute-done.34 = bf16[56,2048]{1,0:T(8,128)(2,1)S(1)} collective-permute-done((bf16[56,2048]{1,0:T(8,128)(2,1)S(1)}, bf16[56,2048]{1,0:T(8,128)(2,1)S(1)}, u32[]{:S(2)}, u32[]{:S(2)}) %collective-permute-start.34) | collective-permute-done | bytes 229408 | tf_op jit(solution)/shard_map/ppermute | solution.py:30
  191.9 0.8 pad_maximum_fusion.2
  192.7 0.8 pad_maximum_fusion.1
  193.5 0.8 pad_maximum_fusion
  (113 shorter events, 5.0 us)
Async XLA Ops:
  0.6 1.0 copy-start
  0.6 11.7 %copy-start.1 = (bf16[160,4096]{1,0:T(8,128)(2,1)S(1)}, bf16[160,4096]{1,0:T(8,128)(2,1)}, u32[]{:S(2)}) copy-start(bf16[160,4096]{1,0:T(8,128)(2,1)} %param.8) | copy-start | bytes 3932164
  0.7 12.1 %copy-start.28 = (f32[4096]{0:T(1024)S(1)}, f32[4096]{0:T(1024)}, u32[]{:S(2)}) copy-start(f32[4096]{0:T(1024)} %param.12) | copy-start | bytes 49156
  1.7 20.2 %copy-start.6 = (bf16[56,2048]{1,0:T(8,128)(2,1)}, bf16[56,2048]{1,0:T(8,128)(2,1)S(1)}, u32[]{:S(2)}) copy-start(bf16[56,2048]{1,0:T(8,128)(2,1)S(1)} %constant_dynamic-slice_fusion.6.refs_6_) | copy-start | bytes 688132
  2.9 22.8 %copy-start.7 = (bf16[56,2048]{1,0:T(8,128)(2,1)}, bf16[56,2048]{1,0:T(8,128)(2,1)S(1)}, u32[]{:S(2)}) copy-start(bf16[56,2048]{1,0:T(8,128)(2,1)S(1)} %get-tuple-element.30.refs_7_) | copy-start | bytes 688132
  2.9 29.4 %copy-start.8 = (bf16[56,2048]{1,0:T(8,128)(2,1)}, bf16[56,2048]{1,0:T(8,128)(2,1)S(1)}, u32[]{:S(2)}) copy-start(bf16[56,2048]{1,0:T(8,128)(2,1)S(1)} %get-tuple-element.28.refs_3_) | copy-start | bytes 688132
  2.9 29.3 %collective-permute-start.1 = (bf16[56,2048]{1,0:T(8,128)(2,1)S(1)}, bf16[56,2048]{1,0:T(8,128)(2,1)}, u32[]{:S(2)}, u32[]{:S(2)}) collective-permute-start(bf16[56,2048]{1,0:T(8,128)(2,1)S(1)} %get-tuple-element.28.refs_3_), channel_id=1, source_target_pairs={{8,0},{9,1},{10,2},{11,3},{12,4},{13,5},{14,6},{15,7},{16,8},{17,9... | collective-permute-start | bytes 688136 | tf_op jit(solution)/shard_map/ppermute | solution.py:30
  11.0 10.9 %collective-permute-start.8 = (bf16[56,2048]{1,0:T(8,128)(2,1)S(1)}, bf16[56,2048]{1,0:T(8,128)(2,1)S(1)}, u32[]{:S(2)}, u32[]{:S(2)}) collective-permute-start(bf16[56,2048]{1,0:T(8,128)(2,1)S(1)} %constant_dynamic-slice_fusion.6.refs_6_), channel_id=1, source_target_pairs={{8,0},{9,1},{10,2},{11,3},{12,4},{13,5},{14,6},{15,7},{16,8},{17,9... | collective-permute-start | bytes 688136 | tf_op jit(solution)/shard_map/ppermute | solution.py:30
  11.8 13.9 %collective-permute-start.10 = (bf16[56,2048]{1,0:T(8,128)(2,1)S(1)}, bf16[56,2048]{1,0:T(8,128)(2,1)}, u32[]{:S(2)}, u32[]{:S(2)}) collective-permute-start(bf16[56,2048]{1,0:T(8,128)(2,1)S(1)} %get-tuple-element.30.refs_7_), channel_id=1, source_target_pairs={{8,0},{9,1},{10,2},{11,3},{12,4},{13,5},{14,6},{15,7},{16,8},{17,9... | collective-permute-start | bytes 688136 | tf_op jit(solution)/shard_map/ppermute | solution.py:30
  13.1 1.9 copy-start.4
  14.3 17.9 %collective-permute-start.14 = (bf16[160,2048]{1,0:T(8,128)(2,1)}, bf16[160,2048]{1,0:T(8,128)(2,1)}, u32[]{:S(2)}, u32[]{:S(2)}) collective-permute-start(bf16[160,2048]{1,0:T(8,128)(2,1)} %get-tuple-element.54), channel_id=1, source_target_pairs={{1,0},{0,1},{3,2},{2,3},{5,4},{4,5},{7,6},{6,7},{9,8},{8,9},{11,10... | collective-permute-start | bytes 1966088 | tf_op jit(solution)/shard_map/ppermute | solution.py:30
  16.0 32.9 %copy-start.3 = (bf16[160,2048]{1,0:T(8,128)(2,1)}, bf16[160,2048]{1,0:T(8,128)(2,1)S(1)}, u32[]{:S(2)}) copy-start(bf16[160,2048]{1,0:T(8,128)(2,1)S(1)} %get-tuple-element.57.x_own.t_mine) | copy-start | bytes 1966084
  16.0 28.3 %collective-permute-start.4 = (bf16[160,2048]{1,0:T(8,128)(2,1)}, bf16[160,2048]{1,0:T(8,128)(2,1)}, u32[]{:S(2)}, u32[]{:S(2)}) collective-permute-start(bf16[160,2048]{1,0:T(8,128)(2,1)} %get-tuple-element.56), channel_id=1, source_target_pairs={{1,0},{0,1},{3,2},{2,3},{5,4},{4,5},{7,6},{6,7},{9,8},{8,9},{11,10... | collective-permute-start | bytes 1966088 | tf_op jit(solution)/shard_map/ppermute | solution.py:30
  21.9 25.4 %copy-start.10 = (bf16[56,2048]{1,0:T(8,128)(2,1)}, bf16[56,2048]{1,0:T(8,128)(2,1)S(1)}, u32[]{:S(2)}) copy-start(bf16[56,2048]{1,0:T(8,128)(2,1)S(1)} %collective-permute-done.8.refs_2_) | copy-start | bytes 688132
  21.9 11.6 %collective-permute-start.9 = (bf16[56,2048]{1,0:T(8,128)(2,1)S(1)}, bf16[56,2048]{1,0:T(8,128)(2,1)S(1)}, u32[]{:S(2)}, u32[]{:S(2)}) collective-permute-start(bf16[56,2048]{1,0:T(8,128)(2,1)S(1)} %broadcast_select_fusion.7), channel_id=1, source_target_pairs={{5,0},{4,1},{7,2},{6,3},{1,4},{0,5},{3,6},{2,7},{13,8},{12,9},{15,... | collective-permute-start | bytes 688136 | tf_op jit(solution)/shard_map/ppermute | solution.py:30
  25.7 10.3 %collective-permute-start.11 = (bf16[56,2048]{1,0:T(8,128)(2,1)S(1)}, bf16[56,2048]{1,0:T(8,128)(2,1)S(1)}, u32[]{:S(2)}, u32[]{:S(2)}) collective-permute-start(bf16[56,2048]{1,0:T(8,128)(2,1)S(1)} %broadcast_select_fusion.6), channel_id=1, source_target_pairs={{5,0},{4,1},{7,2},{6,3},{1,4},{0,5},{3,6},{2,7},{13,8},{12,9},{15,... | collective-permute-start | bytes 688136 | tf_op jit(solution)/shard_map/ppermute | solution.py:30
  32.2 18.3 %collective-permute-start.15 = (bf16[160,2048]{1,0:T(8,128)(2,1)}, bf16[160,2048]{1,0:T(8,128)(2,1)}, u32[]{:S(2)}, u32[]{:S(2)}) collective-permute-start(bf16[160,2048]{1,0:T(8,128)(2,1)} %collective-permute-done.14.x_own.t_other), channel_id=1, source_target_pairs={{2,0},{3,1},{0,2},{1,3},{6,4},{7,5},{4,6},{5,7},{10,8},{11,9},{8,1... | collective-permute-start | bytes 1966088 | tf_op jit(solution)/shard_map/ppermute | solution.py:30
  32.3 15.1 %collective-permute-start.2 = (bf16[56,2048]{1,0:T(8,128)(2,1)S(1)}, bf16[56,2048]{1,0:T(8,128)(2,1)}, u32[]{:S(2)}, u32[]{:S(2)}) collective-permute-start(bf16[56,2048]{1,0:T(8,128)(2,1)S(1)} %broadcast_select_fusion.8), channel_id=1, source_target_pairs={{5,0},{4,1},{7,2},{6,3},{1,4},{0,5},{3,6},{2,7},{13,8},{12,9},{15,... | collective-permute-start | bytes 688136 | tf_op jit(solution)/shard_map/ppermute | solution.py:30
  33.5 13.8 %copy-start.14 = (bf16[56,2048]{1,0:T(8,128)(2,1)}, bf16[56,2048]{1,0:T(8,128)(2,1)S(1)}, u32[]{:S(2)}) copy-start(bf16[56,2048]{1,0:T(8,128)(2,1)S(1)} %collective-permute-done.9.refs_0_) | copy-start | bytes 688132
  33.5 15.4 %collective-permute-start.12 = (bf16[56,2048]{1,0:T(8,128)(2,1)S(1)}, bf16[56,2048]{1,0:T(8,128)(2,1)S(1)}, u32[]{:S(2)}, u32[]{:S(2)}) collective-permute-start(bf16[56,2048]{1,0:T(8,128)(2,1)S(1)} %collective-permute-done.9.refs_0_), channel_id=1, source_target_pairs={{8,0},{9,1},{10,2},{11,3},{12,4},{13,5},{14,6},{15,7},{16,8},{17,9... | collective-permute-start | bytes 688136 | tf_op jit(solution)/shard_map/ppermute | solution.py:30
  36.1 11.3 %copy-start.15 = (bf16[56,2048]{1,0:T(8,128)(2,1)}, bf16[56,2048]{1,0:T(8,128)(2,1)S(1)}, u32[]{:S(2)}) copy-start(bf16[56,2048]{1,0:T(8,128)(2,1)S(1)} %collective-permute-done.11.refs_1_) | copy-start | bytes 688132
  36.1 13.2 %collective-permute-start.13 = (bf16[56,2048]{1,0:T(8,128)(2,1)S(1)}, bf16[56,2048]{1,0:T(8,128)(2,1)S(1)}, u32[]{:S(2)}, u32[]{:S(2)}) collective-permute-start(bf16[56,2048]{1,0:T(8,128)(2,1)S(1)} %collective-permute-done.11.refs_1_), channel_id=1, source_target_pairs={{8,0},{9,1},{10,2},{11,3},{12,4},{13,5},{14,6},{15,7},{16,8},{17,9... | collective-permute-start | bytes 688136 | tf_op jit(solution)/shard_map/ppermute | solution.py:30
  44.3 16.5 %collective-permute-start.5 = (bf16[160,2048]{1,0:T(8,128)(2,1)}, bf16[160,2048]{1,0:T(8,128)(2,1)S(1)}, u32[]{:S(2)}, u32[]{:S(2)}) collective-permute-start(bf16[160,2048]{1,0:T(8,128)(2,1)} %collective-permute-done.4.x_own.t_other), channel_id=1, source_target_pairs={{2,0},{3,1},{0,2},{1,3},{6,4},{7,5},{4,6},{5,7},{10,8},{11,9},{8,1... | collective-permute-start | bytes 1966088 | tf_op jit(solution)/shard_map/ppermute | solution.py:30
  47.4 45.0 %collective-permute-start.20 = (bf16[3,56,4096]{2,1,0:T(8,128)(2,1)}, bf16[3,56,4096]{2,1,0:T(8,128)(2,1)}, u32[]{:S(2)}, u32[]{:S(2)}) collective-permute-start(bf16[3,56,4096]{2,1,0:T(8,128)(2,1)} %convert_element_type.106), channel_id=1, source_target_pairs={{248,0},{249,1},{250,2},{251,3},{252,4},{253,5},{254,6},{255,7},{0... | collective-permute-start | bytes 4128776 | tf_op jit(solution)/shard_map/ppermute | solution.py:30
  48.9 0.7 copy-start.16
  48.9 16.8 %collective-permute-start = (bf16[160,2048]{1,0:T(8,128)(2,1)S(1)}, bf16[160,2048]{1,0:T(8,128)(2,1)}, u32[]{:S(2)}, u32[]{:S(2)}) collective-permute-start(bf16[160,2048]{1,0:T(8,128)(2,1)S(1)} %get-tuple-element.57.x_own.t_mine), channel_id=1, source_target_pairs={{2,0},{3,1},{0,2},{1,3},{6,4},{7,5},{4,6},{5,7},{10,8},{11,9},{8,1... | collective-permute-start | bytes 1966088 | tf_op jit(solution)/shard_map/ppermute | solution.py:30
  50.3 18.3 %collective-permute-start.7 = (bf16[160,2048]{1,0:T(8,128)(2,1)}, bf16[160,2048]{1,0:T(8,128)(2,1)}, u32[]{:S(2)}, u32[]{:S(2)}) collective-permute-start(bf16[160,2048]{1,0:T(8,128)(2,1)} %get-tuple-element.55.x_own.t_mine), channel_id=1, source_target_pairs={{2,0},{3,1},{0,2},{1,3},{6,4},{7,5},{4,6},{5,7},{10,8},{11,9},{8,1... | collective-permute-start | bytes 1966088 | tf_op jit(solution)/shard_map/ppermute | solution.py:30
  50.5 9.5 %collective-permute-start.3 = (bf16[56,2048]{1,0:T(8,128)(2,1)}, bf16[56,2048]{1,0:T(8,128)(2,1)S(1)}, u32[]{:S(2)}, u32[]{:S(2)}) collective-permute-start(bf16[56,2048]{1,0:T(8,128)(2,1)} %collective-permute-done.2.refs_0_), channel_id=1, source_target_pairs={{8,0},{9,1},{10,2},{11,3},{12,4},{13,5},{14,6},{15,7},{16,8},{17,9... | collective-permute-start | bytes 688136 | tf_op jit(solution)/shard_map/ppermute | solution.py:30
  60.0 0.8 copy-start.18
  60.0 14.4 %collective-permute-start.16 = (f32[160,672]{1,0:T(8,128)}, f32[160,672]{1,0:T(8,128)}, u32[]{:S(2)}, u32[]{:S(2)}) collective-permute-start(f32[160,672]{1,0:T(8,128)} %shard_map.114), channel_id=1, source_target_pairs={{1,0},{0,1},{3,2},{2,3},{5,4},{4,5},{7,6},{6,7},{9,8},{8,9},{11,10... | collective-permute-start | bytes 1290248 | tf_op jit(solution)/shard_map/ppermute | solution.py:30
  60.8 0.8 copy-start.9
  64.4 13.6 %collective-permute-start.6 = (f32[160,336]{1,0:T(8,128)}, f32[160,336]{1,0:T(8,128)S(1)}, u32[]{:S(2)}, u32[]{:S(2)}) collective-permute-start(f32[160,336]{1,0:T(8,128)} %shard_map.112), channel_id=1, source_target_pairs={{1,0},{0,1},{3,2},{2,3},{5,4},{4,5},{7,6},{6,7},{9,8},{8,9},{11,10... | collective-permute-start | bytes 645128 | tf_op jit(solution)/shard_map/ppermute | solution.py:30
  72.1 5.9 %copy-start.13 = (f32[160,336]{1,0:T(8,128)S(1)}, f32[160,336]{1,0:T(8,128)}, u32[]{:S(2)}) copy-start(f32[160,336]{1,0:T(8,128)} %shard_map.111) | copy-start | bytes 645124
  78.3 9.4 %copy-start.19 = (bf16[160,336]{1,0:T(8,128)(2,1)}, bf16[160,336]{1,0:T(8,128)(2,1)S(1)}, u32[]{:S(2)}) copy-start(bf16[160,336]{1,0:T(8,128)(2,1)S(1)} %get-tuple-element.60.acts_mine) | copy-start | bytes 322564
  78.4 13.9 %copy-start.27 = (bf16[160,672]{1,0:T(8,128)(2,1)}, bf16[160,672]{1,0:T(8,128)(2,1)S(1)}, u32[]{:S(2)}) copy-start(bf16[160,672]{1,0:T(8,128)(2,1)S(1)} %pad_maximum_fusion.3.acts_mine) | copy-start | bytes 645124
  78.4 14.1 %collective-permute-start.17 = (bf16[160,672]{1,0:T(8,128)(2,1)S(1)}, bf16[160,672]{1,0:T(8,128)(2,1)}, u32[]{:S(2)}, u32[]{:S(2)}) collective-permute-start(bf16[160,672]{1,0:T(8,128)(2,1)S(1)} %pad_maximum_fusion.3.acts_mine), channel_id=1, source_target_pairs={{1,0},{0,1},{3,2},{2,3},{5,4},{4,5},{7,6},{6,7},{9,8},{8,9},{11,10... | collective-permute-start | bytes 645128 | tf_op jit(solution)/shard_map/ppermute | solution.py:30
  79.2 8.4 %collective-permute-start.26 = (bf16[160,336]{1,0:T(8,128)(2,1)S(1)}, bf16[160,336]{1,0:T(8,128)(2,1)S(1)}, u32[]{:S(2)}, u32[]{:S(2)}) collective-permute-start(bf16[160,336]{1,0:T(8,128)(2,1)S(1)} %get-tuple-element.60.acts_mine), channel_id=1, source_target_pairs={{1,0},{0,1},{3,2},{2,3},{5,4},{4,5},{7,6},{6,7},{9,8},{8,9},{11,10... | collective-permute-start | bytes 322568 | tf_op jit(solution)/shard_map/ppermute | solution.py:30
  92.3 12.5 %collective-permute-start.27 = (bf16[56,2048]{1,0:T(8,128)(2,1)}, bf16[56,2048]{1,0:T(8,128)(2,1)}, u32[]{:S(2)}, u32[]{:S(2)}) collective-permute-start(bf16[56,2048]{1,0:T(8,128)(2,1)} %get-tuple-element.39), channel_id=1, source_target_pairs={{248,0},{249,1},{250,2},{251,3},{252,4},{253,5},{254,6},{255,7},{0... | collective-permute-start | bytes 688136 | tf_op jit(solution)/shard_map/ppermute | solution.py:30
  92.4 57.8 %collective-permute-start.21 = (bf16[3,56,4096]{2,1,0:T(8,128)(2,1)}, bf16[3,56,4096]{2,1,0:T(8,128)(2,1)S(1)}, u32[]{:S(2)}, u32[]{:S(2)}) collective-permute-start(bf16[3,56,4096]{2,1,0:T(8,128)(2,1)} %collective-permute-done.20), channel_id=1, source_target_pairs={{253,0},{252,1},{255,2},{254,3},{1,4},{0,5},{3,6},{2,7},{5,8},{4,9... | collective-permute-start | bytes 4128776 | tf_op jit(solution)/shard_map/ppermute | solution.py:30
  98.1 40.9 %collective-permute-start.31 = (bf16[56,2048]{1,0:T(8,128)(2,1)}, bf16[56,2048]{1,0:T(8,128)(2,1)}, u32[]{:S(2)}, u32[]{:S(2)}) collective-permute-start(bf16[56,2048]{1,0:T(8,128)(2,1)} %get-tuple-element.47), channel_id=1, source_target_pairs={{248,0},{249,1},{250,2},{251,3},{252,4},{253,5},{254,6},{255,7},{0... | collective-permute-start | bytes 688136 | tf_op jit(solution)/shard_map/ppermute | solution.py:30
  99.3 42.0 %collective-permute-start.23 = (bf16[56,2048]{1,0:T(8,128)(2,1)}, bf16[56,2048]{1,0:T(8,128)(2,1)S(1)}, u32[]{:S(2)}, u32[]{:S(2)}) collective-permute-start(bf16[56,2048]{1,0:T(8,128)(2,1)} %get-tuple-element.36), channel_id=1, source_target_pairs={{248,0},{249,1},{250,2},{251,3},{252,4},{253,5},{254,6},{255,7},{0... | collective-permute-start | bytes 688136 | tf_op jit(solution)/shard_map/ppermute | solution.py:30
  103.8 37.5 %copy-start.23 = (f32[56,2048]{1,0:T(8,128)S(1)}, f32[56,2048]{1,0:T(8,128)}, u32[]{:S(2)}) copy-start(f32[56,2048]{1,0:T(8,128)} %get-tuple-element.35) | copy-start | bytes 1376260
  103.8 57.5 %collective-permute-start.18 = (bf16[320,2048]{1,0:T(8,128)(2,1)}, bf16[320,2048]{1,0:T(8,128)(2,1)S(1)}, u32[]{:S(2)}, u32[]{:S(2)}) collective-permute-start(bf16[320,2048]{1,0:T(8,128)(2,1)} %get-tuple-element.32), channel_id=1, source_target_pairs={{2,0},{3,1},{0,2},{1,3},{6,4},{7,5},{4,6},{5,7},{10,8},{11,9},{8,1... | collective-permute-start | bytes 3932168 | tf_op jit(solution)/shard_map/ppermute | solution.py:30
  104.8 42.8 %copy-start.22 = (f32[56,2048]{1,0:T(8,128)S(1)}, f32[56,2048]{1,0:T(8,128)}, u32[]{:S(2)}) copy-start(f32[56,2048]{1,0:T(8,128)} %get-tuple-element.45) | copy-start | bytes 1376260
  106.0 44.4 %collective-permute-start.28 = (bf16[56,2048]{1,0:T(8,128)(2,1)S(1)}, bf16[56,2048]{1,0:T(8,128)(2,1)S(1)}, u32[]{:S(2)}, u32[]{:S(2)}) collective-permute-start(bf16[56,2048]{1,0:T(8,128)(2,1)S(1)} %add_convert_fusion.2), channel_id=1, source_target_pairs={{5,0},{4,1},{7,2},{6,3},{1,4},{0,5},{3,6},{2,7},{13,8},{12,9},{15,... | collective-permute-start | bytes 688136 | tf_op jit(solution)/shard_map/ppermute | solution.py:30
  138.9 11.1 %copy-start.21 = (f32[56,2048]{1,0:T(8,128)S(1)}, f32[56,2048]{1,0:T(8,128)}, u32[]{:S(2)}) copy-start(f32[56,2048]{1,0:T(8,128)} %get-tuple-element.34) | copy-start | bytes 1376260
  140.1 7.4 %collective-permute-start.32 = (bf16[56,2048]{1,0:T(8,128)(2,1)S(1)}, bf16[56,2048]{1,0:T(8,128)(2,1)S(1)}, u32[]{:S(2)}, u32[]{:S(2)}) collective-permute-start(bf16[56,2048]{1,0:T(8,128)(2,1)S(1)} %add_convert_fusion.1), channel_id=1, source_target_pairs={{5,0},{4,1},{7,2},{6,3},{1,4},{0,5},{3,6},{2,7},{13,8},{12,9},{15,... | collective-permute-start | bytes 688136 | tf_op jit(solution)/shard_map/ppermute | solution.py:30
  141.4 8.7 %collective-permute-start.24 = (bf16[56,2048]{1,0:T(8,128)(2,1)S(1)}, bf16[56,2048]{1,0:T(8,128)(2,1)S(1)}, u32[]{:S(2)}, u32[]{:S(2)}) collective-permute-start(bf16[56,2048]{1,0:T(8,128)(2,1)S(1)} %add_convert_fusion.3), channel_id=1, source_target_pairs={{5,0},{4,1},{7,2},{6,3},{1,4},{0,5},{3,6},{2,7},{13,8},{12,9},{15,... | collective-permute-start | bytes 688136 | tf_op jit(solution)/shard_map/ppermute | solution.py:30
  147.6 2.7 %copy-start.20 = (f32[56,2048]{1,0:T(8,128)S(1)}, f32[56,2048]{1,0:T(8,128)}, u32[]{:S(2)}) copy-start(f32[56,2048]{1,0:T(8,128)} %get-tuple-element.37) | copy-start | bytes 1376260
  147.6 11.1 %collective-permute-start.33 = (bf16[56,2048]{1,0:T(8,128)(2,1)S(1)}, bf16[56,2048]{1,0:T(8,128)(2,1)S(1)}, u32[]{:S(2)}, u32[]{:S(2)}) collective-permute-start(bf16[56,2048]{1,0:T(8,128)(2,1)S(1)} %fusion.20), channel_id=1, source_target_pairs={{248,0},{249,1},{250,2},{251,3},{252,4},{253,5},{254,6},{255,7},{0... | collective-permute-start | bytes 688136 | tf_op jit(solution)/shard_map/ppermute | solution.py:30
  150.1 11.1 %collective-permute-start.25 = (bf16[56,2048]{1,0:T(8,128)(2,1)S(1)}, bf16[56,2048]{1,0:T(8,128)(2,1)S(1)}, u32[]{:S(2)}, u32[]{:S(2)}) collective-permute-start(bf16[56,2048]{1,0:T(8,128)(2,1)S(1)} %fusion.10), channel_id=1, source_target_pairs={{248,0},{249,1},{250,2},{251,3},{252,4},{253,5},{254,6},{255,7},{0... | collective-permute-start | bytes 688136 | tf_op jit(solution)/shard_map/ppermute | solution.py:30
  150.3 11.0 %copy-start.11 = (f32[160,2048]{1,0:T(8,128)S(1)}, f32[160,2048]{1,0:T(8,128)}, u32[]{:S(2)}) copy-start(f32[160,2048]{1,0:T(8,128)} %get-tuple-element.33) | copy-start | bytes 3932164
  150.3 18.4 %collective-permute-start.22 = (bf16[3,56,2048]{2,1,0:T(8,128)(2,1)S(1)}, bf16[3,56,2048]{2,1,0:T(8,128)(2,1)S(1)}, u32[]{:S(2)}, u32[]{:S(2)}) collective-permute-start(bf16[3,56,2048]{2,1,0:T(8,128)(2,1)S(1)} %constant_dynamic-slice_fusion), channel_id=1, source_target_pairs={{1,0},{0,1},{3,2},{2,3},{5,4},{4,5},{7,6},{6,7},{9,8},{8,9},{11,10... | collective-permute-start | bytes 2064392 | tf_op jit(solution)/shard_map/ppermute | solution.py:30
  150.5 18.4 %collective-permute-start.29 = (bf16[56,2048]{1,0:T(8,128)(2,1)S(1)}, bf16[56,2048]{1,0:T(8,128)(2,1)S(1)}, u32[]{:S(2)}, u32[]{:S(2)}) collective-permute-start(bf16[56,2048]{1,0:T(8,128)(2,1)S(1)} %fusion.15), channel_id=1, source_target_pairs={{248,0},{249,1},{250,2},{251,3},{252,4},{253,5},{254,6},{255,7},{0... | collective-permute-start | bytes 688136 | tf_op jit(solution)/shard_map/ppermute | solution.py:30
  161.4 7.4 %copy-start.24 = (f32[56,2048]{1,0:T(8,128)S(1)}, f32[56,2048]{1,0:T(8,128)}, u32[]{:S(2)}) copy-start(f32[56,2048]{1,0:T(8,128)} %get-tuple-element.41) | copy-start | bytes 1376260
  161.5 21.2 %collective-permute-start.19 = (bf16[160,2048]{1,0:T(8,128)(2,1)S(1)}, bf16[160,2048]{1,0:T(8,128)(2,1)S(1)}, u32[]{:S(2)}, u32[]{:S(2)}) collective-permute-start(bf16[160,2048]{1,0:T(8,128)(2,1)S(1)} %add_convert_fusion), channel_id=1, source_target_pairs={{1,0},{0,1},{3,2},{2,3},{5,4},{4,5},{7,6},{6,7},{9,8},{8,9},{11,10... | collective-permute-start | bytes 1966088 | tf_op jit(solution)/shard_map/ppermute | solution.py:30
  168.8 1.0 copy-start.26
  168.9 2.5 %copy-start.25 = (f32[56,2048]{1,0:T(8,128)S(1)}, f32[56,2048]{1,0:T(8,128)}, u32[]{:S(2)}) copy-start(f32[56,2048]{1,0:T(8,128)} %get-tuple-element.49) | copy-start | bytes 1376260
  169.0 19.0 %collective-permute-start.35 = (bf16[56,2048]{1,0:T(8,128)(2,1)S(1)}, bf16[56,2048]{1,0:T(8,128)(2,1)S(1)}, u32[]{:S(2)}, u32[]{:S(2)}) collective-permute-start(bf16[56,2048]{1,0:T(8,128)(2,1)S(1)} %fusion.18), channel_id=1, source_target_pairs={{1,0},{0,1},{3,2},{2,3},{5,4},{4,5},{7,6},{6,7},{9,8},{8,9},{11,10... | collective-permute-start | bytes 688136 | tf_op jit(solution)/shard_map/ppermute | solution.py:30
  170.0 12.7 %copy-start.12 = (f32[160,2048]{1,0:T(8,128)S(1)}, f32[160,2048]{1,0:T(8,128)}, u32[]{:S(2)}) copy-start(f32[160,2048]{1,0:T(8,128)} %get-tuple-element.31) | copy-start | bytes 3932164
  170.0 21.9 %collective-permute-start.30 = (bf16[56,2048]{1,0:T(8,128)(2,1)S(1)}, bf16[56,2048]{1,0:T(8,128)(2,1)S(1)}, u32[]{:S(2)}, u32[]{:S(2)}) collective-permute-start(bf16[56,2048]{1,0:T(8,128)(2,1)S(1)} %fusion.13), channel_id=1, source_target_pairs={{1,0},{0,1},{3,2},{2,3},{5,4},{4,5},{7,6},{6,7},{9,8},{8,9},{11,10... | collective-permute-start | bytes 688136 | tf_op jit(solution)/shard_map/ppermute | solution.py:30
  171.5 20.3 %collective-permute-start.34 = (bf16[56,2048]{1,0:T(8,128)(2,1)S(1)}, bf16[56,2048]{1,0:T(8,128)(2,1)S(1)}, u32[]{:S(2)}, u32[]{:S(2)}) collective-permute-start(bf16[56,2048]{1,0:T(8,128)(2,1)S(1)} %fusion.23), channel_id=1, source_target_pairs={{1,0},{0,1},{3,2},{2,3},{5,4},{4,5},{7,6},{6,7},{9,8},{8,9},{11,10... | collective-permute-start | bytes 688136 | tf_op jit(solution)/shard_map/ppermute | solution.py:30
  182.7 1.7 copy-start.2
  184.5 1.3 copy-start.5
  (2 other events, 1.3 us)
